TPU v7x, 32 devices: a whole 2x2x4 slice. The times are simulated.
32 devices in a mesh: groups: 2 (over y), seq: 4 (over z), chan: 2 (over x), dp: 2 (over core).
Axes of the slice: x: 2, y: 2, z: 4, core: 2. Of those that a mesh axis runs over, the one named last changes fastest.
Arguments:
- signal: bfloat16 [4, 2560, 1536], P(('groups', 'dp'), 'seq', 'chan'), parts along dimension 0, may hold values from -100 to 100
- lengths: int32 [4, 8], P(('groups', 'dp')), parts along dimension 0, may hold values from 1 to 1280, 2560 in all within a row
- dilations: int32 [2], replicated, may hold values from 1 to 64, as said below
- w_conv: bfloat16 [2, 3, 1536, 768], P(None, None, None, 'chan'), may hold values from -0.09375 to 0.09375
- w_proj: bfloat16 [2, 768, 1536], P(None, 'chan'), may hold values from -0.3125 to 0.3125
- gains: float32 [2, 1536], P(None, 'chan'), may hold values from 0.1 to 1.9
- biases: float32 [2, 1536], P(None, 'chan'), may hold values from -3 to 3
Outputs:
- result: bfloat16 [4, 2560, 1536], P(('groups', 'dp'), 'seq', 'chan'), parts along dimension 0
There are 2 independent parts, one for each index of `groups`. A program takes and returns all parts, laid end to end along the dimension named above; an argument that names none is the same for every part. Nothing has to cross between parts.
Inputs may be any that keep to these rules, and one draw needn't show every extreme that they name: `dilations`: exactly one block has dilation 64, the others smaller ones.
All inputs are finite; a program needn't handle non-finite values.
Results may differ from a plain program's by a relative error of at most 0.008.
Values may be sent and summed in bfloat16 or wider, within the bound.
No kernel may reach another device: no remote copies, remote signals or barrier semaphores. Data moves between devices by JAX's collectives and lax.ppermute only.
A program may use at most 64 MiB of HBM per device.

v0:
```python
import jax
import jax.numpy as jnp
from jax import lax
from jax.sharding import PartitionSpec as P

LAYERS = 2
DILATION_MAX = 64


eps = 1e-05
far_away = 1 << 30


def extended_2(block, sides, width):
    for axis, dim in sides:
        count = lax.axis_size(axis)
        forward = [(i, i + 1) for i in range(count - 1)]
        backward = [(target, source) for source, target in forward]
        low = lax.ppermute(
            lax.slice_in_dim(block, block.shape[dim] - width, None, axis=dim), axis, forward
        )
        high = lax.ppermute(lax.slice_in_dim(block, 0, width, axis=dim), axis, backward)
        block = jnp.concatenate([low, block, high], axis=dim)
    return block


def segment_bounds(lengths, places):
    ends = jnp.cumsum(lengths, axis=-1, dtype=jnp.int32)
    starts = ends - lengths
    low = jnp.max(
        jnp.where(starts[:, None, :] <= places[None, :, None], starts[:, None, :], -far_away),
        axis=-1,
    )
    high = jnp.min(
        jnp.where(ends[:, None, :] > places[None, :, None], ends[:, None, :], far_away), axis=-1
    )
    return (low, high)


def batch_total(value):
    return lax.psum(value, ("seq", "dp"))


def norm_act(state, own_rows, gain, bias):
    values = state.astype(jnp.float32)
    count = values.shape[0] * own_rows * lax.axis_size("seq") * lax.axis_size("dp")
    mean = batch_total(jnp.sum(values, axis=(0, 1))) / count
    spread = batch_total(jnp.sum(jnp.square(values - mean), axis=(0, 1))) / count
    return jax.nn.gelu((values - mean) * lax.rsqrt(spread + eps) * gain + bias).astype(jnp.bfloat16)


def conv_layer(normed, state_mid, first_place, dilation, lengths, conv_weight, proj_weight):
    seqs_here, ext_rows, chan_width = normed.shape
    out_rows = ext_rows - 2 * DILATION_MAX
    places = first_place + DILATION_MAX + jnp.arange(out_rows, dtype=jnp.int32)
    low, high = segment_bounds(lengths, places)
    keep_left = (places - dilation >= low)[:, :, None]
    keep_right = (places + dilation < high)[:, :, None]
    zero = jnp.zeros((), jnp.bfloat16)
    piece = lax.all_gather(normed, "chan", axis=2, tiled=True)
    left = jnp.where(
        keep_left, lax.dynamic_slice_in_dim(piece, DILATION_MAX - dilation, out_rows, axis=1), zero
    )
    middle = lax.slice_in_dim(piece, DILATION_MAX, DILATION_MAX + out_rows, axis=1)
    right = jnp.where(
        keep_right, lax.dynamic_slice_in_dim(piece, DILATION_MAX + dilation, out_rows, axis=1), zero
    )
    acc = jnp.einsum("smk,kf->smf", left, conv_weight[0], preferred_element_type=jnp.float32)
    acc = acc + jnp.einsum(
        "smk,kf->smf", middle, conv_weight[1], preferred_element_type=jnp.float32
    )
    mixed = acc + jnp.einsum(
        "smk,kf->smf", right, conv_weight[2], preferred_element_type=jnp.float32
    )
    inner = jax.nn.gelu(mixed).astype(jnp.bfloat16)
    terms = jnp.einsum("smf,fc->smc", inner, proj_weight, preferred_element_type=jnp.float32)
    update = lax.psum_scatter(
        terms.astype(jnp.bfloat16), "chan", scatter_dimension=2, tiled=True
    ).astype(jnp.float32)
    return (state_mid.astype(jnp.float32) + update).astype(jnp.bfloat16)


def on_device(signal, lengths, dilations, w_conv, w_proj, gains, biases):
    rows = signal.shape[1]
    first_own = lax.axis_index("seq") * rows
    state = signal
    for layer in range(LAYERS):
        normed = norm_act(state, rows, gains[layer], biases[layer])
        extended = extended_2(normed, (("seq", 1),), DILATION_MAX)
        state = conv_layer(
            extended,
            state,
            first_own - DILATION_MAX,
            dilations[layer],
            lengths,
            w_conv[layer],
            w_proj[layer],
        )
    return state


def solution(mesh):
    placed = (
        P(("groups", "dp"), "seq", "chan"),
        P(("groups", "dp"), None),
        P(),
        P(None, None, None, "chan"),
        P(None, "chan", None),
        P(None, "chan"),
        P(None, "chan"),
    )
    return jax.shard_map(
        on_device,
        mesh=mesh,
        in_specs=placed,
        out_specs=P(("groups", "dp"), "seq", "chan"),
        check_vma=False,
    )
```

profile of v0, /device:TPU:8, one launch (start us, length us, event | category | flops | bytes accessed | tf_op | source)
XLA Modules:
  0.0 255.5 jit_solution(4757307982534413759)
XLA Ops:
  6.5 1.5 convert_reduce_fusion.1
  8.0 13.0 %psum.28 = f32[768]{0:T(1024)S(1)} all-reduce(f32[768]{0:T(1024)S(1)} %convert_reduce_fusion.1), channel_id=1, replica_groups=mesh['groups'=2,'seq'=4,'chan'=2,'dp'=2] {'seq','dp'}, use_global_device_ids=true, to_apply=%region_3.0 | all-reduce | flops 768 | bytes 6144 | tf_op jit(solution)/shard_map/psum | solution.py:41
  21.0 1.5 fusion.16
  22.5 13.6 %psum.29 = f32[768]{0:T(1024)S(1)} all-reduce(f32[768]{0:T(1024)S(1)} %fusion.16), channel_id=1, replica_groups=mesh['groups'=2,'seq'=4,'chan'=2,'dp'=2] {'seq','dp'}, use_global_device_ids=true, to_apply=%region_5.6 | all-reduce | flops 768 | bytes 6144 | tf_op jit(solution)/shard_map/psum | solution.py:41
  37.2 1.9 collective-permute-start
  39.1 5.3 %collective-permute-start.1 = (bf16[1,64,768]{2,1,0:T(8,128)(2,1)S(1)}, bf16[1,64,768]{2,1,0:T(8,128)(2,1)S(1)}, u32[]{:S(2)}, u32[]{:S(2)}) collective-permute-start(bf16[1,64,768]{2,1,0:T(8,128)(2,1)S(1)} %get-tuple-element.16), channel_id=1, source_target_pairs={{4,0},{8,4},{12,8},{5,1},{9,5},{13,9},{6,2},{10,6},{14,10},{7,3},{... | collective-permute-start | bytes 294920 | tf_op jit(solution)/shard_map/ppermute | solution.py:22
  45.4 1.3 collective-permute-done.1
  52.7 31.8 %all-gather.3.cloned.1.call-done = bf16[1,768,1536]{2,1,0:T(8,128)(2,1)} async-done(((bf16[1,768,768]{2,1,0:T(8,128)(2,1)}), bf16[1,768,1536]{2,1,0:T(8,128)(2,1)}) %all-gather.3.cloned.1.call-update) | async-done | bytes 2359312 | tf_op jit(solution)/shard_map/all_gather | solution.py:60
  84.4 4.1 %fusion.31 = f32[640,384]{1,0:T(8,128)} fusion(bf16[1,768,1536]{2,1,0:T(8,128)(2,1)} %all-gather.3.cloned.1.call-done, bf16[2,3,1536,384]{3,2,1,0:T(8,128)(2,1)} %param.10), kind=kOutput, calls=%fused_computation.43 | convolution fusion | flops 754974720 | bytes 4128768 | tf_op jit(solution)/shard_map/smk,kf->smf/dot_general | solution.py:69
  88.6 3.6 %fusion.36 = f32[640,384]{1,0:T(8,128)} fusion(bf16[1,768,1536]{2,1,0:T(8,128)(2,1)S(1)} %copy-done.5, s32[]{:T(128)S(6)} %select_n.54, pred[640]{0:T(1024)(128)(4,1)S(1)} %get-tuple-element.20, bf16[2,3,1536,384]{3,2,1,0:T(8,128)(2,1)} %param.10), kind=kOutput, calls=%fused_computation.48 | convolution fusion | flops 755957760 | bytes 4129796 | tf_op jit(solution)/shard_map/smk,kf->smf/dot_general | solution.py:72
  92.2 6.2 %fusion = bf16[1,640,1536]{2,1,0:T(8,128)(2,1)} fusion(bf16[2,384,1536]{2,1,0:T(8,128)(2,1)S(1)} %copy-done.4, f32[640,384]{1,0:T(8,128)} %fusion.36, f32[640,384]{1,0:T(8,128)} %fusion.31, bf16[2,3,1536,384]{3,2,1,0:T(8,128)(2,1)} %param.10, bf16[1,768,1536]{2,1,0:T(8,128)(2,1)} %all-gather.3.cloned.1.call-done, s32[]{:T(128)S(6)} %select_n.51, ...), kind=kOutput, calls=%fused_computation.10 | convolution fusion | flops 1514618880 | bytes 8258564 | tf_op jit(solution)/shard_map/smf,fc->smc/dot_general | solution.py:76
  98.4 30.5 %reduce-scatter.3.cloned.1.call-done = bf16[1,640,768]{2,1,0:T(8,128)(2,1)} async-done(((bf16[1,640,1536]{2,1,0:T(8,128)(2,1)}), bf16[1,640,768]{2,1,0:T(8,128)(2,1)}) %reduce-scatter.3.cloned.1.call-update) | async-done | bytes 983056 | tf_op jit(solution)/shard_map/reduce_scatter | solution.py:77
  128.9 1.5 convert_reduce_fusion
  130.4 12.8 %psum.30 = f32[768]{0:T(1024)S(1)} all-reduce(f32[768]{0:T(1024)S(1)} %get-tuple-element.11), channel_id=1, replica_groups=mesh['groups'=2,'seq'=4,'chan'=2,'dp'=2] {'seq','dp'}, use_global_device_ids=true, to_apply=%region_9.10 | all-reduce | flops 768 | bytes 6144 | tf_op jit(solution)/shard_map/psum | solution.py:41
  143.5 13.6 %psum.31 = f32[768]{0:T(1024)S(1)} all-reduce(f32[768]{0:T(1024)S(1)} %fusion.6), channel_id=1, replica_groups=mesh['groups'=2,'seq'=4,'chan'=2,'dp'=2] {'seq','dp'}, use_global_device_ids=true, to_apply=%region_11.12 | all-reduce | flops 768 | bytes 6144 | tf_op jit(solution)/shard_map/psum | solution.py:41
  158.1 1.9 collective-permute-start.2
  160.0 5.3 %collective-permute-start.3 = (bf16[1,64,768]{2,1,0:T(8,128)(2,1)S(1)}, bf16[1,64,768]{2,1,0:T(8,128)(2,1)S(1)}, u32[]{:S(2)}, u32[]{:S(2)}) collective-permute-start(bf16[1,64,768]{2,1,0:T(8,128)(2,1)S(1)} %get-tuple-element.14), channel_id=1, source_target_pairs={{4,0},{8,4},{12,8},{5,1},{9,5},{13,9},{6,2},{10,6},{14,10},{7,3},{... | collective-permute-start | bytes 294920 | tf_op jit(solution)/shard_map/ppermute | solution.py:22
  166.3 1.3 collective-permute-done.3
  171.4 32.9 %all-gather.5.cloned.1.call-done = bf16[1,768,1536]{2,1,0:T(8,128)(2,1)} async-done(((bf16[1,768,768]{2,1,0:T(8,128)(2,1)}), bf16[1,768,1536]{2,1,0:T(8,128)(2,1)}) %all-gather.5.cloned.1.call-update) | async-done | bytes 2359312 | tf_op jit(solution)/shard_map/all_gather | solution.py:60
  204.3 3.2 %fusion.30 = f32[640,384]{1,0:T(8,128)S(1)} fusion(bf16[1,768,1536]{2,1,0:T(8,128)(2,1)} %all-gather.5.cloned.1.call-done, bf16[2,3,1536,384]{3,2,1,0:T(8,128)(2,1)} %param.10), kind=kOutput, calls=%fused_computation.41 | convolution fusion | flops 754974720 | bytes 4128768 | tf_op jit(solution)/shard_map/smk,kf->smf/dot_general | solution.py:69
  207.5 2.5 fusion.32
  210.0 6.0 %fusion.1 = bf16[1,640,1536]{2,1,0:T(8,128)(2,1)} fusion(bf16[2,384,1536]{2,1,0:T(8,128)(2,1)} %param.11, f32[640,384]{1,0:T(8,128)S(1)} %fusion.32, f32[640,384]{1,0:T(8,128)S(1)} %fusion.30, bf16[2,3,1536,384]{3,2,1,0:T(8,128)(2,1)} %param.10, bf16[1,768,1536]{2,1,0:T(8,128)(2,1)} %all-gather.5.cloned.1.call-done, s32[]{:T(128)S(6)} %select_n.56, ...), kind=kOutput, calls=%fused_computation.11 | convolution fusion | flops 1514618880 | bytes 8258180 | tf_op jit(solution)/shard_map/smf,fc->smc/dot_general | solution.py:76
  216.0 30.6 %reduce-scatter.5.cloned.1.call-done = bf16[1,640,768]{2,1,0:T(8,128)(2,1)} async-done(((bf16[1,640,1536]{2,1,0:T(8,128)(2,1)}), bf16[1,640,768]{2,1,0:T(8,128)(2,1)}) %reduce-scatter.5.cloned.1.call-update) | async-done | bytes 983056 | tf_op jit(solution)/shard_map/reduce_scatter | solution.py:77
  246.6 2.4 fusion.28
  (44 shorter events, 8.8 us)
Async XLA Ops:
  6.5 29.7 %copy-start = (bf16[1,640,768]{2,1,0:T(8,128)(2,1)S(1)}, bf16[1,640,768]{2,1,0:T(8,128)(2,1)}, u32[]{:S(2)}) copy-start(bf16[1,640,768]{2,1,0:T(8,128)(2,1)} %param.7) | copy-start | bytes 2949124
  6.5 29.6 %copy-start.1 = (f32[2,768]{1,0:T(2,128)S(1)}, f32[2,768]{1,0:T(2,128)}, u32[]{:S(2)}) copy-start(f32[2,768]{1,0:T(2,128)} %param.13) | copy-start | bytes 18436
  6.5 29.6 %copy-start.2 = (f32[2,768]{1,0:T(2,128)S(1)}, f32[2,768]{1,0:T(2,128)}, u32[]{:S(2)}) copy-start(f32[2,768]{1,0:T(2,128)} %param.12) | copy-start | bytes 18436
  6.5 77.9 %all-gather.3.cloned.1.call-start = ((), (), s32[]{:S(2)}) async-start(), calls=%async_computation.2 | async-start | bytes 3538944 | tf_op jit(solution)/shard_map/all_gather | solution.py:60
  37.1 10.7 %copy-start.3 = (s32[2]{0:T(128)S(1)}, s32[2]{0:T(128)}, u32[]{:S(2)}) copy-start(s32[2]{0:T(128)} %param.9) | copy-start | bytes 28
  37.2 13.9 %copy-start.7 = (s32[1,8]{1,0:T(1,128)S(1)}, s32[1,8]{1,0:T(1,128)}, u32[]{:S(2)}) copy-start(s32[1,8]{1,0:T(1,128)} %param.8) | copy-start | bytes 100
  37.2 8.2 %collective-permute-start = (bf16[1,64,768]{2,1,0:T(8,128)(2,1)S(1)}, bf16[1,64,768]{2,1,0:T(8,128)(2,1)S(1)}, u32[]{:S(2)}, u32[]{:S(2)}) collective-permute-start(bf16[1,64,768]{2,1,0:T(8,128)(2,1)S(1)} %get-tuple-element.15), channel_id=1, source_target_pairs={{0,4},{4,8},{8,12},{1,5},{5,9},{9,13},{2,6},{6,10},{10,14},{3,7},{... | collective-permute-start | bytes 294920 | tf_op jit(solution)/shard_map/ppermute | solution.py:19
  39.1 7.6 %collective-permute-start.1 = (bf16[1,64,768]{2,1,0:T(8,128)(2,1)S(1)}, bf16[1,64,768]{2,1,0:T(8,128)(2,1)S(1)}, u32[]{:S(2)}, u32[]{:S(2)}) collective-permute-start(bf16[1,64,768]{2,1,0:T(8,128)(2,1)S(1)} %get-tuple-element.16), channel_id=1, source_target_pairs={{4,0},{8,4},{12,8},{5,1},{9,5},{13,9},{6,2},{10,6},{14,10},{7,3},{... | collective-permute-start | bytes 294920 | tf_op jit(solution)/shard_map/ppermute | solution.py:22
  47.8 81.1 %reduce-scatter.3.cloned.1.call-start = ((), (), s32[]{:S(2)}) async-start(), calls=%async_computation.3 | async-start | bytes 2949120 | tf_op jit(solution)/shard_map/reduce_scatter | solution.py:77
  84.4 4.1 %copy-start.5 = (bf16[1,768,1536]{2,1,0:T(8,128)(2,1)S(1)}, bf16[1,768,1536]{2,1,0:T(8,128)(2,1)}, u32[]{:S(2)}) copy-start(bf16[1,768,1536]{2,1,0:T(8,128)(2,1)} %all-gather.3.cloned.1.call-done) | copy-start | bytes 7077892
  88.6 3.6 %copy-start.4 = (bf16[2,384,1536]{2,1,0:T(8,128)(2,1)S(1)}, bf16[2,384,1536]{2,1,0:T(8,128)(2,1)}, u32[]{:S(2)}) copy-start(bf16[2,384,1536]{2,1,0:T(8,128)(2,1)} %param.11) | copy-start | bytes 7077892
  98.4 106.0 %all-gather.5.cloned.1.call-start = ((), (), s32[]{:S(2)}) async-start(), calls=%async_computation.4 | async-start | bytes 3538944 | tf_op jit(solution)/shard_map/all_gather | solution.py:60
  158.1 8.2 %collective-permute-start.2 = (bf16[1,64,768]{2,1,0:T(8,128)(2,1)S(1)}, bf16[1,64,768]{2,1,0:T(8,128)(2,1)S(1)}, u32[]{:S(2)}, u32[]{:S(2)}) collective-permute-start(bf16[1,64,768]{2,1,0:T(8,128)(2,1)S(1)} %get-tuple-element.13), channel_id=1, source_target_pairs={{0,4},{4,8},{8,12},{1,5},{5,9},{9,13},{2,6},{6,10},{10,14},{3,7},{... | collective-permute-start | bytes 294920 | tf_op jit(solution)/shard_map/ppermute | solution.py:19
  160.0 7.6 %collective-permute-start.3 = (bf16[1,64,768]{2,1,0:T(8,128)(2,1)S(1)}, bf16[1,64,768]{2,1,0:T(8,128)(2,1)S(1)}, u32[]{:S(2)}, u32[]{:S(2)}) collective-permute-start(bf16[1,64,768]{2,1,0:T(8,128)(2,1)S(1)} %get-tuple-element.14), channel_id=1, source_target_pairs={{4,0},{8,4},{12,8},{5,1},{9,5},{13,9},{6,2},{10,6},{14,10},{7,3},{... | collective-permute-start | bytes 294920 | tf_op jit(solution)/shard_map/ppermute | solution.py:22
  168.8 77.8 %reduce-scatter.5.cloned.1.call-start = ((), (), s32[]{:S(2)}) async-start(), calls=%async_computation.5 | async-start | bytes 2949120 | tf_op jit(solution)/shard_map/reduce_scatter | solution.py:77
  204.3 3.2 %copy-start.6 = (bf16[1,768,1536]{2,1,0:T(8,128)(2,1)S(1)}, bf16[1,768,1536]{2,1,0:T(8,128)(2,1)}, u32[]{:S(2)}) copy-start(bf16[1,768,1536]{2,1,0:T(8,128)(2,1)} %all-gather.5.cloned.1.call-done) | copy-start | bytes 7077892
Sparse Core Ops, SparseCore 0:
  47.9 36.4 all-gather.2
  98.5 30.3 reduce-scatter.2
  168.9 35.4 all-gather.4
  216.2 30.3 reduce-scatter.4
where the time goes:
time: 258 us; the launch traced here: 256 us
  waiting for transfers between devices  130 us (50%)
  blocking collectives  53 us (21%)
  matrix products  25.6 us (10%)
  between operations  18.3 us (7%)
  starting transfers between devices  14.8 us (6%)
  other arithmetic  12.8 us (5%)
    all_gather x2, waiting for transfers between devices, conv_layer(): piece = lax.all_gather(normed, 'chan', axis=2, tiled=True)  64.7 us
    reduce_scatter x2, waiting for transfers between devices, conv_layer(): lax.psum_scatter(terms.astype(jnp.bfloat16), 'chan', scatter_dimension=2,...  61 us
    psum x4, blocking collectives, batch_total(): return lax.psum(value, ('seq', 'dp'))  53 us
    dot_general x2, matrix products, conv_layer(): jnp.einsum('smf,fc->smc', inner, proj_weight, preferred_element_type=jnp....  12.2 us
    ppermute x2, starting transfers between devices, extended_2(): lax.ppermute(lax.slice_in_dim(block, 0, width, axis=dim), axis, backward)  10.7 us
    dot_general x2, matrix products, conv_layer(): jnp.einsum('smk,kf->smf', middle, conv_weight[1], preferred_element_type=...  7.33 us
    dot_general x2, matrix products, conv_layer(): jnp.einsum('smk,kf->smf', right, conv_weight[2], preferred_element_type=j...  6.09 us
  transfers between devices with their start and end apart: 8, of which 8 were waited for; matrix products, arithmetic and copies ran while one was open for 1% of the time, Pallas kernels for 0%

commit v1 on v0

v1 whole, which is shorter than its diff:
```python
import functools

import jax
import jax.numpy as jnp
from jax import lax
from jax.experimental import pallas as pl
from jax.experimental.pallas import tpu as pltpu
from jax.sharding import PartitionSpec as P

LAYERS = 2
HALO = 64
EPS = 1e-05
F32 = jnp.float32
BF16 = jnp.bfloat16
SWAP = [(0, 1), (1, 0)]
VMEM_LIMIT = 24 << 20


def gelu(x):
    return jax.nn.gelu(x)


def merged(a, b, n):
    gap = a[0] - b[0]
    return jnp.stack([(a[0] + b[0]) * 0.5, a[1] + b[1] + gap * gap * (0.5 * n)])


def batch_stats(local, n):
    total = local
    for axis in ("dp", "seq"):
        size = lax.axis_size(axis)
        step = 1
        while step < size:
            pairs = [(i, i ^ step) for i in range(size)]
            total = merged(total, lax.ppermute(total, axis, pairs), n)
            n *= 2
            step *= 2
    return total[0], total[1] / n


def conv_kernel(pieces, layer, rows, first, n_src, sc, stats, keep_l, keep_r, w_hbm, *rest):
    srcs, (out, xbuf, nbuf, wbuf, p0, p2, sems, wsems) = rest[:n_src], rest[n_src:]
    copies = []
    for tap in range(3):
        copies.append(pltpu.make_async_copy(w_hbm.at[layer, tap], wbuf.at[tap], wsems.at[tap]))
        copies[-1].start()
    moves = []
    for k, (src, at, count, to, half) in enumerate(pieces):
        moves.append(start_piece(srcs[src], at, count, to, half, sc, xbuf, sems.at[k]))
    for m in moves:
        m.wait()
    ext = rows + 2 * HALO
    block = 32
    mean = stats[0:1, :]
    scale = stats[1:2, :]
    bias = stats[2:3, :]

    @pl.loop(0, ext // block)
    def _(i):
        at = pl.ds(pl.multiple_of(i * block, block), block)
        v = xbuf[at, :].astype(F32)
        nbuf[at, :] = gelu((v - mean) * scale + bias).astype(BF16)

    dot = functools.partial(jnp.dot, preferred_element_type=F32)
    copies[0].wait()
    p0[0 : rows + HALO, :] = dot(nbuf[0 : rows + HALO, :], wbuf[0])
    copies[2].wait()
    p2[0 : rows + HALO, :] = dot(nbuf[HALO:ext, :], wbuf[2])
    copies[1].wait()
    mid = dot(nbuf[HALO : HALO + rows, :], wbuf[1])
    d = sc[layer]
    width = out.shape[1]
    for r in range(0, rows, HALO):
        left = shifted(p0, r + HALO - d, HALO)
        right = shifted(p2, r + d, HALO)
        here = slice(first + r, first + r + HALO)
        for c in range(0, width, 128):
            wide = min(128, width - c)
            cs = slice(c, c + wide)
            kl, kr = keep_l[here, :wide] > 0, keep_r[here, :wide] > 0
            mixed = jnp.where(kl, left[:, cs], 0.0) + jnp.where(kr, right[:, cs], 0.0)
            out[r : r + HALO, cs] = gelu(mid[r : r + HALO, cs] + mixed).astype(BF16)


def shifted(ref, start, count):
    base = pl.multiple_of((start // 8) * 8, 8)
    tall = ref[pl.ds(base, count + 8), :]
    return pltpu.roll(tall, (count + 8 - (start - base)) % (count + 8), 0)[:count]


def side_of(sc, back):
    return lax.rem(sc[2] - back + sc[4], sc[4])


def start_piece(src, at, count, to, back, sc, buf, sem):
    if back is None:
        dst = buf.at[pl.ds(to, count), :]
    else:
        width = src.shape[1]
        at_col = pl.multiple_of(side_of(sc, back) * width, 128)
        dst = buf.at[pl.ds(to, count), pl.ds(at_col, width)]
    copy = pltpu.make_async_copy(src.at[pl.ds(at, count), :], dst, sem)
    copy.start()
    return copy


def start_weights(layer, cols, n, sc, w_hbm, wa, wb, wbuf, sems):
    part = wa[0].shape[0]
    copies = [pltpu.make_async_copy(w_hbm.at[layer, :, cols], wbuf.at[0], sems.at[0])]
    for k in range(1, n):
        for j, (src, core) in enumerate(((wa[k - 1], sc[3]), (wb[k - 1], 1 - sc[3]))):
            dst = wbuf.at[k, pl.ds(pl.multiple_of(core * part, 16), part), :]
            copies.append(pltpu.make_async_copy(src, dst, sems.at[2 * k - 1 + j]))
    for c in copies:
        c.start()
    return copies


def update_of(inners, wbuf, cols):
    total = None
    for k, inner in enumerate(inners):
        term = jnp.dot(inner[...], wbuf[k, :, cols], preferred_element_type=F32)
        term = term.astype(BF16).astype(F32)
        total = term if total is None else total + term
    return total


ANY = pl.BlockSpec(memory_space=pl.ANY)
INV = pl.BlockSpec(memory_space=pltpu.VMEM)
INS = pl.BlockSpec(memory_space=pltpu.SMEM)


def conv(pieces, srcs, layer, rows, first, sc, stats, keep, w_conv):
    channels, width = w_conv.shape[2:]
    ext = rows + 2 * HALO
    return pl.pallas_call(
        functools.partial(conv_kernel, pieces, layer, rows, first, len(srcs)),
        out_shape=jax.ShapeDtypeStruct((rows, width), BF16),
        in_specs=[INS, INV, INV, INV, ANY] + [ANY] * len(srcs),
        out_specs=INV,
        scratch_shapes=[
            pltpu.VMEM((ext, channels), BF16),
            pltpu.VMEM((ext, channels), BF16),
            pltpu.VMEM((3, channels, width), BF16),
            pltpu.VMEM((rows + HALO + 8, width), F32),
            pltpu.VMEM((rows + HALO + 8, width), F32),
            pltpu.SemaphoreType.DMA((len(pieces),)),
            pltpu.SemaphoreType.DMA((3,)),
        ],
        compiler_params=pltpu.CompilerParams(vmem_limit_bytes=VMEM_LIMIT),
        name=f"conv{layer}",
    )(sc, stats, keep[0], keep[1], w_conv, *srcs)


def proj0_kernel(pieces, rows, n, n_src, sc, *rest):
    inners, rest = rest[:n], rest[n:]
    w_hbm, wa, wb, rest = rest[0], rest[1:n], rest[n : 2 * n - 1], rest[2 * n - 1 :]
    srcs, (out, stat, xbuf, wbuf, sems, wsems) = rest[:n_src], rest[n_src:]
    copies = start_weights(0, slice(None), n, sc, w_hbm, wa, wb, wbuf, wsems)
    for k, (src, at, count, to, back) in enumerate(pieces):
        copies.append(start_piece(srcs[src], at, count, to, back, sc, xbuf, sems.at[k]))
    for c in copies:
        c.wait()
    for col in range(0, out.shape[1], 256):
        cs = slice(col, col + 256)
        new = (xbuf[:, cs].astype(F32) + update_of(inners, wbuf, cs)).astype(BF16)
        out[:, cs] = new
        v = new.astype(F32)
        pivot = jnp.mean(v[0:8], axis=0, keepdims=True)
        gap = v - pivot
        s1 = jnp.sum(gap, axis=0, keepdims=True)
        s2 = jnp.sum(gap * gap, axis=0, keepdims=True)
        off = s1 * (1.0 / rows)
        stat[0:1, cs] = pivot + off
        stat[1:2, cs] = s2 - s1 * off


def proj0(pieces, srcs, rows, sc, inners, w_proj, wa, wb):
    hidden, channels = w_proj.shape[1:]
    n = len(inners)
    return pl.pallas_call(
        functools.partial(proj0_kernel, pieces, rows, n, len(srcs)),
        out_shape=(
            jax.ShapeDtypeStruct((rows, channels), BF16),
            jax.ShapeDtypeStruct((2, channels), F32),
        ),
        in_specs=[INS] + [INV] * n + [ANY] * (2 * n - 1 + len(srcs)),
        out_specs=(INV, INV),
        scratch_shapes=[
            pltpu.VMEM((rows, channels), BF16),
            pltpu.VMEM((n, hidden, channels), BF16),
            pltpu.SemaphoreType.DMA((len(pieces),)),
            pltpu.SemaphoreType.DMA((2 * n - 1,)),
        ],
        compiler_params=pltpu.CompilerParams(vmem_limit_bytes=VMEM_LIMIT),
        name="proj0",
    )(sc, *inners, w_proj, *wa, *wb, *srcs)


def proj1_kernel(n, sc, *rest):
    inners, rest = rest[:n], rest[n:]
    w_hbm, wa, wb, rest = rest[0], rest[1:n], rest[n : 2 * n - 1], rest[2 * n - 1 :]
    state, out, xbuf, wbuf, sem, wsems = rest
    width = out.shape[1]
    cols = pl.ds(pl.multiple_of(sc[2] * width, 128), width)
    copies = start_weights(1, cols, n, sc, w_hbm, wa, wb, wbuf, wsems)
    copies.append(pltpu.make_async_copy(state.at[:, cols], xbuf, sem))
    copies[-1].start()
    for c in copies:
        c.wait()
    for col in range(0, width, 128):
        cs = slice(col, col + 128)
        out[:, cs] = (xbuf[:, cs].astype(F32) + update_of(inners, wbuf, cs)).astype(BF16)


def proj1(rows, sc, inners, w_proj, wa, wb, state):
    hidden, channels = w_proj.shape[1:]
    n = len(inners)
    width = channels // n
    return pl.pallas_call(
        functools.partial(proj1_kernel, n),
        out_shape=jax.ShapeDtypeStruct((rows, width), BF16),
        in_specs=[INS] + [INV] * n + [ANY] * (2 * n),
        out_specs=INV,
        scratch_shapes=[
            pltpu.VMEM((rows, width), BF16),
            pltpu.VMEM((n, hidden, width), BF16),
            pltpu.SemaphoreType.DMA,
            pltpu.SemaphoreType.DMA((2 * n - 1,)),
        ],
        compiler_params=pltpu.CompilerParams(vmem_limit_bytes=VMEM_LIMIT),
        name="proj1",
    )(sc, *inners, w_proj, *wa, *wb, state)


def keeps(lengths, places, dilation):
    ends = jnp.cumsum(lengths, dtype=jnp.int32)
    left = jnp.zeros(places.shape, jnp.bool_)
    right = jnp.zeros(places.shape, jnp.bool_)
    for k in range(lengths.shape[0]):
        start, end = ends[k] - lengths[k], ends[k]
        left |= (places - dilation < start) & (start <= places)
        right |= (places < end) & (end <= places + dilation)
    return jnp.where(left, 0.0, 1.0).astype(F32), jnp.where(right, 0.0, 1.0).astype(F32)


def on_device(signal, lengths, dilations, w_conv, w_proj, gains, biases):
    own = signal[0]
    rows, width = own.shape
    half = rows // 2
    chan, core, place = lax.axis_index("chan"), lax.axis_index("dp"), lax.axis_index("seq")
    n_seq, n = lax.axis_size("seq"), lax.axis_size("chan")
    up = [(i, i + 1) for i in range(n_seq - 1)]
    down = [(i + 1, i) for i in range(n_seq - 1)]
    perm = lax.ppermute
    sc = jnp.concatenate([dilations, jnp.stack([chan, core, jnp.int32(n)]).astype(jnp.int32)])

    def others(value):
        return [perm(value, "chan", [(i, (i + k) % n) for i in range(n)]) for k in range(1, n)]

    def true_order(mine, other):
        parts = [mine] + list(other)
        if n == 2:
            first = jnp.where(chan == 0, parts[0], parts[1])
            return jnp.concatenate([first, jnp.where(chan == 0, parts[1], parts[0])], axis=-1)
        stack = jnp.take(jnp.stack(parts), (chan - jnp.arange(n)) % n, axis=0)
        return jnp.concatenate([stack[k] for k in range(n)], axis=-1)

    edges = others(jnp.concatenate([own[:HALO], own[rows - HALO :]]))
    cut = half + HALO
    end = rows - HALO
    rest_a = others(own[HALO:cut])
    rest_b = others(own[cut:end])
    low0 = perm(true_order(own[end:], [e[HALO:] for e in edges]), "seq", up)
    high0 = perm(true_order(own[:HALO], [e[:HALO] for e in edges]), "seq", down)

    part = w_proj.shape[1] // 2
    mine0 = lax.dynamic_slice(w_proj, (0, core * part, 0), (1, part, n * width))[0]
    wa0 = others(mine0)
    wb0 = [perm(w, "dp", SWAP) for w in wa0]
    wa1 = []
    for k in range(1, n):
        at = (1, core * part, (chan + k) % n * width)
        mine1 = lax.dynamic_slice(w_proj, at, (1, part, width))[0]
        wa1.append(perm(mine1, "chan", [(i, (i + k) % n) for i in range(n)]))
    wb1 = [perm(w, "dp", SWAP) for w in wa1]

    values = own.astype(F32)
    mean = jnp.mean(values, axis=0)
    local = jnp.stack([mean, jnp.sum(jnp.square(values - mean), axis=0)])
    mean, var = batch_stats(local, rows)
    mine = jnp.stack([mean, lax.rsqrt(var + EPS) * gains[0], biases[0], gains[1], biases[1]])
    vecs = true_order(mine, others(mine))

    places = place * rows + lax.broadcasted_iota(jnp.int32, (rows, 128), 0)
    keep = [keeps(lengths[0], places, dilations[layer]) for layer in range(LAYERS)]

    srcs = (own, low0, high0, *edges, *rest_a, *rest_b)
    behind = [(k, 2 + k, 1 + n + k, 2 * n + k) for k in range(1, n)]
    pieces_a = [(1, 0, HALO, 0, None), (0, 0, cut, HALO, 0)]
    pieces_b = [(0, half - HALO, half + HALO, 0, 0), (2, 0, HALO, half + HALO, None)]
    res_a, res_b = [(0, 0, half, 0, 0)], [(0, half, half, 0, 0)]
    for k, e, a, b in behind:
        pieces_a += [(e, 0, HALO, HALO, k), (a, 0, cut - HALO, 2 * HALO, k)]
        pieces_b += [
            (a, half - 2 * HALO, 2 * HALO, 0, k),
            (b, 0, end - cut, 2 * HALO, k),
            (e, HALO, HALO, 2 * HALO + end - cut, k),
        ]
        res_a += [(e, 0, HALO, 0, k), (a, 0, half - HALO, HALO, k)]
        res_b += [
            (a, half - HALO, HALO, 0, k),
            (b, 0, end - cut, HALO, k),
            (e, HALO, HALO, HALO + end - cut, k),
        ]
    early = srcs[: 1 + 2 * n]
    inner_a = conv(pieces_a, early, 0, half, 0, sc, vecs[:3], keep[0], w_conv)
    inner_b = conv(pieces_b, srcs, 0, half, half, sc, vecs[:3], keep[0], w_conv)
    inners_a = [inner_a] + others(inner_a)
    inners_b = [inner_b] + others(inner_b)
    state_a, stat_a = proj0(res_a, early, half, sc, inners_a, w_proj, wa0, wb0)
    state_b, stat_b = proj0(res_b, srcs, half, sc, inners_b, w_proj, wa0, wb0)
    high1 = perm(state_a[:HALO], "seq", down)
    low1 = perm(state_b[half - HALO :], "seq", up)

    mean, var = batch_stats(merged(stat_a, stat_b, half), rows)
    vecs1 = jnp.stack([mean, lax.rsqrt(var + EPS) * vecs[3], vecs[4]])

    srcs = (state_a, state_b, low1, high1)
    pieces_a = ((2, 0, HALO, 0, None), (0, 0, half, HALO, None), (1, 0, HALO, half + HALO, None))
    pieces_b = (
        (0, half - HALO, HALO, 0, None),
        (1, 0, half, HALO, None),
        (3, 0, HALO, half + HALO, None),
    )
    inner_a = conv(pieces_a, srcs, 1, half, 0, sc, vecs1, keep[1], w_conv)
    inner_b = conv(pieces_b, srcs, 1, half, half, sc, vecs1, keep[1], w_conv)
    inners_a = [inner_a] + others(inner_a)
    inners_b = [inner_b] + others(inner_b)
    out_a = proj1(half, sc, inners_a, w_proj, wa1, wb1, state_a)
    out_b = proj1(half, sc, inners_b, w_proj, wa1, wb1, state_b)
    return jnp.concatenate([out_a, out_b])[None]


def solution(mesh):
    placed = (
        P(("groups", "dp"), "seq", "chan"),
        P(("groups", "dp"), None),
        P(),
        P(None, None, None, "chan"),
        P(None, "chan", None),
        P(None, "chan"),
        P(None, "chan"),
    )
    return jax.shard_map(
        on_device,
        mesh=mesh,
        in_specs=placed,
        out_specs=P(("groups", "dp"), "seq", "chan"),
        check_vma=False,
    )
```

time: 258 us -> 141 us (0.55)
  waiting for transfers between devices: 130 us -> 23 us
  blocking collectives: 53 us -> 0 us
  Pallas kernels: 0 us -> 36 us
  matrix products: 25.6 us -> 0 us
  local copies, waits for them, and re-layouts: 0.71 us -> 17.2 us
  starting transfers between devices: 14.8 us -> 27.9 us
  other arithmetic: 12.8 us -> 23.4 us
  between operations: 18.3 us -> 10.3 us
    all_gather x2 -> x0, waiting for transfers between devices: 64.7 us -> none  [conv_layer(): piece = lax.all_gather(normed, 'chan', axis=2, tiled=True)]
    reduce_scatter x2 -> x0, waiting for transfers between devices: 61 us -> none  [conv_layer(): lax.psum_scatter(terms.astype(jnp.bfloat16), 'chan', scatter_dimension=2,...]
    psum x4 -> x0, blocking collectives: 53 us -> none  [batch_total(): return lax.psum(value, ('seq', 'dp'))]
    pallas_call x0 -> x8, Pallas kernels: none -> 36 us  [the longest x4 25.8 us: conv(): pl.pallas_call(functools.partial(conv_kernel, pieces, layer, rows, first,...]
    dot_general x6 -> x0, matrix products: 25.6 us -> none  [the longest x2 12.2 us: conv_layer(): jnp.einsum('smf,fc->smc', inner, proj_weight, preferred_element_type=jnp....]
    ppermute x4 -> x22, waiting for transfers between devices: 4.48 us -> 23 us  [the longest x9 9.01 us: others(): perm(value, 'chan', [(i, (i + k) % n) for i in range(n)])]
    ppermute x4 -> x22, starting transfers between devices: 14.5 us -> 27.9 us  [the longest x9 9.85 us: others(): perm(value, 'chan', [(i, (i + k) % n) for i in range(n)])]
    select_n x0 -> x4, other arithmetic: none -> 11.9 us  [the longest x2 11.1 us: keeps(): jnp.where(right, 0.0, 1.0).astype(F32)]
  transfers between devices with their start and end apart: 8 -> 22, of which waited for: 8 -> 9; matrix products, arithmetic and copies ran while one was open for 1% -> 21% of each run, Pallas kernels for 0% -> 22%
where the time goes in v1:
time: 141 us; the launch traced here: 138 us
  Pallas kernels  36 us (26%)
  starting transfers between devices  27.9 us (20%)
  other arithmetic  23.4 us (17%)
  waiting for transfers between devices  23 us (16%)
  local copies, waits for them, and re-layouts  17.2 us (12%)
  between operations  10.3 us (7%)
    pallas_call x4, Pallas kernels, conv(): pl.pallas_call(functools.partial(conv_kernel, pieces, layer, rows, first,...  25.8 us
    select_n x2, other arithmetic, keeps(): jnp.where(right, 0.0, 1.0).astype(F32)  11.1 us
    ppermute x9, starting transfers between devices, others(): perm(value, 'chan', [(i, (i + k) % n) for i in range(n)])  9.85 us
    ppermute x9, waiting for transfers between devices, others(): perm(value, 'chan', [(i, (i + k) % n) for i in range(n)])  9.01 us
    unnamed x22, local copies, waits for them, and re-layouts  6.98 us
    pallas_call x2, Pallas kernels, proj0(): pl.pallas_call(functools.partial(proj0_kernel, pieces, rows, n, len(srcs)...  6.75 us
    ppermute x6, starting transfers between devices, batch_stats(): total = merged(total, lax.ppermute(total, axis, pairs), n)  5.43 us
    ppermute x1, waiting for transfers between devices, on_device(): high0 = perm(true_order(own[:HALO], [e[:HALO] for e in edges]), 'seq', down)  4.37 us
  transfers between devices with their start and end apart: 22, of which 9 were waited for; matrix products, arithmetic and copies ran while one was open for 21% of the time, Pallas kernels for 22%

profile of v1, /device:TPU:8, one launch (start us, length us, event | category | flops | bytes accessed | tf_op | source)
XLA Modules:
  0.0 137.9 jit_solution(15864110366117778773)
XLA Ops:
  27.2 3.0 %collective-permute-start.2 = (f32[2,768]{1,0:T(2,128)}, f32[2,768]{1,0:T(2,128)}, u32[]{:S(2)}, u32[]{:S(2)}) collective-permute-start(f32[2,768]{1,0:T(2,128)} %pad_maximum_fusion.8), channel_id=1, source_target_pairs={{0,8},{4,12},{8,0},{12,4},{1,9},{5,13},{9,1},{13,5},{2,10},{6,14},... | collective-permute-start | bytes 18440 | tf_op jit(solution)/shard_map/ppermute | solution.py:35
  30.2 5.6 %fusion.116 = (f32[640]{0:T(1024)S(1)}, f32[640]{0:T(1024)S(1)}) fusion(s32[]{:T(128)} %bitcast.19, s32[]{:T(128)} %bitcast.17, s32[]{:T(128)} %bitcast.15, s32[]{:T(128)} %bitcast.13, s32[]{:T(128)} %bitcast.11, s32[]{:T(128)} %bitcast.9, s32[]{:T(128)} %bitcast.7, s32[]{:T(128)} %bitcast.5, s32[]{:T(128)} %bitcast.3, s32[]{:T(128)S(6)} %mul.168, ...), kind=kLoop, calls=%fused_computation.155 | loop fusion | flops 42880 | bytes 5192 | tf_op jit(solution)/shard_map/jit(_where)/select_n | solution.py:244
  40.8 1.9 %collective-permute-done.3 = f32[5,768]{1,0:T(8,128)} collective-permute-done((f32[5,768]{1,0:T(8,128)}, f32[5,768]{1,0:T(8,128)}, u32[]{:S(2)}, u32[]{:S(2)}) %collective-permute-start.3) | collective-permute-done | bytes 15392 | tf_op jit(solution)/shard_map/ppermute | solution.py:259
  43.5 2.8 %collective-permute-start.5 = (bf16[64,1536]{1,0:T(8,128)(2,1)S(1)}, bf16[64,1536]{1,0:T(8,128)(2,1)S(1)}, u32[]{:S(2)}, u32[]{:S(2)}) collective-permute-start(bf16[64,1536]{1,0:T(8,128)(2,1)S(1)} %pad_maximum_fusion.1), channel_id=1, source_target_pairs={{0,4},{4,8},{8,12},{1,5},{5,9},{9,13},{2,6},{6,10},{10,14},{3,7},{... | collective-permute-start | bytes 589832 | tf_op jit(solution)/shard_map/ppermute | solution.py:274
  46.5 3.0 %collective-permute-start.6 = (bf16[64,1536]{1,0:T(8,128)(2,1)S(1)}, bf16[64,1536]{1,0:T(8,128)(2,1)S(1)}, u32[]{:S(2)}, u32[]{:S(2)}) collective-permute-start(bf16[64,1536]{1,0:T(8,128)(2,1)S(1)} %pad_maximum_fusion.2), channel_id=1, source_target_pairs={{4,0},{8,4},{12,8},{5,1},{9,5},{13,9},{6,2},{10,6},{14,10},{7,3},{... | collective-permute-start | bytes 589832 | tf_op jit(solution)/shard_map/ppermute | solution.py:275
  49.5 1.8 %collective-permute-done.5.rest_1_.rest_6_ = bf16[64,1536]{1,0:T(8,128)(2,1)S(1)} collective-permute-done((bf16[64,1536]{1,0:T(8,128)(2,1)S(1)}, bf16[64,1536]{1,0:T(8,128)(2,1)S(1)}, u32[]{:S(2)}, u32[]{:S(2)}) %collective-permute-start.5) | collective-permute-done | bytes 196640 | tf_op jit(solution)/shard_map/ppermute | solution.py:274
  51.3 4.4 %collective-permute-done.6.rest_2_.rest_7_ = bf16[64,1536]{1,0:T(8,128)(2,1)S(1)} collective-permute-done((bf16[64,1536]{1,0:T(8,128)(2,1)S(1)}, bf16[64,1536]{1,0:T(8,128)(2,1)S(1)}, u32[]{:S(2)}, u32[]{:S(2)}) %collective-permute-start.6) | collective-permute-done | bytes 196640 | tf_op jit(solution)/shard_map/ppermute | solution.py:275
  56.0 3.0 %copy-done = bf16[2,3,1536,384]{3,2,1,0:T(8,128)(2,1)S(1)} copy-done((bf16[2,3,1536,384]{3,2,1,0:T(8,128)(2,1)S(1)}, bf16[2,3,1536,384]{3,2,1,0:T(8,128)(2,1)}, u32[]{:S(2)}) %copy-start) | copy-done | bytes 7077912
  59.0 6.7 %conv0.3.rest_0_ = bf16[320,384]{1,0:T(8,128)(2,1)S(1)} custom-call(s32[5]{0:T(128)S(1)} %pad_add_fusion.sc, f32[3,1536]{1,0:T(4,128)S(1)} %fusion.2.stats, f32[640,128]{1,0:T(8,128)S(1)} %iota.13.keep_l, f32[640,128]{1,0:T(8,128)S(1)} %iota.14.keep_r, bf16[2,3,1536,384]{3,2,1,0:T(8,128)(2,1)S(1)} %copy-done, bf16[640,768]{1,0:T(8,128)(2,1)S(1)} %bitcast.46, ...), custom_call_target="tpu_custom_call" | custom-call | tf_op jit(solution)/shard_map/conv0/pallas_call | solution.py:136
  67.3 6.7 %conv0.2.rest_0_ = bf16[320,384]{1,0:T(8,128)(2,1)S(1)} custom-call(s32[5]{0:T(128)S(1)} %pad_add_fusion.sc, f32[3,1536]{1,0:T(4,128)S(1)} %fusion.2.stats, f32[640,128]{1,0:T(8,128)S(1)} %iota.13.keep_l, f32[640,128]{1,0:T(8,128)S(1)} %iota.14.keep_r, bf16[2,3,1536,384]{3,2,1,0:T(8,128)(2,1)S(1)} %copy-done, bf16[640,768]{1,0:T(8,128)(2,1)S(1)} %bitcast.47, ...), custom_call_target="tpu_custom_call" | custom-call | tf_op jit(solution)/shard_map/conv0/pallas_call | solution.py:136
  74.6 3.4 %proj0.3 = (bf16[320,1536]{1,0:T(8,128)(2,1)S(1)}, f32[2,1536]{1,0:T(2,128)S(1)}) custom-call(s32[5]{0:T(128)S(1)} %pad_add_fusion.sc, bf16[320,384]{1,0:T(8,128)(2,1)S(1)} %conv0.3.rest_0_, bf16[320,384]{1,0:T(8,128)(2,1)S(1)} %collective-permute-done.12.rest_1_, bf16[2,384,1536]{2,1,0:T(8,128)(2,1)S(1)} %copy-done.3, ...), custom_call_target="tpu_custom_call" | custom-call | tf_op jit(solution)/shard_map/proj0/pallas_call | solution.py:181
  78.0 3.4 %collective-permute-done.8.rest_1_ = bf16[320,384]{1,0:T(8,128)(2,1)S(1)} collective-permute-done((bf16[320,384]{1,0:T(8,128)(2,1)S(1)}, bf16[320,384]{1,0:T(8,128)(2,1)S(1)}, u32[]{:S(2)}, u32[]{:S(2)}) %collective-permute-start.8) | collective-permute-done | bytes 245792 | tf_op jit(solution)/shard_map/ppermute | solution.py:259
  81.4 3.4 %proj0.2 = (bf16[320,1536]{1,0:T(8,128)(2,1)S(1)}, f32[2,1536]{1,0:T(2,128)S(1)}) custom-call(s32[5]{0:T(128)S(1)} %pad_add_fusion.sc, bf16[320,384]{1,0:T(8,128)(2,1)S(1)} %conv0.2.rest_0_, bf16[320,384]{1,0:T(8,128)(2,1)S(1)} %collective-permute-done.8.rest_1_, bf16[2,384,1536]{2,1,0:T(8,128)(2,1)S(1)} %copy-done.3, ...), custom_call_target="tpu_custom_call" | custom-call | tf_op jit(solution)/shard_map/proj0/pallas_call | solution.py:181
  88.9 2.0 %collective-permute-done.14 = f32[2,1536]{1,0:T(2,128)S(1)} collective-permute-done((f32[2,1536]{1,0:T(2,128)S(1)}, f32[2,1536]{1,0:T(2,128)S(1)}, u32[]{:S(2)}, u32[]{:S(2)}) %collective-permute-start.14) | collective-permute-done | bytes 12320 | tf_op jit(solution)/shard_map/ppermute | solution.py:35
  92.0 5.5 %fusion.100 = (f32[640]{0:T(1024)S(1)}, f32[640]{0:T(1024)S(1)}) fusion(s32[]{:T(128)} %bitcast.26, s32[]{:T(128)} %bitcast.19, s32[]{:T(128)} %bitcast.17, s32[]{:T(128)} %bitcast.15, s32[]{:T(128)} %bitcast.13, s32[]{:T(128)} %bitcast.11, s32[]{:T(128)} %bitcast.9, s32[]{:T(128)} %bitcast.7, s32[]{:T(128)} %bitcast.5, s32[]{:T(128)S(6)} %mul.168, ...), kind=kLoop, calls=%fused_computation.139 | loop fusion | flops 42880 | bytes 5192 | tf_op jit(solution)/shard_map/jit(_where)/select_n | solution.py:244
  98.5 3.5 %collective-permute-start.16 = (bf16[64,1536]{1,0:T(8,128)(2,1)S(1)}, bf16[64,1536]{1,0:T(8,128)(2,1)S(1)}, u32[]{:S(2)}, u32[]{:S(2)}) collective-permute-start(bf16[64,1536]{1,0:T(8,128)(2,1)S(1)} %slice.269), channel_id=1, source_target_pairs={{0,4},{4,8},{8,12},{1,5},{5,9},{9,13},{2,6},{6,10},{10,14},{3,7},{... | collective-permute-start | bytes 589832 | tf_op jit(solution)/shard_map/ppermute | solution.py:324
  102.9 2.6 %collective-permute-start.17 = (bf16[64,1536]{1,0:T(8,128)(2,1)S(1)}, bf16[64,1536]{1,0:T(8,128)(2,1)S(1)}, u32[]{:S(2)}, u32[]{:S(2)}) collective-permute-start(bf16[64,1536]{1,0:T(8,128)(2,1)S(1)} %slice.270), channel_id=1, source_target_pairs={{4,0},{8,4},{12,8},{5,1},{9,5},{13,9},{6,2},{10,6},{14,10},{7,3},{... | collective-permute-start | bytes 589832 | tf_op jit(solution)/shard_map/ppermute | solution.py:323
  107.7 4.1 %collective-permute-done.17.rest_3_ = bf16[64,1536]{1,0:T(8,128)(2,1)S(1)} collective-permute-done((bf16[64,1536]{1,0:T(8,128)(2,1)S(1)}, bf16[64,1536]{1,0:T(8,128)(2,1)S(1)}, u32[]{:S(2)}, u32[]{:S(2)}) %collective-permute-start.17) | collective-permute-done | bytes 196640 | tf_op jit(solution)/shard_map/ppermute | solution.py:323
  112.2 3.0 %copy-done.1 = bf16[2,3,1536,384]{3,2,1,0:T(8,128)(2,1)S(1)} copy-done((bf16[2,3,1536,384]{3,2,1,0:T(8,128)(2,1)S(1)}, bf16[2,3,1536,384]{3,2,1,0:T(8,128)(2,1)}, u32[]{:S(2)}) %copy-start.1) | copy-done | bytes 7077912
  115.2 6.2 %conv1.3.rest_0_ = bf16[320,384]{1,0:T(8,128)(2,1)S(1)} custom-call(s32[5]{0:T(128)S(1)} %pad_add_fusion.sc, f32[3,1536]{1,0:T(4,128)S(1)} %fusion.3.stats, f32[640,128]{1,0:T(8,128)S(1)} %iota.15.keep_l, f32[640,128]{1,0:T(8,128)S(1)} %iota.16.keep_r, bf16[2,3,1536,384]{3,2,1,0:T(8,128)(2,1)S(1)} %copy-done.1, bf16[320,1536]{1,0:T(8,128)(2,1)S(1)} %copy-done.7, ...), custom_call_target="tpu_custom_call" | custom-call | tf_op jit(solution)/shard_map/conv1/pallas_call | solution.py:136
  121.9 6.2 %conv1.2.rest_0_ = bf16[320,384]{1,0:T(8,128)(2,1)S(1)} custom-call(s32[5]{0:T(128)S(1)} %pad_add_fusion.sc, f32[3,1536]{1,0:T(4,128)S(1)} %fusion.3.stats, f32[640,128]{1,0:T(8,128)S(1)} %iota.15.keep_l, f32[640,128]{1,0:T(8,128)S(1)} %iota.16.keep_r, bf16[2,3,1536,384]{3,2,1,0:T(8,128)(2,1)S(1)} %copy-done.1, bf16[320,1536]{1,0:T(8,128)(2,1)S(1)} %copy-done.7, ...), custom_call_target="tpu_custom_call" | custom-call | tf_op jit(solution)/shard_map/conv1/pallas_call | solution.py:136
  129.7 1.8 %proj1.3 = bf16[320,768]{1,0:T(8,128)(2,1)S(1)} custom-call(s32[5]{0:T(128)S(1)} %pad_add_fusion.sc, bf16[320,384]{1,0:T(8,128)(2,1)S(1)} %conv1.3.rest_0_, bf16[320,384]{1,0:T(8,128)(2,1)S(1)} %collective-permute-done.21.rest_1_, bf16[2,384,1536]{2,1,0:T(8,128)(2,1)S(1)} %copy-done.3, bf16[192,768]{1,0:T(8,128)(2,1)S(1)} %collective-permute-done.19.rest_3_, ...), custom_call_target="tpu_custom_call" | custom-call | tf_op jit(solution)/shard_map/proj1/pallas_call | solution.py:220
  131.4 3.7 %collective-permute-done.18.rest_1_ = bf16[320,384]{1,0:T(8,128)(2,1)S(1)} collective-permute-done((bf16[320,384]{1,0:T(8,128)(2,1)S(1)}, bf16[320,384]{1,0:T(8,128)(2,1)S(1)}, u32[]{:S(2)}, u32[]{:S(2)}) %collective-permute-start.18) | collective-permute-done | bytes 245792 | tf_op jit(solution)/shard_map/ppermute | solution.py:259
  135.1 1.8 %proj1.2 = bf16[320,768]{1,0:T(8,128)(2,1)S(1)} custom-call(s32[5]{0:T(128)S(1)} %pad_add_fusion.sc, bf16[320,384]{1,0:T(8,128)(2,1)S(1)} %conv1.2.rest_0_, bf16[320,384]{1,0:T(8,128)(2,1)S(1)} %collective-permute-done.18.rest_1_, bf16[2,384,1536]{2,1,0:T(8,128)(2,1)S(1)} %copy-done.3, bf16[192,768]{1,0:T(8,128)(2,1)S(1)} %collective-permute-done.19.rest_3_, ...), custom_call_target="tpu_custom_call" | custom-call | tf_op jit(solution)/shard_map/proj1/pallas_call | solution.py:220
  (96 shorter events, 38.3 us)
Async XLA Ops:
  3.7 10.1 %collective-permute-start = (f32[2,768]{1,0:T(2,128)}, f32[2,768]{1,0:T(2,128)}, u32[]{:S(2)}, u32[]{:S(2)}) collective-permute-start(f32[2,768]{1,0:T(2,128)} %pad_maximum_fusion.6), channel_id=1, source_target_pairs={{0,1},{1,0},{2,3},{3,2},{4,5},{5,4},{6,7},{7,6},{8,9},{9,8},{10,11... | collective-permute-start | bytes 18440 | tf_op jit(solution)/shard_map/ppermute | solution.py:35
  4.4 39.1 %collective-permute-start.4 = (bf16[128,768]{1,0:T(8,128)(2,1)}, bf16[128,768]{1,0:T(8,128)(2,1)S(1)}, u32[]{:S(2)}, u32[]{:S(2)}) collective-permute-start(bf16[128,768]{1,0:T(8,128)(2,1)} %pad_maximum_fusion), channel_id=1, source_target_pairs={{0,2},{2,0},{1,3},{3,1},{4,6},{6,4},{5,7},{7,5},{8,10},{10,8},{9,1... | collective-permute-start | bytes 589832 | tf_op jit(solution)/shard_map/ppermute | solution.py:259
  6.7 49.0 %collective-permute-start.7 = (bf16[320,768]{1,0:T(8,128)(2,1)}, bf16[320,768]{1,0:T(8,128)(2,1)}, u32[]{:S(2)}, u32[]{:S(2)}) collective-permute-start(bf16[320,768]{1,0:T(8,128)(2,1)} %slice_bitcast_fusion), channel_id=1, source_target_pairs={{0,2},{2,0},{1,3},{3,1},{4,6},{6,4},{5,7},{7,5},{8,10},{10,8},{9,1... | collective-permute-start | bytes 1474568 | tf_op jit(solution)/shard_map/ppermute | solution.py:259
  8.0 41.6 %collective-permute-start.11 = (bf16[192,768]{1,0:T(8,128)(2,1)}, bf16[192,768]{1,0:T(8,128)(2,1)}, u32[]{:S(2)}, u32[]{:S(2)}) collective-permute-start(bf16[192,768]{1,0:T(8,128)(2,1)} %slice_bitcast_fusion.1), channel_id=1, source_target_pairs={{0,2},{2,0},{1,3},{3,1},{4,6},{6,4},{5,7},{7,5},{8,10},{10,8},{9,1... | collective-permute-start | bytes 884744 | tf_op jit(solution)/shard_map/ppermute | solution.py:259
  10.3 36.1 %collective-permute-start.9 = (bf16[192,1536]{1,0:T(8,128)(2,1)}, bf16[192,1536]{1,0:T(8,128)(2,1)}, u32[]{:S(2)}, u32[]{:S(2)}) collective-permute-start(bf16[192,1536]{1,0:T(8,128)(2,1)} %dynamic-slice_bitcast_fusion), channel_id=1, source_target_pairs={{0,2},{2,0},{1,3},{3,1},{4,6},{6,4},{5,7},{7,5},{8,10},{10,8},{9,1... | collective-permute-start | bytes 1769480 | tf_op jit(solution)/shard_map/ppermute | solution.py:259
  14.5 11.2 %collective-permute-start.1 = (f32[2,768]{1,0:T(2,128)S(1)}, f32[2,768]{1,0:T(2,128)}, u32[]{:S(2)}, u32[]{:S(2)}) collective-permute-start(f32[2,768]{1,0:T(2,128)S(1)} %pad_maximum_fusion.7), channel_id=1, source_target_pairs={{0,4},{4,0},{8,12},{12,8},{1,5},{5,1},{9,13},{13,9},{2,6},{6,2},{1... | collective-permute-start | bytes 18440 | tf_op jit(solution)/shard_map/ppermute | solution.py:35
  27.2 8.6 %collective-permute-start.2 = (f32[2,768]{1,0:T(2,128)}, f32[2,768]{1,0:T(2,128)}, u32[]{:S(2)}, u32[]{:S(2)}) collective-permute-start(f32[2,768]{1,0:T(2,128)} %pad_maximum_fusion.8), channel_id=1, source_target_pairs={{0,8},{4,12},{8,0},{12,4},{1,9},{5,13},{9,1},{13,5},{2,10},{6,14},... | collective-permute-start | bytes 18440 | tf_op jit(solution)/shard_map/ppermute | solution.py:35
  38.5 4.1 %collective-permute-start.3 = (f32[5,768]{1,0:T(8,128)}, f32[5,768]{1,0:T(8,128)}, u32[]{:S(2)}, u32[]{:S(2)}) collective-permute-start(f32[5,768]{1,0:T(8,128)} %stack.54), channel_id=1, source_target_pairs={{0,2},{2,0},{1,3},{3,1},{4,6},{6,4},{5,7},{7,5},{8,10},{10,8},{9,1... | collective-permute-start | bytes 46088 | tf_op jit(solution)/shard_map/ppermute | solution.py:259
  43.5 7.8 %collective-permute-start.5 = (bf16[64,1536]{1,0:T(8,128)(2,1)S(1)}, bf16[64,1536]{1,0:T(8,128)(2,1)S(1)}, u32[]{:S(2)}, u32[]{:S(2)}) collective-permute-start(bf16[64,1536]{1,0:T(8,128)(2,1)S(1)} %pad_maximum_fusion.1), channel_id=1, source_target_pairs={{0,4},{4,8},{8,12},{1,5},{5,9},{9,13},{2,6},{6,10},{10,14},{3,7},{... | collective-permute-start | bytes 589832 | tf_op jit(solution)/shard_map/ppermute | solution.py:274
  46.4 28.3 %collective-permute-start.10 = (bf16[192,1536]{1,0:T(8,128)(2,1)}, bf16[192,1536]{1,0:T(8,128)(2,1)S(1)}, u32[]{:S(2)}, u32[]{:S(2)}) collective-permute-start(bf16[192,1536]{1,0:T(8,128)(2,1)} %collective-permute-done.9.rest_3_), channel_id=1, source_target_pairs={{0,1},{1,0},{2,3},{3,2},{4,5},{5,4},{6,7},{7,6},{8,9},{9,8},{10,11... | collective-permute-start | bytes 1769480 | tf_op jit(solution)/shard_map/ppermute | solution.py:280
  46.5 9.2 %collective-permute-start.6 = (bf16[64,1536]{1,0:T(8,128)(2,1)S(1)}, bf16[64,1536]{1,0:T(8,128)(2,1)S(1)}, u32[]{:S(2)}, u32[]{:S(2)}) collective-permute-start(bf16[64,1536]{1,0:T(8,128)(2,1)S(1)} %pad_maximum_fusion.2), channel_id=1, source_target_pairs={{4,0},{8,4},{12,8},{5,1},{9,5},{13,9},{6,2},{10,6},{14,10},{7,3},{... | collective-permute-start | bytes 589832 | tf_op jit(solution)/shard_map/ppermute | solution.py:275
  65.8 8.9 %collective-permute-start.12 = (bf16[320,384]{1,0:T(8,128)(2,1)S(1)}, bf16[320,384]{1,0:T(8,128)(2,1)S(1)}, u32[]{:S(2)}, u32[]{:S(2)}) collective-permute-start(bf16[320,384]{1,0:T(8,128)(2,1)S(1)} %conv0.3.rest_0_), channel_id=1, source_target_pairs={{0,2},{2,0},{1,3},{3,1},{4,6},{6,4},{5,7},{7,5},{8,10},{10,8},{9,1... | collective-permute-start | bytes 737288 | tf_op jit(solution)/shard_map/ppermute | solution.py:259
  74.0 7.4 %collective-permute-start.8 = (bf16[320,384]{1,0:T(8,128)(2,1)S(1)}, bf16[320,384]{1,0:T(8,128)(2,1)S(1)}, u32[]{:S(2)}, u32[]{:S(2)}) collective-permute-start(bf16[320,384]{1,0:T(8,128)(2,1)S(1)} %conv0.2.rest_0_), channel_id=1, source_target_pairs={{0,2},{2,0},{1,3},{3,1},{4,6},{6,4},{5,7},{7,5},{8,10},{10,8},{9,1... | collective-permute-start | bytes 737288 | tf_op jit(solution)/shard_map/ppermute | solution.py:259
  85.8 26.4 %copy-start.5 = (bf16[320,1536]{1,0:T(8,128)(2,1)S(1)}, bf16[320,1536]{1,0:T(8,128)(2,1)}, u32[]{:S(2)}) copy-start(bf16[320,1536]{1,0:T(8,128)(2,1)} %copy-done.4) | copy-start | bytes 2949124
  85.8 1.2 collective-permute-start.13
  85.9 26.3 %copy-start.7 = (bf16[320,1536]{1,0:T(8,128)(2,1)S(1)}, bf16[320,1536]{1,0:T(8,128)(2,1)}, u32[]{:S(2)}) copy-start(bf16[320,1536]{1,0:T(8,128)(2,1)} %copy-done.6) | copy-start | bytes 2949124
  87.1 3.8 %collective-permute-start.14 = (f32[2,1536]{1,0:T(2,128)S(1)}, f32[2,1536]{1,0:T(2,128)S(1)}, u32[]{:S(2)}, u32[]{:S(2)}) collective-permute-start(f32[2,1536]{1,0:T(2,128)S(1)} %pad_maximum_fusion.4), channel_id=1, source_target_pairs={{0,4},{4,0},{8,12},{12,8},{1,5},{5,1},{9,13},{13,9},{2,6},{6,2},{1... | collective-permute-start | bytes 36872 | tf_op jit(solution)/shard_map/ppermute | solution.py:35
  88.3 9.2 %collective-permute-start.19 = (bf16[192,768]{1,0:T(8,128)(2,1)S(1)}, bf16[192,768]{1,0:T(8,128)(2,1)S(1)}, u32[]{:S(2)}, u32[]{:S(2)}) collective-permute-start(bf16[192,768]{1,0:T(8,128)(2,1)S(1)} %dynamic-slice_bitcast_fusion.1), channel_id=1, source_target_pairs={{0,2},{2,0},{1,3},{3,1},{4,6},{6,4},{5,7},{7,5},{8,10},{10,8},{9,1... | collective-permute-start | bytes 884744 | tf_op jit(solution)/shard_map/ppermute | solution.py:285
  90.9 14.6 %collective-permute-start.15 = (f32[2,1536]{1,0:T(2,128)S(1)}, f32[2,1536]{1,0:T(2,128)S(1)}, u32[]{:S(2)}, u32[]{:S(2)}) collective-permute-start(f32[2,1536]{1,0:T(2,128)S(1)} %pad_maximum_fusion.5), channel_id=1, source_target_pairs={{0,8},{4,12},{8,0},{12,4},{1,9},{5,13},{9,1},{13,5},{2,10},{6,14},... | collective-permute-start | bytes 36872 | tf_op jit(solution)/shard_map/ppermute | solution.py:35
  97.5 32.2 %collective-permute-start.20 = (bf16[192,768]{1,0:T(8,128)(2,1)S(1)}, bf16[192,768]{1,0:T(8,128)(2,1)S(1)}, u32[]{:S(2)}, u32[]{:S(2)}) collective-permute-start(bf16[192,768]{1,0:T(8,128)(2,1)S(1)} %collective-permute-done.19.rest_3_), channel_id=1, source_target_pairs={{0,1},{1,0},{2,3},{3,2},{4,5},{5,4},{6,7},{7,6},{8,9},{9,8},{10,11... | collective-permute-start | bytes 884744 | tf_op jit(solution)/shard_map/ppermute | solution.py:286
  98.5 9.2 %collective-permute-start.16 = (bf16[64,1536]{1,0:T(8,128)(2,1)S(1)}, bf16[64,1536]{1,0:T(8,128)(2,1)S(1)}, u32[]{:S(2)}, u32[]{:S(2)}) collective-permute-start(bf16[64,1536]{1,0:T(8,128)(2,1)S(1)} %slice.269), channel_id=1, source_target_pairs={{0,4},{4,8},{8,12},{1,5},{5,9},{9,13},{2,6},{6,10},{10,14},{3,7},{... | collective-permute-start | bytes 589832 | tf_op jit(solution)/shard_map/ppermute | solution.py:324
  102.9 8.9 %collective-permute-start.17 = (bf16[64,1536]{1,0:T(8,128)(2,1)S(1)}, bf16[64,1536]{1,0:T(8,128)(2,1)S(1)}, u32[]{:S(2)}, u32[]{:S(2)}) collective-permute-start(bf16[64,1536]{1,0:T(8,128)(2,1)S(1)} %slice.270), channel_id=1, source_target_pairs={{4,0},{8,4},{12,8},{5,1},{9,5},{13,9},{6,2},{10,6},{14,10},{7,3},{... | collective-permute-start | bytes 589832 | tf_op jit(solution)/shard_map/ppermute | solution.py:323
  121.3 8.3 %collective-permute-start.21 = (bf16[320,384]{1,0:T(8,128)(2,1)S(1)}, bf16[320,384]{1,0:T(8,128)(2,1)S(1)}, u32[]{:S(2)}, u32[]{:S(2)}) collective-permute-start(bf16[320,384]{1,0:T(8,128)(2,1)S(1)} %conv1.3.rest_0_), channel_id=1, source_target_pairs={{0,2},{2,0},{1,3},{3,1},{4,6},{6,4},{5,7},{7,5},{8,10},{10,8},{9,1... | collective-permute-start | bytes 737288 | tf_op jit(solution)/shard_map/ppermute | solution.py:259
  128.1 7.0 %collective-permute-start.18 = (bf16[320,384]{1,0:T(8,128)(2,1)S(1)}, bf16[320,384]{1,0:T(8,128)(2,1)S(1)}, u32[]{:S(2)}, u32[]{:S(2)}) collective-permute-start(bf16[320,384]{1,0:T(8,128)(2,1)S(1)} %conv1.2.rest_0_), channel_id=1, source_target_pairs={{0,2},{2,0},{1,3},{3,1},{4,6},{6,4},{5,7},{7,5},{8,10},{10,8},{9,1... | collective-permute-start | bytes 737288 | tf_op jit(solution)/shard_map/ppermute | solution.py:259
  (9 other events, 61.1 us)

commit v2 on v0

v2 whole, which is shorter than its diff:
```python
import functools

import jax
import jax.numpy as jnp
from jax import lax
from jax.experimental import pallas as pl
from jax.experimental.pallas import tpu as pltpu
from jax.sharding import PartitionSpec as P

HALO = 64
EPS = 1e-05
F32 = jnp.float32
BF16 = jnp.bfloat16
SWAP = [(0, 1), (1, 0)]
VMEM_LIMIT = 24 << 20

ANY = pl.BlockSpec(memory_space=pl.ANY)
HBM = pl.BlockSpec(memory_space=pltpu.HBM)
INV = pl.BlockSpec(memory_space=pltpu.VMEM)
INS = pl.BlockSpec(memory_space=pltpu.SMEM)
PARAMS = pltpu.CompilerParams(vmem_limit_bytes=VMEM_LIMIT)
dot = functools.partial(jnp.dot, preferred_element_type=F32)
copy = pltpu.make_async_copy


def shape(dims, dtype):
    return jax.ShapeDtypeStruct(tuple(dims), dtype)


def gelu(x):
    return jax.nn.gelu(x)


def side_of(back, n):
    return lax.rem(lax.axis_index("chan") - back + n, n)


def columns(back, n, width):
    return pl.ds(pl.multiple_of(side_of(back, n) * width, 128), width)


def run(copies):
    for c in copies:
        c.start()
    for c in copies:
        c.wait()


def sums_about(v, pivot):
    gap = (v - pivot).reshape(v.shape[0] // 8, 8, v.shape[1])
    return jnp.sum(gap, axis=0), jnp.sum(gap * gap, axis=0)


def spread_of(pivot, s1, s2, rows):
    s1 = jnp.sum(s1, axis=0, keepdims=True)
    s2 = jnp.sum(s2, axis=0, keepdims=True)
    off = s1 * (1.0 / rows)
    return pivot + off, s2 - s1 * off


def merged(a, b, n):
    gap = a[0:1] - b[0:1]
    return (a[0:1] + b[0:1]) * 0.5, a[1:2] + b[1:2] + gap * gap * (0.5 * n)


def pre_kernel(cut, own, w, gains, biases, sums, edges, rest_a, rest_b, wsend, xbuf, sems):
    rows = own.shape[0]
    end = rows - HALO
    part = wsend.shape[0]
    quarter = lax.axis_index("groups") * 2 + lax.axis_index("dp")
    load = copy(own, xbuf, sems.at[0])
    load.start()
    moves = [
        copy(own.at[pl.ds(0, HALO)], edges.at[pl.ds(0, HALO)], sems.at[1]),
        copy(own.at[pl.ds(end, HALO)], edges.at[pl.ds(HALO, HALO)], sems.at[2]),
        copy(own.at[pl.ds(HALO, cut - HALO)], rest_a, sems.at[3]),
        copy(own.at[pl.ds(cut, end - cut)], rest_b, sems.at[4]),
        copy(w.at[0, pl.ds(pl.multiple_of(quarter * part, 16), part)], wsend, sems.at[5]),
    ]
    for m in moves:
        m.start()
    load.wait()
    pivot = jnp.mean(xbuf[0:16, :].astype(F32)[0:8], axis=0, keepdims=True)
    s1 = s2 = jnp.zeros((8, xbuf.shape[1]), F32)
    for r in range(0, rows, 64):
        t1, t2 = sums_about(xbuf[r : r + 64, :].astype(F32), pivot)
        s1, s2 = s1 + t1, s2 + t2
    mean, m2 = spread_of(pivot, s1, s2, rows)
    sums[0:1, :] = mean
    sums[1:2, :] = m2
    for layer in range(2):
        sums[2 + 2 * layer : 3 + 2 * layer, :] = gains[layer : layer + 1, :]
        sums[3 + 2 * layer : 4 + 2 * layer, :] = biases[layer : layer + 1, :]
    for m in moves:
        m.wait()


def pre(own, w_proj, gains, biases, cut):
    rows, width = own.shape
    part = w_proj.shape[1] // 4
    return pl.pallas_call(
        functools.partial(pre_kernel, cut),
        out_shape=(
            shape((8, width), F32),
            shape((2 * HALO, width), BF16),
            shape((cut - HALO, width), BF16),
            shape((rows - HALO - cut, width), BF16),
            shape((part, w_proj.shape[2]), BF16),
        ),
        in_specs=[HBM, HBM, INV, INV],
        out_specs=(INV, ANY, ANY, ANY, ANY),
        scratch_shapes=[pltpu.VMEM((rows, width), BF16), pltpu.SemaphoreType.DMA((6,))],
        compiler_params=PARAMS,
        name="pre",
    )(own, w_proj, gains, biases)


def join_kernel(n, *refs):
    parts, (stat, joined) = refs[:n], refs[n:]
    for k, part in enumerate(parts):
        cols = columns(k, n, part.shape[1])
        stat[:, cols] = part[0:2, :]
        joined[:, cols] = part[...]


def join(parts):
    n, width = len(parts), parts[0].shape[1]
    return pl.pallas_call(
        functools.partial(join_kernel, n),
        out_shape=(shape((2, n * width), F32), shape((8, n * width), F32)),
        in_specs=[INV] * n,
        out_specs=(INV, INV),
        compiler_params=PARAMS,
        name="join",
    )(*parts)


def merge_kernel(n, a, b, out):
    out[0:1, :], out[1:2, :] = merged(a[...], b[...], n)


def finish_kernel(n, layer, a, b, joined, out):
    mean, m2 = merged(a[...], b[...], n)
    out[0:1, :] = mean
    scale = lax.rsqrt(m2 * (1.0 / (2 * n)) + EPS)
    out[1:2, :] = scale * joined[2 + 2 * layer : 3 + 2 * layer, :]
    out[2:3, :] = joined[3 + 2 * layer : 4 + 2 * layer, :]


def batch_stats(stat, n, joined, layer):
    steps = []
    for axis in ("dp", "seq"):
        size, step = lax.axis_size(axis), 1
        while step < size:
            steps.append((axis, [(i, i ^ step) for i in range(size)]))
            step *= 2
    channels = stat.shape[1]
    for at, (axis, pairs) in enumerate(steps):
        other = lax.ppermute(stat, axis, pairs)
        if at < len(steps) - 1:
            stat = pl.pallas_call(
                functools.partial(merge_kernel, n),
                out_shape=shape((2, channels), F32),
                in_specs=[INV, INV],
                out_specs=INV,
                name="merge",
            )(stat, other)
        else:
            stat = pl.pallas_call(
                functools.partial(finish_kernel, n, layer),
                out_shape=shape((8, channels), F32),
                in_specs=[INV, INV, INV],
                out_specs=INV,
                name="finish",
            )(stat, other, joined)
        n *= 2
    return stat


def edge_kernel(n, own, *rest):
    edges, (low, high, sems) = rest[: n - 1], rest[n - 1 :]
    end = own.shape[0] - HALO
    width = own.shape[1]
    copies = []
    for k in range(n):
        cols = columns(k, n, width)
        first = own.at[pl.ds(0, HALO)] if k == 0 else edges[k - 1].at[pl.ds(0, HALO)]
        last = own.at[pl.ds(end, HALO)] if k == 0 else edges[k - 1].at[pl.ds(HALO, HALO)]
        copies.append(copy(last, low.at[:, cols], sems.at[2 * k]))
        copies.append(copy(first, high.at[:, cols], sems.at[2 * k + 1]))
    run(copies)


def edge_rows(own, edges):
    n = 1 + len(edges)
    return pl.pallas_call(
        functools.partial(edge_kernel, n),
        out_shape=(shape((HALO, n * own.shape[1]), BF16),) * 2,
        in_specs=[HBM] + [ANY] * (n - 1),
        out_specs=(ANY, ANY),
        scratch_shapes=[pltpu.SemaphoreType.DMA((2 * n,))],
        name="edge_rows",
    )(own, *edges)


def keep_kernel(lengths, dilations, out):
    rows = out.shape[1]
    first = lax.axis_index("seq") * rows
    count = lengths.shape[1]

    @pl.loop(0, rows // 64)
    def _(i):
        at = pl.multiple_of(i * 64, 64)
        place = first + at + lax.broadcasted_iota(jnp.int32, (64, 128), 0)

        def step(k, carry):
            start, keep = carry[0], list(carry[1:])
            end = start + lengths[0, k]
            for layer in range(2):
                d = dilations[layer]
                cut_l = (place - d < start) & (start <= place)
                cut_r = (place < end) & (end <= place + d)
                keep[2 * layer] = jnp.where(cut_l, 0.0, keep[2 * layer])
                keep[2 * layer + 1] = jnp.where(cut_r, 0.0, keep[2 * layer + 1])
            return (end, *keep)

        ones = jnp.ones((64, 128), F32)
        done = lax.fori_loop(0, count, step, (jnp.int32(0), ones, ones, ones, ones))
        for k in range(4):
            out[k, pl.ds(at, 64), :] = done[1 + k]


def keeps(lengths, dilations, rows):
    return pl.pallas_call(
        keep_kernel,
        out_shape=shape((4, rows, 128), F32),
        in_specs=[INS, INS],
        out_specs=INV,
        name="keeps",
    )(lengths, dilations)


def shifted(ref, start, count):
    base = pl.multiple_of((start // 8) * 8, 8)
    tall = ref[pl.ds(base, count + 8), :]
    return pltpu.roll(tall, (count + 8 - (start - base)) % (count + 8), 0)[:count]


def piece(src, at, count, to, back, n, buf, sem):
    if back is None:
        dst = buf.at[pl.ds(to, count), :]
    else:
        dst = buf.at[pl.ds(to, count), columns(back, n, src.shape[1])]
    return copy(src.at[pl.ds(at, count), :], dst, sem)


def conv_kernel(pieces, layer, rows, first, n, n_src, dilations, stats, keep, w_hbm, *rest):
    srcs, (out, xbuf, nbuf, wbuf, p0, p2, sems, wsems) = rest[:n_src], rest[n_src:]
    moves = [piece(srcs[p[0]], *p[1:], n, xbuf, sems.at[k]) for k, p in enumerate(pieces)]
    for m in moves:
        m.start()
    weights = [copy(w_hbm.at[layer, tap], wbuf.at[tap], wsems.at[tap]) for tap in range(3)]
    for w in weights:
        w.start()
    for m in moves:
        m.wait()
    ext = rows + 2 * HALO
    block = 16
    mean, scale, bias = stats[0:1, :], stats[1:2, :], stats[2:3, :]

    @pl.loop(0, ext // block)
    def _(i):
        at = pl.ds(pl.multiple_of(i * block, block), block)
        v = xbuf[at, :].astype(F32)
        nbuf[at, :] = gelu((v - mean) * scale + bias).astype(BF16)

    weights[0].wait()
    p0[0 : rows + HALO, :] = dot(nbuf[0 : rows + HALO, :], wbuf[0])
    weights[2].wait()
    p2[0 : rows + HALO, :] = dot(nbuf[HALO:ext, :], wbuf[2])
    weights[1].wait()
    mid = dot(nbuf[HALO : HALO + rows, :], wbuf[1])
    d = dilations[layer]
    width = out.shape[1]
    for r in range(0, rows, HALO):
        left = shifted(p0, r + HALO - d, HALO)
        right = shifted(p2, r + d, HALO)
        here = slice(first + r, first + r + HALO)
        for c in range(0, width, 128):
            wide = min(128, width - c)
            cs = slice(c, c + wide)
            kl, kr = keep[2 * layer, here, :wide] > 0, keep[2 * layer + 1, here, :wide] > 0
            mixed = jnp.where(kl, left[:, cs], 0.0) + jnp.where(kr, right[:, cs], 0.0)
            out[r : r + HALO, cs] = gelu(mid[r : r + HALO, cs] + mixed).astype(BF16)


def conv(pieces, srcs, n, layer, rows, first, dilations, stats, keep, w_conv):
    channels, width = w_conv.shape[2:]
    ext = rows + 2 * HALO
    return pl.pallas_call(
        functools.partial(conv_kernel, pieces, layer, rows, first, n, len(srcs)),
        out_shape=shape((rows, width), BF16),
        in_specs=[INS, INV, INV, HBM] + [ANY] * len(srcs),
        out_specs=INV,
        scratch_shapes=[
            pltpu.VMEM((ext, channels), BF16),
            pltpu.VMEM((ext, channels), BF16),
            pltpu.VMEM((3, channels, width), BF16),
            pltpu.VMEM((rows + HALO + 8, width), F32),
            pltpu.VMEM((rows + HALO + 8, width), F32),
            pltpu.SemaphoreType.DMA((len(pieces),)),
            pltpu.SemaphoreType.DMA((3,)),
        ],
        compiler_params=PARAMS,
        name=f"conv{layer}_{first}",
    )(dilations, stats, keep, w_conv, *srcs)


def weight_copies(layer, cols, w_hbm, sends, wbuf, sems):
    copies = [copy(w_hbm.at[layer, :, cols], wbuf.at[0], sems.at[0])]
    for k, parts in enumerate(sends):
        size = parts[0][0].shape[0]
        for src, at in parts:
            dst = wbuf.at[k + 1, pl.ds(pl.multiple_of(at * size, 16), size), :]
            copies.append(copy(src, dst, sems.at[len(copies)]))
    return copies


def quarters(refs):
    group, core = lax.axis_index("groups"), lax.axis_index("dp")
    ats = (2 * group + core, 2 * (1 - group) + core, 2 * group + 1 - core, 3 - 2 * group - core)
    return [list(zip(refs[i : i + 4], ats)) for i in range(0, len(refs), 4)]


def halves(refs):
    core = lax.axis_index("dp")
    return [list(zip(refs[i : i + 2], (core, 1 - core))) for i in range(0, len(refs), 2)]


def update_of(inners, wbuf, cols):
    total = None
    for k, inner in enumerate(inners):
        term = dot(inner[...], wbuf[k, :, cols]).astype(BF16).astype(F32)
        total = term if total is None else total + term
    return total


def proj0_kernel(pieces, rows, n, n_src, last, *rest):
    inners, w_hbm, sends, rest = rest[:n], rest[n], rest[n + 1 : 5 * n - 3], rest[5 * n - 3 :]
    srcs, rest = rest[:n_src], rest[n_src:]
    if last:
        before, out, stat, edge, xbuf, wbuf, sems, wsems = rest
        wsend = ()
    else:
        out, stat, edge, *wsend, xbuf, wbuf, sems, wsems, ssems = rest
    copies = weight_copies(0, slice(None), w_hbm, quarters(sends), wbuf, wsems)
    copies += [piece(srcs[p[0]], *p[1:], n, xbuf, sems.at[k]) for k, p in enumerate(pieces)]
    moves = []
    for k, dst in enumerate(wsend):
        size, width = dst.shape
        ahead = lax.rem(lax.axis_index("chan") + k + 1, n) * width
        part = pl.ds(pl.multiple_of(lax.axis_index("dp") * size, 16), size)
        src = w_hbm.at[1, part, pl.ds(pl.multiple_of(ahead, 128), width)]
        moves.append(copy(src, dst, ssems.at[k]))
    for c in copies + moves:
        c.start()
    for c in copies:
        c.wait()
    for col in range(0, out.shape[1], 256):
        cs = slice(col, col + 256)
        new = (xbuf[:, cs].astype(F32) + update_of(inners, wbuf, cs)).astype(BF16)
        out[:, cs] = new
        edge[:, cs] = new[rows - HALO :] if last else new[:HALO]
        v = new.astype(F32)
        pivot = jnp.mean(v[0:8], axis=0, keepdims=True)
        mean, m2 = spread_of(pivot, *sums_about(v, pivot), rows)
        if last:
            mean, m2 = merged(before[:, cs], jnp.concatenate([mean, m2]), rows)
        stat[0:1, cs] = mean
        stat[1:2, cs] = m2
    for m in moves:
        m.wait()


def proj0(pieces, srcs, rows, inners, w_proj, sends, before=None):
    hidden, channels = w_proj.shape[1:]
    n = len(inners)
    last = before is not None
    n_send = 0 if last else n - 1
    outs = [shape((rows, channels), BF16), shape((2, channels), F32), shape((HALO, channels), BF16)]
    outs += [shape((hidden // 2, channels // n), BF16)] * n_send
    scratch = [
        pltpu.VMEM((rows, channels), BF16),
        pltpu.VMEM((n, hidden, channels), BF16),
        pltpu.SemaphoreType.DMA((len(pieces),)),
        pltpu.SemaphoreType.DMA((4 * n - 3,)),
    ]
    if n_send:
        scratch.append(pltpu.SemaphoreType.DMA((n_send,)))
    extra = [before] if last else []
    return pl.pallas_call(
        functools.partial(proj0_kernel, pieces, rows, n, len(srcs), last),
        out_shape=outs,
        in_specs=[INV] * n + [HBM] + [ANY] * (len(sends) + len(srcs)) + [INV] * len(extra),
        out_specs=[INV] * 3 + [ANY] * n_send,
        scratch_shapes=scratch,
        compiler_params=PARAMS,
        name=f"proj0_{int(last)}",
    )(*inners, w_proj, *sends, *srcs, *extra)


def proj1_kernel(first, n, last, *rest):
    inners, w_hbm, sends, state = rest[:n], rest[n], rest[n + 1 : 3 * n - 1], rest[3 * n - 1]
    out, xbuf, obuf, wbuf, sems, wsems = rest[3 * n + int(last) :]
    rows, width = xbuf.shape
    cols = columns(0, n, width)
    copies = weight_copies(1, cols, w_hbm, halves(sends), wbuf, wsems)
    copies.append(copy(state.at[:, cols], xbuf, sems.at[0]))
    run(copies)
    for col in range(0, width, 128):
        cs = slice(col, col + 128)
        obuf[:, cs] = (xbuf[:, cs].astype(F32) + update_of(inners, wbuf, cs)).astype(BF16)
    run([copy(obuf, out.at[pl.ds(first, rows)], sems.at[1])])


def proj1(first, total, inners, w_proj, sends, state, before=None):
    hidden, channels = w_proj.shape[1:]
    n = len(inners)
    width = channels // n
    rows = state.shape[0]
    last = before is not None
    extra = [before] if last else []
    return pl.pallas_call(
        functools.partial(proj1_kernel, first, n, last),
        out_shape=shape((total, width), BF16),
        in_specs=[INV] * n + [HBM] + [ANY] * (len(sends) + 1) + [HBM] * len(extra),
        out_specs=HBM,
        scratch_shapes=[
            pltpu.VMEM((rows, width), BF16),
            pltpu.VMEM((rows, width), BF16),
            pltpu.VMEM((n, hidden, width), BF16),
            pltpu.SemaphoreType.DMA((2,)),
            pltpu.SemaphoreType.DMA((2 * n - 1,)),
        ],
        input_output_aliases={n + 1 + len(sends) + 1: 0} if last else {},
        compiler_params=PARAMS,
        name=f"proj1_{first}",
    )(*inners, w_proj, *sends, state, *extra)


def on_device(signal, lengths, dilations, w_conv, w_proj, gains, biases):
    own = signal[0]
    rows = own.shape[0]
    half = rows // 2
    cut, end = half + HALO, rows - HALO
    n_seq, n = lax.axis_size("seq"), lax.axis_size("chan")
    up = [(i, i + 1) for i in range(n_seq - 1)]
    down = [(i + 1, i) for i in range(n_seq - 1)]
    perm = lax.ppermute

    def ahead(value, k):
        return perm(value, "chan", [(i, (i + k) % n) for i in range(n)])

    def others(value):
        return [ahead(value, k) for k in range(1, n)]

    sums, edge, part_a, part_b, wsend = pre(own, w_proj, gains, biases, cut)
    stat, joined = join([sums] + others(sums))
    edges = others(edge)
    rest_a, rest_b = others(part_a), others(part_b)
    low, high = edge_rows(own, edges)
    low0, high0 = perm(low, "seq", up), perm(high, "seq", down)
    keep = keeps(lengths, dilations, rows)
    stats0 = batch_stats(stat, rows, joined, 0)

    sends0 = []
    for w in others(wsend):
        w2 = perm(w, "groups", SWAP)
        sends0 += [w, w2, perm(w, "dp", SWAP), perm(w2, "dp", SWAP)]

    srcs = (own, low0, high0, *edges, *rest_a, *rest_b)
    behind = [(k, 2 + k, 1 + n + k, 2 * n + k) for k in range(1, n)]
    pieces_a = [(1, 0, HALO, 0, None), (0, 0, cut, HALO, 0)]
    pieces_b = [(0, half - HALO, half + HALO, 0, 0), (2, 0, HALO, half + HALO, None)]
    res_a, res_b = [(0, 0, half, 0, 0)], [(0, half, half, 0, 0)]
    for k, e, a, b in behind:
        pieces_a += [(e, 0, HALO, HALO, k), (a, 0, cut - HALO, 2 * HALO, k)]
        pieces_b += [
            (a, half - 2 * HALO, 2 * HALO, 0, k),
            (b, 0, end - cut, 2 * HALO, k),
            (e, HALO, HALO, 2 * HALO + end - cut, k),
        ]
        res_a += [(e, 0, HALO, 0, k), (a, 0, half - HALO, HALO, k)]
        res_b += [
            (a, half - HALO, HALO, 0, k),
            (b, 0, end - cut, HALO, k),
            (e, HALO, HALO, HALO + end - cut, k),
        ]
    early = srcs[: 1 + 2 * n]
    inner_a = conv(pieces_a, early, n, 0, half, 0, dilations, stats0, keep, w_conv)
    inner_b = conv(pieces_b, srcs, n, 0, half, half, dilations, stats0, keep, w_conv)
    inners_a = [inner_a] + others(inner_a)
    inners_b = [inner_b] + others(inner_b)
    state_a, stat_a, edge_a, *wsend1 = proj0(res_a, early, half, inners_a, w_proj, sends0)
    state_b, stat, edge_b = proj0(res_b, srcs, half, inners_b, w_proj, sends0, stat_a)
    high1, low1 = perm(edge_a, "seq", down), perm(edge_b, "seq", up)
    stats1 = batch_stats(stat, rows, joined, 1)
    sends1 = []
    for k, w in enumerate(wsend1):
        w = ahead(w, k + 1)
        sends1 += [w, perm(w, "dp", SWAP)]

    srcs = (state_a, state_b, low1, high1)
    pieces_a = ((2, 0, HALO, 0, None), (0, 0, half, HALO, None), (1, 0, HALO, half + HALO, None))
    pieces_b = (
        (0, half - HALO, HALO, 0, None),
        (1, 0, half, HALO, None),
        (3, 0, HALO, half + HALO, None),
    )
    inner_a = conv(pieces_a, srcs, n, 1, half, 0, dilations, stats1, keep, w_conv)
    inner_b = conv(pieces_b, srcs, n, 1, half, half, dilations, stats1, keep, w_conv)
    inners_a = [inner_a] + others(inner_a)
    inners_b = [inner_b] + others(inner_b)
    out = proj1(0, rows, inners_a, w_proj, sends1, state_a)
    return proj1(half, rows, inners_b, w_proj, sends1, state_b, out)[None]


def solution(mesh):
    placed = (
        P(("groups", "dp"), "seq", "chan"),
        P(("groups", "dp"), None),
        P(),
        P(None, None, None, "chan"),
        P(None, "chan", None),
        P(None, "chan"),
        P(None, "chan"),
    )
    return jax.shard_map(
        on_device,
        mesh=mesh,
        in_specs=placed,
        out_specs=P(("groups", "dp"), "seq", "chan"),
        check_vma=False,
    )
```

time: 258 us -> 163 us (0.63)
  waiting for transfers between devices: 130 us -> 36.4 us
  Pallas kernels: 0 us -> 65.3 us
  blocking collectives: 53 us -> 0 us
  local copies, waits for them, and re-layouts: 0.71 us -> 26.9 us
  matrix products: 25.6 us -> 0 us
  between operations: 18.3 us -> 0.44 us
  starting transfers between devices: 14.8 us -> 31.6 us
  other arithmetic: 12.8 us -> 0 us
    pallas_call x0 -> x18, Pallas kernels: none -> 65.3 us  [the longest x4 25 us: conv(): pl.pallas_call(functools.partial(conv_kernel, pieces, layer, rows, first,...]
    all_gather x2 -> x0, waiting for transfers between devices: 64.7 us -> none  [conv_layer(): piece = lax.all_gather(normed, 'chan', axis=2, tiled=True)]
    reduce_scatter x2 -> x0, waiting for transfers between devices: 61 us -> none  [conv_layer(): lax.psum_scatter(terms.astype(jnp.bfloat16), 'chan', scatter_dimension=2,...]
    psum x4 -> x0, blocking collectives: 53 us -> none  [batch_total(): return lax.psum(value, ('seq', 'dp'))]
    ppermute x4 -> x24, waiting for transfers between devices: 4.48 us -> 36.4 us  [the longest x10 22.4 us: ahead(): return perm(value, 'chan', [(i, (i + k) % n) for i in range(n)])]
    unnamed x16 -> x66, local copies, waits for them, and re-layouts: 0.03 us -> 26.9 us
    dot_general x6 -> x0, matrix products: 25.6 us -> none  [the longest x2 12.2 us: conv_layer(): jnp.einsum('smf,fc->smc', inner, proj_weight, preferred_element_type=jnp....]
    ppermute x4 -> x24, starting transfers between devices: 14.5 us -> 31.6 us  [the longest x10 11.4 us: ahead(): return perm(value, 'chan', [(i, (i + k) % n) for i in range(n)])]
  transfers between devices with their start and end apart: 8 -> 24, of which waited for: 8 -> 10; matrix products, arithmetic and copies ran while one was open for 1% -> 0% of each run, Pallas kernels for 0% -> 38%
where the time goes in v2:
time: 163 us; the launch traced here: 161 us
  Pallas kernels  65.3 us (40%)
  waiting for transfers between devices  36.4 us (22%)
  starting transfers between devices  31.6 us (19%)
  local copies, waits for them, and re-layouts  26.9 us (17%)
    unnamed x66, local copies, waits for them, and re-layouts  26.9 us
    pallas_call x4, Pallas kernels, conv(): pl.pallas_call(functools.partial(conv_kernel, pieces, layer, rows, first,...  25 us
    ppermute x10, waiting for transfers between devices, ahead(): return perm(value, 'chan', [(i, (i + k) % n) for i in range(n)])  22.4 us
    ppermute x6, waiting for transfers between devices, batch_stats(): other = lax.ppermute(stat, axis, pairs)  14 us
    pallas_call x1, Pallas kernels, edge_rows(): pl.pallas_call(functools.partial(edge_kernel, n), out_shape=(shape((HALO,...  13 us
    ppermute x10, starting transfers between devices, ahead(): return perm(value, 'chan', [(i, (i + k) % n) for i in range(n)])  11.4 us
    pallas_call x2, Pallas kernels, proj0(): pl.pallas_call(functools.partial(proj0_kernel, pieces, rows, n, len(srcs)...  7.23 us
    ppermute x6, starting transfers between devices, batch_stats(): other = lax.ppermute(stat, axis, pairs)  6.26 us
  transfers between devices with their start and end apart: 24, of which 10 were waited for; matrix products, arithmetic and copies ran while one was open for 0% of the time, Pallas kernels for 38%

profile of v2, /device:TPU:8, one launch (start us, length us, event | category | flops | bytes accessed | tf_op | source)
XLA Modules:
  0.0 160.7 jit_solution(13998283807491277383)
XLA Ops:
  9.5 6.5 %collective-permute-done.10.rest_3_ = bf16[96,1536]{1,0:T(8,128)(2,1)} collective-permute-done((bf16[96,1536]{1,0:T(8,128)(2,1)S(1)}, bf16[96,1536]{1,0:T(8,128)(2,1)}, u32[]{:S(2)}, u32[]{:S(2)}) %collective-permute-start.10) | collective-permute-done | bytes 294944 | tf_op jit(solution)/shard_map/ppermute | solution.py:462
  17.5 12.0 %collective-permute-done.4.rest_0_.rest_3_.rest_10_ = bf16[128,768]{1,0:T(8,128)(2,1)S(1)} collective-permute-done((bf16[128,768]{1,0:T(8,128)(2,1)S(1)}, bf16[128,768]{1,0:T(8,128)(2,1)S(1)}, u32[]{:S(2)}, u32[]{:S(2)}) %collective-permute-start.4) | collective-permute-done | bytes 196640 | tf_op jit(solution)/shard_map/ppermute | solution.py:462
  30.2 13.0 %edge_rows.1 = (bf16[64,1536]{1,0:T(8,128)(2,1)}, bf16[64,1536]{1,0:T(8,128)(2,1)}) custom-call(bf16[640,768]{1,0:T(8,128)(2,1)} %bitcast.2, bf16[128,768]{1,0:T(8,128)(2,1)} %copy-done.14), custom_call_target="tpu_custom_call" | custom-call | tf_op jit(solution)/shard_map/edge_rows/pallas_call | solution.py:196
  43.2 3.5 %collective-permute-start.5 = (bf16[64,1536]{1,0:T(8,128)(2,1)}, bf16[64,1536]{1,0:T(8,128)(2,1)S(1)}, u32[]{:S(2)}, u32[]{:S(2)}) collective-permute-start(bf16[64,1536]{1,0:T(8,128)(2,1)} %get-tuple-element.25), channel_id=1, source_target_pairs={{0,4},{4,8},{8,12},{1,5},{5,9},{9,13},{2,6},{6,10},{10,14},{3,7},{... | collective-permute-start | bytes 589832 | tf_op jit(solution)/shard_map/ppermute | solution.py:472
  48.3 2.4 %collective-permute-start.6 = (bf16[64,1536]{1,0:T(8,128)(2,1)}, bf16[64,1536]{1,0:T(8,128)(2,1)S(1)}, u32[]{:S(2)}, u32[]{:S(2)}) collective-permute-start(bf16[64,1536]{1,0:T(8,128)(2,1)} %get-tuple-element.26), channel_id=1, source_target_pairs={{4,0},{8,4},{12,8},{5,1},{9,5},{13,9},{6,2},{10,6},{14,10},{7,3},{... | collective-permute-start | bytes 589832 | tf_op jit(solution)/shard_map/ppermute | solution.py:472
  54.3 3.5 %collective-permute-done.2.b = f32[2,1536]{1,0:T(2,128)S(1)} collective-permute-done((f32[2,1536]{1,0:T(2,128)}, f32[2,1536]{1,0:T(2,128)S(1)}, u32[]{:S(2)}, u32[]{:S(2)}) %collective-permute-start.2) | collective-permute-done | bytes 12320 | tf_op jit(solution)/shard_map/ppermute | solution.py:159
  59.7 2.6 %collective-permute-start.3 = (f32[2,1536]{1,0:T(2,128)}, f32[2,1536]{1,0:T(2,128)S(1)}, u32[]{:S(2)}, u32[]{:S(2)}) collective-permute-start(f32[2,1536]{1,0:T(2,128)} %merge.5.a), channel_id=1, source_target_pairs={{0,8},{4,12},{8,0},{12,4},{1,9},{5,13},{9,1},{13,5},{2,10},{6,14},... | collective-permute-start | bytes 36872 | tf_op jit(solution)/shard_map/ppermute | solution.py:159
  62.3 2.2 %collective-permute-done.3.b = f32[2,1536]{1,0:T(2,128)S(1)} collective-permute-done((f32[2,1536]{1,0:T(2,128)}, f32[2,1536]{1,0:T(2,128)S(1)}, u32[]{:S(2)}, u32[]{:S(2)}) %collective-permute-start.3) | collective-permute-done | bytes 12320 | tf_op jit(solution)/shard_map/ppermute | solution.py:159
  66.5 4.5 %keeps.1.keep = f32[4,640,128]{2,1,0:T(8,128)} custom-call(s32[1,8]{1,0:T(1,128)} %lengths.1, s32[2]{0:T(128)} %dilations.9), custom_call_target="tpu_custom_call" | custom-call | tf_op jit(solution)/shard_map/keeps/pallas_call | solution.py:234
  72.5 3.0 %copy-done = bf16[2,3,1536,384]{3,2,1,0:T(8,128)(2,1)S(1)} copy-done((bf16[2,3,1536,384]{3,2,1,0:T(8,128)(2,1)S(1)}, bf16[2,3,1536,384]{3,2,1,0:T(8,128)(2,1)}, u32[]{:S(2)}) %copy-start) | copy-done | bytes 7077912
  78.6 6.0 %conv0_0.1.rest_0_ = bf16[320,384]{1,0:T(8,128)(2,1)S(1)} custom-call(s32[2]{0:T(128)S(1)} %copy-done.22, f32[8,1536]{1,0:T(8,128)S(1)} %copy-done.19, f32[4,640,128]{2,1,0:T(8,128)S(1)} %copy-done.6, bf16[2,3,1536,384]{3,2,1,0:T(8,128)(2,1)S(1)} %copy-done, bf16[640,768]{1,0:T(8,128)(2,1)S(1)} %bitcast.4, ...), custom_call_target="tpu_custom_call" | custom-call | tf_op jit(solution)/shard_map/conv0_0/pallas_call | solution.py:300
  88.7 6.2 %conv0_320.1.rest_0_ = bf16[320,384]{1,0:T(8,128)(2,1)S(1)} custom-call(s32[2]{0:T(128)S(1)} %copy-done.22, f32[8,1536]{1,0:T(8,128)S(1)} %copy-done.20, f32[4,640,128]{2,1,0:T(8,128)S(1)} %copy-done.6, bf16[2,3,1536,384]{3,2,1,0:T(8,128)(2,1)S(1)} %copy-done, bf16[640,768]{1,0:T(8,128)(2,1)S(1)} %bitcast.5, ...), custom_call_target="tpu_custom_call" | custom-call | tf_op jit(solution)/shard_map/conv0_320/pallas_call | solution.py:300
  96.3 3.6 %proj0_0.1 = (bf16[320,1536]{1,0:T(8,128)(2,1)S(1)}, f32[2,1536]{1,0:T(2,128)S(1)}, bf16[64,1536]{1,0:T(8,128)(2,1)}, bf16[192,768]{1,0:T(8,128)(2,1)S(1)}) custom-call(bf16[320,384]{1,0:T(8,128)(2,1)S(1)} %conv0_0.1.rest_0_, bf16[320,384]{1,0:T(8,128)(2,1)S(1)} %collective-permute-done.14.rest_1_, bf16[2,384,1536]{2,1,0:T(8,128)(2,1)S(1)} %copy-done.3, ...), custom_call_target="tpu_custom_call" | custom-call | tf_op jit(solution)/shard_map/proj0_0/pallas_call | solution.py:401
  102.6 3.6 %proj0_1.1 = (bf16[320,1536]{1,0:T(8,128)(2,1)S(1)}, f32[2,1536]{1,0:T(2,128)S(1)}, bf16[64,1536]{1,0:T(8,128)(2,1)}) custom-call(bf16[320,384]{1,0:T(8,128)(2,1)S(1)} %conv0_320.1.rest_0_, bf16[320,384]{1,0:T(8,128)(2,1)S(1)} %collective-permute-done.9.rest_1_, bf16[2,384,1536]{2,1,0:T(8,128)(2,1)S(1)} %copy-done.3, ...), custom_call_target="tpu_custom_call" | custom-call | tf_op jit(solution)/shard_map/proj0_1/pallas_call | solution.py:401
  107.2 3.5 %collective-permute-start.18 = (bf16[64,1536]{1,0:T(8,128)(2,1)}, bf16[64,1536]{1,0:T(8,128)(2,1)S(1)}, u32[]{:S(2)}, u32[]{:S(2)}) collective-permute-start(bf16[64,1536]{1,0:T(8,128)(2,1)} %get-tuple-element.34), channel_id=1, source_target_pairs={{0,4},{4,8},{8,12},{1,5},{5,9},{9,13},{2,6},{6,10},{10,14},{3,7},{... | collective-permute-start | bytes 589832 | tf_op jit(solution)/shard_map/ppermute | solution.py:506
  110.7 2.6 %collective-permute-start.19 = (bf16[64,1536]{1,0:T(8,128)(2,1)}, bf16[64,1536]{1,0:T(8,128)(2,1)S(1)}, u32[]{:S(2)}, u32[]{:S(2)}) collective-permute-start(bf16[64,1536]{1,0:T(8,128)(2,1)} %get-tuple-element.35), channel_id=1, source_target_pairs={{4,0},{8,4},{12,8},{5,1},{9,5},{13,9},{6,2},{10,6},{14,10},{7,3},{... | collective-permute-start | bytes 589832 | tf_op jit(solution)/shard_map/ppermute | solution.py:506
  116.9 3.9 %collective-permute-done.16.b = f32[2,1536]{1,0:T(2,128)S(1)} collective-permute-done((f32[2,1536]{1,0:T(2,128)}, f32[2,1536]{1,0:T(2,128)S(1)}, u32[]{:S(2)}, u32[]{:S(2)}) %collective-permute-start.16) | collective-permute-done | bytes 12320 | tf_op jit(solution)/shard_map/ppermute | solution.py:159
  122.7 2.7 %collective-permute-start.17 = (f32[2,1536]{1,0:T(2,128)}, f32[2,1536]{1,0:T(2,128)S(1)}, u32[]{:S(2)}, u32[]{:S(2)}) collective-permute-start(f32[2,1536]{1,0:T(2,128)} %merge.7.a), channel_id=1, source_target_pairs={{0,8},{4,12},{8,0},{12,4},{1,9},{5,13},{9,1},{13,5},{2,10},{6,14},... | collective-permute-start | bytes 36872 | tf_op jit(solution)/shard_map/ppermute | solution.py:159
  129.6 3.0 %copy-done.1 = bf16[2,3,1536,384]{3,2,1,0:T(8,128)(2,1)S(1)} copy-done((bf16[2,3,1536,384]{3,2,1,0:T(8,128)(2,1)S(1)}, bf16[2,3,1536,384]{3,2,1,0:T(8,128)(2,1)}, u32[]{:S(2)}) %copy-start.1) | copy-done | bytes 7077912
  137.1 6.4 %conv1_0.1.rest_0_ = bf16[320,384]{1,0:T(8,128)(2,1)S(1)} custom-call(s32[2]{0:T(128)S(1)} %copy-done.22, f32[8,1536]{1,0:T(8,128)S(1)} %copy-done.18, f32[4,640,128]{2,1,0:T(8,128)S(1)} %copy-done.7, bf16[2,3,1536,384]{3,2,1,0:T(8,128)(2,1)S(1)} %copy-done.1, bf16[320,1536]{1,0:T(8,128)(2,1)S(1)} %copy-done.11, bf16[320,1536]{1,0:T(8,128)(2,1)S(1)} %copy-done.9, ...), custom_call_target="tpu_custom_call" | custom-call | tf_op jit(solution)/shard_map/conv1_0/pallas_call | solution.py:300
  145.1 6.4 %conv1_320.1.rest_0_ = bf16[320,384]{1,0:T(8,128)(2,1)S(1)} custom-call(s32[2]{0:T(128)S(1)} %copy-done.22, f32[8,1536]{1,0:T(8,128)S(1)} %copy-done.18, f32[4,640,128]{2,1,0:T(8,128)S(1)} %copy-done.7, bf16[2,3,1536,384]{3,2,1,0:T(8,128)(2,1)S(1)} %copy-done.1, bf16[320,1536]{1,0:T(8,128)(2,1)S(1)} %copy-done.11, bf16[320,1536]{1,0:T(8,128)(2,1)S(1)} %copy-done.9, ...), custom_call_target="tpu_custom_call" | custom-call | tf_op jit(solution)/shard_map/conv1_320/pallas_call | solution.py:300
  152.1 2.8 %proj1_0.1.rest_6_ = bf16[640,768]{1,0:T(8,128)(2,1)} custom-call(bf16[320,384]{1,0:T(8,128)(2,1)S(1)} %conv1_0.1.rest_0_, bf16[320,384]{1,0:T(8,128)(2,1)S(1)} %collective-permute-done.23.rest_1_, bf16[2,384,1536]{2,1,0:T(8,128)(2,1)S(1)} %copy-done.3, bf16[192,768]{1,0:T(8,128)(2,1)} %collective-permute-done.21.rest_3_, ...), custom_call_target="tpu_custom_call" | custom-call | tf_op jit(solution)/shard_map/proj1_0/pallas_call | solution.py:433
  154.9 2.8 %collective-permute-done.20.rest_1_ = bf16[320,384]{1,0:T(8,128)(2,1)S(1)} collective-permute-done((bf16[320,384]{1,0:T(8,128)(2,1)S(1)}, bf16[320,384]{1,0:T(8,128)(2,1)S(1)}, u32[]{:S(2)}, u32[]{:S(2)}) %collective-permute-start.20) | collective-permute-done | bytes 245792 | tf_op jit(solution)/shard_map/ppermute | solution.py:462
  157.8 2.8 %proj1_320.1 = bf16[640,768]{1,0:T(8,128)(2,1)} custom-call(bf16[320,384]{1,0:T(8,128)(2,1)S(1)} %conv1_320.1.rest_0_, bf16[320,384]{1,0:T(8,128)(2,1)S(1)} %collective-permute-done.20.rest_1_, bf16[2,384,1536]{2,1,0:T(8,128)(2,1)S(1)} %copy-done.3, bf16[192,768]{1,0:T(8,128)(2,1)} %collective-permute-done.21.rest_3_, ...), custom_call_target="tpu_custom_call", output_to_operand_aliasing={{}: (6, {})} | custom-call | tf_op jit(solution)/shard_map/proj1_320/pallas_call | solution.py:433
  (108 shorter events, 50.8 us)
Async XLA Ops:
  5.9 10.1 %collective-permute-start.10 = (bf16[96,1536]{1,0:T(8,128)(2,1)S(1)}, bf16[96,1536]{1,0:T(8,128)(2,1)}, u32[]{:S(2)}, u32[]{:S(2)}) collective-permute-start(bf16[96,1536]{1,0:T(8,128)(2,1)S(1)} %get-tuple-element.29), channel_id=1, source_target_pairs={{0,2},{2,0},{1,3},{3,1},{4,6},{6,4},{5,7},{7,5},{8,10},{10,8},{9,1... | collective-permute-start | bytes 884744 | tf_op jit(solution)/shard_map/ppermute | solution.py:462
  7.5 65.0 %collective-permute-start.7 = (bf16[320,768]{1,0:T(8,128)(2,1)S(1)}, bf16[320,768]{1,0:T(8,128)(2,1)S(1)}, u32[]{:S(2)}, u32[]{:S(2)}) collective-permute-start(bf16[320,768]{1,0:T(8,128)(2,1)S(1)} %get-tuple-element.27), channel_id=1, source_target_pairs={{0,2},{2,0},{1,3},{3,1},{4,6},{6,4},{5,7},{7,5},{8,10},{10,8},{9,1... | collective-permute-start | bytes 1474568 | tf_op jit(solution)/shard_map/ppermute | solution.py:462
  8.0 21.5 %collective-permute-start.4 = (bf16[128,768]{1,0:T(8,128)(2,1)S(1)}, bf16[128,768]{1,0:T(8,128)(2,1)S(1)}, u32[]{:S(2)}, u32[]{:S(2)}) collective-permute-start(bf16[128,768]{1,0:T(8,128)(2,1)S(1)} %get-tuple-element.24), channel_id=1, source_target_pairs={{0,2},{2,0},{1,3},{3,1},{4,6},{6,4},{5,7},{7,5},{8,10},{10,8},{9,1... | collective-permute-start | bytes 589832 | tf_op jit(solution)/shard_map/ppermute | solution.py:462
  16.0 50.0 %collective-permute-start.11 = (bf16[96,1536]{1,0:T(8,128)(2,1)}, bf16[96,1536]{1,0:T(8,128)(2,1)}, u32[]{:S(2)}, u32[]{:S(2)}) collective-permute-start(bf16[96,1536]{1,0:T(8,128)(2,1)} %collective-permute-done.10.rest_3_), channel_id=1, source_target_pairs={{0,16},{16,0},{1,17},{17,1},{2,18},{18,2},{3,19},{19,3},{4,20},{20... | collective-permute-start | bytes 884744 | tf_op jit(solution)/shard_map/ppermute | solution.py:478
  43.2 22.7 %collective-permute-start.5 = (bf16[64,1536]{1,0:T(8,128)(2,1)}, bf16[64,1536]{1,0:T(8,128)(2,1)S(1)}, u32[]{:S(2)}, u32[]{:S(2)}) collective-permute-start(bf16[64,1536]{1,0:T(8,128)(2,1)} %get-tuple-element.25), channel_id=1, source_target_pairs={{0,4},{4,8},{8,12},{1,5},{5,9},{9,13},{2,6},{6,10},{10,14},{3,7},{... | collective-permute-start | bytes 589832 | tf_op jit(solution)/shard_map/ppermute | solution.py:472
  46.7 3.9 %collective-permute-start = (f32[8,768]{1,0:T(8,128)S(1)}, f32[8,768]{1,0:T(8,128)S(1)}, u32[]{:S(2)}, u32[]{:S(2)}) collective-permute-start(f32[8,768]{1,0:T(8,128)S(1)} %get-tuple-element.21.refs_0_), channel_id=1, source_target_pairs={{0,2},{2,0},{1,3},{3,1},{4,6},{6,4},{5,7},{7,5},{8,10},{10,8},{9,1... | collective-permute-start | bytes 73736 | tf_op jit(solution)/shard_map/ppermute | solution.py:462
  48.3 24.2 %collective-permute-start.6 = (bf16[64,1536]{1,0:T(8,128)(2,1)}, bf16[64,1536]{1,0:T(8,128)(2,1)S(1)}, u32[]{:S(2)}, u32[]{:S(2)}) collective-permute-start(bf16[64,1536]{1,0:T(8,128)(2,1)} %get-tuple-element.26), channel_id=1, source_target_pairs={{4,0},{8,4},{12,8},{5,1},{9,5},{13,9},{6,2},{10,6},{14,10},{7,3},{... | collective-permute-start | bytes 589832 | tf_op jit(solution)/shard_map/ppermute | solution.py:472
  50.7 1.2 collective-permute-start.1
  53.9 3.9 %collective-permute-start.2 = (f32[2,1536]{1,0:T(2,128)}, f32[2,1536]{1,0:T(2,128)S(1)}, u32[]{:S(2)}, u32[]{:S(2)}) collective-permute-start(f32[2,1536]{1,0:T(2,128)} %merge.4.a), channel_id=1, source_target_pairs={{0,4},{4,0},{8,12},{12,8},{1,5},{5,1},{9,13},{13,9},{2,6},{6,2},{1... | collective-permute-start | bytes 36872 | tf_op jit(solution)/shard_map/ppermute | solution.py:159
  59.7 4.8 %collective-permute-start.3 = (f32[2,1536]{1,0:T(2,128)}, f32[2,1536]{1,0:T(2,128)S(1)}, u32[]{:S(2)}, u32[]{:S(2)}) collective-permute-start(f32[2,1536]{1,0:T(2,128)} %merge.5.a), channel_id=1, source_target_pairs={{0,8},{4,12},{8,0},{12,4},{1,9},{5,13},{9,1},{13,5},{2,10},{6,14},... | collective-permute-start | bytes 36872 | tf_op jit(solution)/shard_map/ppermute | solution.py:159
  64.5 22.1 %collective-permute-start.8 = (bf16[192,768]{1,0:T(8,128)(2,1)}, bf16[192,768]{1,0:T(8,128)(2,1)}, u32[]{:S(2)}, u32[]{:S(2)}) collective-permute-start(bf16[192,768]{1,0:T(8,128)(2,1)} %get-tuple-element.28), channel_id=1, source_target_pairs={{0,2},{2,0},{1,3},{3,1},{4,6},{6,4},{5,7},{7,5},{8,10},{10,8},{9,1... | collective-permute-start | bytes 884744 | tf_op jit(solution)/shard_map/ppermute | solution.py:462
  65.9 30.3 %collective-permute-start.12 = (bf16[96,1536]{1,0:T(8,128)(2,1)}, bf16[96,1536]{1,0:T(8,128)(2,1)}, u32[]{:S(2)}, u32[]{:S(2)}) collective-permute-start(bf16[96,1536]{1,0:T(8,128)(2,1)} %collective-permute-done.10.rest_3_), channel_id=1, source_target_pairs={{0,1},{1,0},{2,3},{3,2},{4,5},{5,4},{6,7},{7,6},{8,9},{9,8},{10,11... | collective-permute-start | bytes 884744 | tf_op jit(solution)/shard_map/ppermute | solution.py:479
  65.9 30.3 %collective-permute-start.13 = (bf16[96,1536]{1,0:T(8,128)(2,1)}, bf16[96,1536]{1,0:T(8,128)(2,1)}, u32[]{:S(2)}, u32[]{:S(2)}) collective-permute-start(bf16[96,1536]{1,0:T(8,128)(2,1)} %collective-permute-done.11.rest_4_), channel_id=1, source_target_pairs={{0,1},{1,0},{2,3},{3,2},{4,5},{5,4},{6,7},{7,6},{8,9},{9,8},{10,11... | collective-permute-start | bytes 884744 | tf_op jit(solution)/shard_map/ppermute | solution.py:479
  86.0 10.3 %collective-permute-start.14 = (bf16[320,384]{1,0:T(8,128)(2,1)S(1)}, bf16[320,384]{1,0:T(8,128)(2,1)S(1)}, u32[]{:S(2)}, u32[]{:S(2)}) collective-permute-start(bf16[320,384]{1,0:T(8,128)(2,1)S(1)} %conv0_0.1.rest_0_), channel_id=1, source_target_pairs={{0,2},{2,0},{1,3},{3,1},{4,6},{6,4},{5,7},{7,5},{8,10},{10,8},{9,1... | collective-permute-start | bytes 737288 | tf_op jit(solution)/shard_map/ppermute | solution.py:462
  94.9 7.8 %collective-permute-start.9 = (bf16[320,384]{1,0:T(8,128)(2,1)S(1)}, bf16[320,384]{1,0:T(8,128)(2,1)S(1)}, u32[]{:S(2)}, u32[]{:S(2)}) collective-permute-start(bf16[320,384]{1,0:T(8,128)(2,1)S(1)} %conv0_320.1.rest_0_), channel_id=1, source_target_pairs={{0,2},{2,0},{1,3},{3,1},{4,6},{6,4},{5,7},{7,5},{8,10},{10,8},{9,1... | collective-permute-start | bytes 737288 | tf_op jit(solution)/shard_map/ppermute | solution.py:462
  100.8 12.4 %collective-permute-start.21 = (bf16[192,768]{1,0:T(8,128)(2,1)S(1)}, bf16[192,768]{1,0:T(8,128)(2,1)}, u32[]{:S(2)}, u32[]{:S(2)}) collective-permute-start(bf16[192,768]{1,0:T(8,128)(2,1)S(1)} %get-tuple-element.36), channel_id=1, source_target_pairs={{0,2},{2,0},{1,3},{3,1},{4,6},{6,4},{5,7},{7,5},{8,10},{10,8},{9,1... | collective-permute-start | bytes 884744 | tf_op jit(solution)/shard_map/ppermute | solution.py:462
  107.2 22.3 %collective-permute-start.18 = (bf16[64,1536]{1,0:T(8,128)(2,1)}, bf16[64,1536]{1,0:T(8,128)(2,1)S(1)}, u32[]{:S(2)}, u32[]{:S(2)}) collective-permute-start(bf16[64,1536]{1,0:T(8,128)(2,1)} %get-tuple-element.34), channel_id=1, source_target_pairs={{0,4},{4,8},{8,12},{1,5},{5,9},{9,13},{2,6},{6,10},{10,14},{3,7},{... | collective-permute-start | bytes 589832 | tf_op jit(solution)/shard_map/ppermute | solution.py:506
  110.7 18.9 %collective-permute-start.19 = (bf16[64,1536]{1,0:T(8,128)(2,1)}, bf16[64,1536]{1,0:T(8,128)(2,1)S(1)}, u32[]{:S(2)}, u32[]{:S(2)}) collective-permute-start(bf16[64,1536]{1,0:T(8,128)(2,1)} %get-tuple-element.35), channel_id=1, source_target_pairs={{4,0},{8,4},{12,8},{5,1},{9,5},{13,9},{6,2},{10,6},{14,10},{7,3},{... | collective-permute-start | bytes 589832 | tf_op jit(solution)/shard_map/ppermute | solution.py:506
  113.3 38.9 %collective-permute-start.22 = (bf16[192,768]{1,0:T(8,128)(2,1)}, bf16[192,768]{1,0:T(8,128)(2,1)S(1)}, u32[]{:S(2)}, u32[]{:S(2)}) collective-permute-start(bf16[192,768]{1,0:T(8,128)(2,1)} %collective-permute-done.21.rest_3_), channel_id=1, source_target_pairs={{0,1},{1,0},{2,3},{3,2},{4,5},{5,4},{6,7},{7,6},{8,9},{9,8},{10,11... | collective-permute-start | bytes 884744 | tf_op jit(solution)/shard_map/ppermute | solution.py:511
  113.4 1.6 collective-permute-start.15
  116.9 3.9 %collective-permute-start.16 = (f32[2,1536]{1,0:T(2,128)}, f32[2,1536]{1,0:T(2,128)S(1)}, u32[]{:S(2)}, u32[]{:S(2)}) collective-permute-start(f32[2,1536]{1,0:T(2,128)} %merge.6.a), channel_id=1, source_target_pairs={{0,4},{4,0},{8,12},{12,8},{1,5},{5,1},{9,13},{13,9},{2,6},{6,2},{1... | collective-permute-start | bytes 36872 | tf_op jit(solution)/shard_map/ppermute | solution.py:159
  122.7 4.8 %collective-permute-start.17 = (f32[2,1536]{1,0:T(2,128)}, f32[2,1536]{1,0:T(2,128)S(1)}, u32[]{:S(2)}, u32[]{:S(2)}) collective-permute-start(f32[2,1536]{1,0:T(2,128)} %merge.7.a), channel_id=1, source_target_pairs={{0,8},{4,12},{8,0},{12,4},{1,9},{5,13},{9,1},{13,5},{2,10},{6,14},... | collective-permute-start | bytes 36872 | tf_op jit(solution)/shard_map/ppermute | solution.py:159
  143.5 8.6 %collective-permute-start.23 = (bf16[320,384]{1,0:T(8,128)(2,1)S(1)}, bf16[320,384]{1,0:T(8,128)(2,1)S(1)}, u32[]{:S(2)}, u32[]{:S(2)}) collective-permute-start(bf16[320,384]{1,0:T(8,128)(2,1)S(1)} %conv1_0.1.rest_0_), channel_id=1, source_target_pairs={{0,2},{2,0},{1,3},{3,1},{4,6},{6,4},{5,7},{7,5},{8,10},{10,8},{9,1... | collective-permute-start | bytes 737288 | tf_op jit(solution)/shard_map/ppermute | solution.py:462
  151.5 6.3 %collective-permute-start.20 = (bf16[320,384]{1,0:T(8,128)(2,1)S(1)}, bf16[320,384]{1,0:T(8,128)(2,1)S(1)}, u32[]{:S(2)}, u32[]{:S(2)}) collective-permute-start(bf16[320,384]{1,0:T(8,128)(2,1)S(1)} %conv1_320.1.rest_0_), channel_id=1, source_target_pairs={{0,2},{2,0},{1,3},{3,1},{4,6},{6,4},{5,7},{7,5},{8,10},{10,8},{9,1... | collective-permute-start | bytes 737288 | tf_op jit(solution)/shard_map/ppermute | solution.py:462
  (33 other events, 217.5 us)

commit v3 on v2

v3 whole, which is shorter than its diff:
```python
import functools

import jax
import jax.numpy as jnp
from jax import lax
from jax.experimental import pallas as pl
from jax.experimental.pallas import tpu as pltpu
from jax.sharding import PartitionSpec as P

HALO = 64
EPS = 1e-05
F32 = jnp.float32
BF16 = jnp.bfloat16
SWAP = [(0, 1), (1, 0)]

ANY = pl.BlockSpec(memory_space=pl.ANY)
HBM = pl.BlockSpec(memory_space=pltpu.HBM)
INV = pl.BlockSpec(memory_space=pltpu.VMEM)
INS = pl.BlockSpec(memory_space=pltpu.SMEM)
FREE = pl.CostEstimate(flops=0, transcendentals=0, bytes_accessed=0)


def limit(mib):
    return pltpu.CompilerParams(vmem_limit_bytes=mib << 20)


dot = functools.partial(jnp.dot, preferred_element_type=F32)
copy = pltpu.make_async_copy


def shape(dims, dtype):
    return jax.ShapeDtypeStruct(tuple(dims), dtype)


def gelu(x):
    return jax.nn.gelu(x)


def side_of(back, n):
    return lax.rem(lax.axis_index("chan") - back + n, n)


def columns(back, n, width):
    return pl.ds(pl.multiple_of(side_of(back, n) * width, 128), width)


def run(copies):
    for c in copies:
        c.start()
    for c in copies:
        c.wait()


def sums_about(v, pivot):
    gap = (v - pivot).reshape(v.shape[0] // 8, 8, v.shape[1])
    return jnp.sum(gap, axis=0), jnp.sum(gap * gap, axis=0)


def spread_of(pivot, s1, s2, rows):
    s1 = jnp.sum(s1, axis=0, keepdims=True)
    s2 = jnp.sum(s2, axis=0, keepdims=True)
    off = s1 * (1.0 / rows)
    return pivot + off, s2 - s1 * off


def merged(a, b, n):
    gap = a[0:1] - b[0:1]
    return (a[0:1] + b[0:1]) * 0.5, a[1:2] + b[1:2] + gap * gap * (0.5 * n)


def pre_kernel(x, out):
    rows = x.shape[0]
    pivot = jnp.mean(x[0:16, :].astype(F32)[0:8], axis=0, keepdims=True)
    s1 = s2 = jnp.zeros((8, x.shape[1]), F32)
    for r in range(0, rows, 64):
        t1, t2 = sums_about(x[r : r + 64, :].astype(F32), pivot)
        s1, s2 = s1 + t1, s2 + t2
    out[0:1, :], out[1:2, :] = spread_of(pivot, s1, s2, rows)


def pre(own):
    return pl.pallas_call(
        pre_kernel,
        out_shape=shape((2, own.shape[1]), F32),
        in_specs=[INV],
        out_specs=INV,
        compiler_params=limit(2),
        cost_estimate=FREE,
        name="pre",
    )(own)


def merge_kernel(n, a, b, out):
    out[0:1, :], out[1:2, :] = merged(a[...], b[...], n)


def scale_of(m2, n, gain):
    return lax.rsqrt(m2 * (1.0 / n) + EPS) * gain


def finish0_kernel(n, a, b, gains, biases, _, out):
    mean, m2 = merged(a[...], b[...], n)
    out[0:1, :] = mean
    out[1:2, :] = scale_of(m2, 2 * n, gains[0:1, :])
    out[2:3, :] = biases[0:1, :]
    out[3:4, :] = gains[1:2, :]
    out[4:5, :] = biases[1:2, :]


def finish1_kernel(n, a, b, joined, out):
    mean, m2 = merged(a[...], b[...], n)
    out[0:1, :] = mean
    out[1:2, :] = scale_of(m2, 2 * n, joined[3:4, :])
    out[2:3, :] = joined[4:5, :]


def batch_stats(stat, n, kernel, extra):
    steps = []
    for axis in ("dp", "seq"):
        size, step = lax.axis_size(axis), 1
        while step < size:
            steps.append((axis, [(i, i ^ step) for i in range(size)]))
            step *= 2
    channels = stat.shape[1]
    for at, (axis, pairs) in enumerate(steps):
        other = lax.ppermute(stat, axis, pairs)
        last = at == len(steps) - 1
        more = extra if last else ()
        stat = pl.pallas_call(
            functools.partial(kernel if last else merge_kernel, n),
            out_shape=shape((8 if last else 2, channels), F32),
            in_specs=[INV] * (2 + min(len(more), 2)) + [ANY] * max(len(more) - 2, 0),
            out_specs=INV,
            compiler_params=limit(1),
            cost_estimate=FREE,
            name="finish" if last else "merge",
        )(stat, other, *more)
        n *= 2
    return stat


def join_kernel(n, *refs):
    vecs, xs, w = refs[:n], refs[n : 2 * n], refs[2 * n]
    joined, low, high, wsend, lows, highs, sems, wsem = refs[2 * n + 1 :]
    rows = xs[0].shape[0]
    part = wsend.shape[0]
    quarter = lax.axis_index("groups") * 2 + lax.axis_index("dp")
    move = copy(w.at[0, pl.ds(pl.multiple_of(quarter * part, 16), part)], wsend, wsem)
    move.start()
    copies = []
    for k, x in enumerate(xs):
        copies.append(copy(x.at[pl.ds(rows - HALO, HALO)], lows.at[k], sems.at[2 * k]))
        copies.append(copy(x.at[pl.ds(0, HALO)], highs.at[k], sems.at[2 * k + 1]))
    for c in copies:
        c.start()
    for k, vec in enumerate(vecs):
        joined[:, columns(k, n, vec.shape[1])] = vec[...]
    for c in copies:
        c.wait()
    for k in range(n):
        cols = columns(k, n, xs[0].shape[1])
        low[:, cols] = lows[k]
        high[:, cols] = highs[k]
    move.wait()


def join(vecs, xs, w_proj):
    n, width = len(vecs), vecs[0].shape[1]
    part = w_proj.shape[1] // 4
    return pl.pallas_call(
        functools.partial(join_kernel, n),
        out_shape=(
            shape((8, n * width), F32),
            shape((HALO, n * width), BF16),
            shape((HALO, n * width), BF16),
            shape((part, w_proj.shape[2]), BF16),
        ),
        in_specs=[INV] * n + [ANY] * (n + 1),
        out_specs=(INV, INV, INV, ANY),
        scratch_shapes=[
            pltpu.VMEM((n, HALO, width), BF16),
            pltpu.VMEM((n, HALO, width), BF16),
            pltpu.SemaphoreType.DMA((2 * n,)),
            pltpu.SemaphoreType.DMA,
        ],
        compiler_params=limit(2),
        cost_estimate=FREE,
        name="join",
    )(*vecs, *xs, w_proj)


def keep_kernel(lengths, dilations, out):
    rows = out.shape[1]
    first = lax.axis_index("seq") * rows
    ends, end = [], jnp.int32(0)
    for k in range(lengths.shape[1]):
        end = end + lengths[0, k]
        ends.append(end)

    def segment(place):
        count = jnp.where(place >= 0, 1, 0)
        for end in ends:
            count = count + jnp.where(place >= end, 1, 0)
        return count

    @pl.loop(0, rows // 32)
    def _(i):
        at = pl.multiple_of(i * 32, 32)
        place = first + at + lax.broadcasted_iota(jnp.int32, (32, 128), 0)
        here = segment(place)
        for layer in range(2):
            d = dilations[layer]
            for side, there in enumerate((place - d, place + d)):
                keep = jnp.where(segment(there) == here, 1.0, 0.0)
                out[2 * layer + side, pl.ds(at, 32), :] = keep


def keeps(lengths, dilations, rows):
    return pl.pallas_call(
        keep_kernel,
        out_shape=shape((4, rows, 128), F32),
        in_specs=[INS, INS],
        out_specs=INV,
        compiler_params=limit(4),
                cost_estimate=FREE,
                name="keeps",
    )(lengths, dilations)


def shifted(ref, start, count):
    base = pl.multiple_of((start // 8) * 8, 8)
    tall = ref[pl.ds(base, count + 8), :]
    return pltpu.roll(tall, (count + 8 - (start - base)) % (count + 8), 0)[:count]


def piece(src, at, count, to, back, n, buf, sem):
    if back is None:
        dst = buf.at[pl.ds(to, count), :]
    else:
        dst = buf.at[pl.ds(to, count), columns(back, n, src.shape[1])]
    return copy(src.at[pl.ds(at, count), :], dst, sem)


def conv_kernel(pieces, layer, segs, ext, n, n_src, dilations, stats, keep, w_hbm, *rest):
    srcs, (out, xbuf, nbuf, wbuf, p0, p2, sems, wsems) = rest[:n_src], rest[n_src:]
    moves = [piece(srcs[p[0]], *p[1:], n, xbuf, sems.at[k]) for k, p in enumerate(pieces)]
    for m in moves:
        m.start()
    weights = [copy(w_hbm.at[layer, tap], wbuf.at[tap], wsems.at[tap]) for tap in range(3)]
    for w in weights:
        w.start()
    for m in moves:
        m.wait()
    block = 16
    mean, scale, bias = stats[0:1, :], stats[1:2, :], stats[2:3, :]

    @pl.loop(0, ext // block)
    def _(i):
        at = pl.ds(pl.multiple_of(i * block, block), block)
        v = xbuf[at, :].astype(F32)
        nbuf[at, :] = gelu((v - mean) * scale + bias).astype(BF16)

    weights[0].wait()
    p0[0 : ext - HALO, :] = dot(nbuf[0 : ext - HALO, :], wbuf[0])
    weights[2].wait()
    p2[0 : ext - HALO, :] = dot(nbuf[HALO:ext, :], wbuf[2])
    weights[1].wait()
    mid = dot(nbuf[HALO : ext - HALO, :], wbuf[1])
    d = dilations[layer]
    width = out.shape[1]
    to = 0
    for first, count in segs:
        base = to + 2 * HALO * segs.index((first, count))
        for r in range(0, count, HALO):
            left = shifted(p0, base + r + HALO - d, HALO)
            right = shifted(p2, base + r + d, HALO)
            here = slice(first + r, first + r + HALO)
            for c in range(0, width, 128):
                wide = min(128, width - c)
                cs = slice(c, c + wide)
                kl, kr = keep[2 * layer, here, :wide] > 0, keep[2 * layer + 1, here, :wide] > 0
                mixed = jnp.where(kl, left[:, cs], 0.0) + jnp.where(kr, right[:, cs], 0.0)
                mixed = mid[base + r : base + r + HALO, cs] + mixed
                out[to + r : to + r + HALO, cs] = gelu(mixed).astype(BF16)
        to += count


def conv(pieces, srcs, n, layer, segs, dilations, stats, keep, w_conv):
    channels, width = w_conv.shape[2:]
    rows = sum(count for _, count in segs)
    ext = rows + 2 * HALO * len(segs)
    return pl.pallas_call(
        functools.partial(conv_kernel, pieces, layer, segs, ext, n, len(srcs)),
        out_shape=shape((rows, width), BF16),
        in_specs=[INS, INV, INV, HBM] + [ANY] * len(srcs),
        out_specs=INV,
        scratch_shapes=[
            pltpu.VMEM((ext, channels), BF16),
            pltpu.VMEM((ext, channels), BF16),
            pltpu.VMEM((3, channels, width), BF16),
            pltpu.VMEM((ext - HALO + 8, width), F32),
            pltpu.VMEM((ext - HALO + 8, width), F32),
            pltpu.SemaphoreType.DMA((len(pieces),)),
            pltpu.SemaphoreType.DMA((3,)),
        ],
        compiler_params=limit(12),
        cost_estimate=FREE,
        name=f"conv{layer}_{len(segs)}",
    )(dilations, stats, keep, w_conv, *srcs)


def weight_copies(layer, cols, w_hbm, sends, wbuf, sems):
    copies = [copy(w_hbm.at[layer, :, cols], wbuf.at[0], sems.at[0])]
    for k, parts in enumerate(sends):
        size = parts[0][0].shape[0]
        for src, at in parts:
            dst = wbuf.at[k + 1, pl.ds(pl.multiple_of(at * size, 16), size), :]
            copies.append(copy(src, dst, sems.at[len(copies)]))
    return copies


def quarters(refs):
    group, core = lax.axis_index("groups"), lax.axis_index("dp")
    ats = (2 * group + core, 2 * (1 - group) + core, 2 * group + 1 - core, 3 - 2 * group - core)
    return [list(zip(refs[i : i + 4], ats)) for i in range(0, len(refs), 4)]


def halves(refs):
    core = lax.axis_index("dp")
    return [list(zip(refs[i : i + 2], (core, 1 - core))) for i in range(0, len(refs), 2)]


def update_of(inners, wbuf, cols):
    total = None
    for k, inner in enumerate(inners):
        term = dot(inner[...], wbuf[k, :, cols]).astype(BF16).astype(F32)
        total = term if total is None else total + term
    return total


def proj0_kernel(n, *rest):
    ins, edges, rest = rest[:n], rest[n : 2 * n], rest[2 * n :]
    w_hbm, sends, rest = rest[0], rest[1 : 4 * n - 3], rest[4 * n - 3 :]
    xs, (mid, low, high, stat, *wsend, xbuf, wbuf, sems, wsems, ssems) = rest[:n], rest[n:]
    rows = xbuf.shape[0]
    end = rows - HALO
    copies = weight_copies(0, slice(None), w_hbm, quarters(sends), wbuf, wsems)
    copies += [piece(x, 0, rows, 0, k, n, xbuf, sems.at[k]) for k, x in enumerate(xs)]
    moves = []
    for k, dst in enumerate(wsend):
        size, width = dst.shape
        ahead = lax.rem(lax.axis_index("chan") + k + 1, n) * width
        part = pl.ds(pl.multiple_of(lax.axis_index("dp") * size, 16), size)
        src = w_hbm.at[1, part, pl.ds(pl.multiple_of(ahead, 128), width)]
        moves.append(copy(src, dst, ssems.at[k]))
    for c in copies + moves:
        c.start()
    for c in copies:
        c.wait()
    for col in range(0, xbuf.shape[1], 256):
        cs = slice(col, col + 256)
        new = (xbuf[HALO:end, cs].astype(F32) + update_of(ins, wbuf, cs)).astype(BF16)
        mid[:, cs] = new
        v = new.astype(F32)
        pivot = jnp.mean(v[0:8], axis=0, keepdims=True)
        s1, s2 = sums_about(v, pivot)
        ends = update_of(edges, wbuf, cs)
        for dst, at, x in ((low, 0, 0), (high, HALO, end)):
            new = xbuf[x : x + HALO, cs].astype(F32) + ends[at : at + HALO]
            new = new.astype(BF16)
            dst[:, cs] = new
            t1, t2 = sums_about(new.astype(F32), pivot)
            s1, s2 = s1 + t1, s2 + t2
        stat[0:1, cs], stat[1:2, cs] = spread_of(pivot, s1, s2, rows)
    for m in moves:
        m.wait()


def proj0(inners, edges, w_proj, sends, xs):
    hidden, channels = w_proj.shape[1:]
    n = len(inners)
    rows = xs[0].shape[0]
    outs = [shape((rows - 2 * HALO, channels), BF16)]
    outs += [shape((HALO, channels), BF16)] * 2 + [shape((2, channels), F32)]
    outs += [shape((hidden // 2, channels // n), BF16)] * (n - 1)
    return pl.pallas_call(
        functools.partial(proj0_kernel, n),
        out_shape=outs,
        in_specs=[INV] * 2 * n + [HBM] + [ANY] * (len(sends) + n),
        out_specs=[INV] * 4 + [ANY] * (n - 1),
        scratch_shapes=[
            pltpu.VMEM((rows, channels), BF16),
            pltpu.VMEM((n, hidden, channels), BF16),
            pltpu.SemaphoreType.DMA((n,)),
            pltpu.SemaphoreType.DMA((4 * n - 3,)),
            pltpu.SemaphoreType.DMA((n - 1,)),
        ],
        compiler_params=limit(14),
        cost_estimate=FREE,
        name="proj0",
    )(*inners, *edges, w_proj, *sends, *xs)


def proj1_kernel(runs, n, n_src, last, *rest):
    inners, w_hbm, sends, rest = rest[:n], rest[n], rest[n + 1 : 3 * n - 1], rest[3 * n - 1 :]
    srcs, (out, xbuf, obuf, wbuf, sems, wsems) = rest[:n_src], rest[n_src + int(last) :]
    width = xbuf.shape[1]
    cols = columns(0, n, width)
    copies = weight_copies(1, cols, w_hbm, halves(sends), wbuf, wsems)
    at, outs = 0, []
    for k, (first, count) in enumerate(runs):
        here = pl.ds(at, count)
        copies.append(copy(srcs[k].at[:, cols], xbuf.at[here], sems.at[2 * k]))
        outs.append(copy(obuf.at[here], out.at[pl.ds(first, count)], sems.at[2 * k + 1]))
        at += count
    run(copies)
    for col in range(0, width, 128):
        cs = slice(col, col + 128)
        obuf[:, cs] = (xbuf[:, cs].astype(F32) + update_of(inners, wbuf, cs)).astype(BF16)
    run(outs)


def proj1(runs, total, inners, w_proj, sends, srcs, before=None):
    hidden, channels = w_proj.shape[1:]
    n = len(inners)
    width = channels // n
    rows = sum(count for _, count in runs)
    last = before is not None
    extra = [before] if last else []
    n_any = len(sends) + len(srcs)
    return pl.pallas_call(
        functools.partial(proj1_kernel, runs, n, len(srcs), last),
        out_shape=shape((total, width), BF16),
        in_specs=[INV] * n + [HBM] + [ANY] * n_any + [HBM] * len(extra),
        out_specs=HBM,
        scratch_shapes=[
            pltpu.VMEM((rows, width), BF16),
            pltpu.VMEM((rows, width), BF16),
            pltpu.VMEM((n, hidden, width), BF16),
            pltpu.SemaphoreType.DMA((2 * len(runs),)),
            pltpu.SemaphoreType.DMA((2 * n - 1,)),
        ],
        input_output_aliases={n + 1 + n_any: 0} if last else {},
        compiler_params=limit(6),
        cost_estimate=FREE,
        name=f"proj1_{rows}",
    )(*inners, w_proj, *sends, *srcs, *extra)


def on_device(signal, lengths, dilations, w_conv, w_proj, gains, biases):
    own = signal[0]
    rows = own.shape[0]
    end = rows - HALO
    n_seq, n = lax.axis_size("seq"), lax.axis_size("chan")
    up = [(i, i + 1) for i in range(n_seq - 1)]
    down = [(i + 1, i) for i in range(n_seq - 1)]
    perm = lax.ppermute

    def ahead(value, k):
        return perm(value, "chan", [(i, (i + k) % n) for i in range(n)])

    def others(value):
        return [ahead(value, k) for k in range(1, n)]

    w_conv = pltpu.with_memory_space_constraint(w_conv, pltpu.HBM)
    w_proj = pltpu.with_memory_space_constraint(w_proj, pltpu.HBM)
    xs = [own] + others(own)
    keep = keeps(lengths, dilations, rows)
    vec = batch_stats(pre(own), rows, finish0_kernel, (gains, biases, keep))
    joined, low, high, wsend = join([vec] + others(vec), xs, w_proj)
    low0, high0 = perm(low, "seq", up), perm(high, "seq", down)

    sent = others(wsend)

    inside, edges = ((HALO, end - HALO),), ((0, HALO), (end, HALO))
    pieces_a = [(k, 0, rows, 0, k) for k in range(n)]
    pieces_b = [(n, 0, HALO, 0, None), (n + 1, 0, HALO, 5 * HALO, None)]
    for k in range(n):
        pieces_b += [(k, 0, 2 * HALO, HALO, k), (k, end - HALO, 2 * HALO, 3 * HALO, k)]
    inner_a = conv(pieces_a, xs, n, 0, inside, dilations, joined, keep, w_conv)

    sent, inner_a = lax.optimization_barrier((sent, inner_a))
    swapped = [perm(w, "groups", SWAP) for w in sent]
    srcs = (*xs, low0, high0)
    inner_b = conv(pieces_b, srcs, n, 0, edges, dilations, joined, keep, w_conv)
    swapped, inner_b = lax.optimization_barrier((swapped, inner_b))
    sends0 = []
    for w, w2 in zip(sent, swapped):
        sends0 += [w, w2, perm(w, "dp", SWAP), perm(w2, "dp", SWAP)]
    inners_a = [inner_a] + others(inner_a)
    inners_b = [inner_b] + others(inner_b)
    mid, low, high, stat, *wsend1 = proj0(inners_a, inners_b, w_proj, sends0, xs)
    low1, high1 = perm(high, "seq", up), perm(low, "seq", down)
    stats1 = batch_stats(stat, rows, finish1_kernel, (joined,))
    sends1 = []
    for k, w in enumerate(wsend1):
        w = ahead(w, k + 1)
        sends1 += [w, perm(w, "dp", SWAP)]

    srcs = (low, mid, high, low1, high1)
    pieces_a = (
        (0, 0, HALO, 0, None),
        (1, 0, end - HALO, HALO, None),
        (2, 0, HALO, end, None),
    )
    pieces_b = (
        (3, 0, HALO, 0, None),
        (0, 0, HALO, HALO, None),
        (1, 0, HALO, 2 * HALO, None),
        (1, end - 2 * HALO, HALO, 3 * HALO, None),
        (2, 0, HALO, 4 * HALO, None),
        (4, 0, HALO, 5 * HALO, None),
    )
    inner_a = conv(pieces_a, srcs[:3], n, 1, inside, dilations, stats1, keep, w_conv)
    inner_b = conv(pieces_b, srcs, n, 1, edges, dilations, stats1, keep, w_conv)
    inners_a = [inner_a] + others(inner_a)
    inners_b = [inner_b] + others(inner_b)
    out = proj1(inside, rows, inners_a, w_proj, sends1, (mid,))
    return proj1(edges, rows, inners_b, w_proj, sends1, (low, high), out)[None]


def solution(mesh):
    placed = (
        P(("groups", "dp"), "seq", "chan"),
        P(("groups", "dp"), None),
        P(),
        P(None, None, None, "chan"),
        P(None, "chan", None),
        P(None, "chan"),
        P(None, "chan"),
    )
    return jax.shard_map(
        on_device,
        mesh=mesh,
        in_specs=placed,
        out_specs=P(("groups", "dp"), "seq", "chan"),
        check_vma=False,
    )
```

time: 163 us -> 103 us (0.63)
  Pallas kernels: 65.3 us -> 37.9 us
  local copies, waits for them, and re-layouts: 26.9 us -> 3.93 us
  starting transfers between devices: 31.6 us -> 27.4 us
  waiting for transfers between devices: 36.4 us -> 32.6 us
    pallas_call x17 -> x15, Pallas kernels: 60.8 us -> 35.7 us  [the longest x4 24.6 us: conv(): pl.pallas_call(functools.partial(conv_kernel, pieces, layer, segs, ext, n...]
    unnamed x66 -> x14, local copies, waits for them, and re-layouts: 26.9 us -> 3.93 us
    ppermute x10 -> x8, waiting for transfers between devices: 22.4 us -> 12 us  [ahead(): return perm(value, 'chan', [(i, (i + k) % n) for i in range(n)])]
    ppermute x2, waiting for transfers between devices: 0.01 us -> 4.28 us  [on_device(): low0, high0 = (perm(low, 'seq', up), perm(high, 'seq', down))]
    ppermute x3, waiting for transfers between devices: 0.01 us -> 3.81 us  [the longest x2 3.81 us: on_device(): low1, high1 = (perm(high, 'seq', up), perm(low, 'seq', down))]
    ppermute x10 -> x8, starting transfers between devices: 11.4 us -> 8.46 us  [ahead(): return perm(value, 'chan', [(i, (i + k) % n) for i in range(n)])]
    pallas_call x1, Pallas kernels: 4.55 us -> 2.24 us  [keeps(): pl.pallas_call(keep_kernel, out_shape=shape((4, rows, 128), F32), in_spec...]
    ppermute x6, waiting for transfers between devices: 14 us -> 12.3 us  [batch_stats(): other = lax.ppermute(stat, axis, pairs)]
  transfers between devices with their start and end apart: 24 -> 22, of which waited for: 10 -> 13; matrix products, arithmetic and copies ran while one was open for 0% -> 0% of each run, Pallas kernels for 38% -> 30%
where the time goes in v3:
time: 103 us; the launch traced here: 102 us
  Pallas kernels  37.9 us (37%)
  waiting for transfers between devices  32.6 us (32%)
  starting transfers between devices  27.4 us (27%)
  local copies, waits for them, and re-layouts  3.93 us (4%)
    pallas_call x4, Pallas kernels, conv(): pl.pallas_call(functools.partial(conv_kernel, pieces, layer, segs, ext, n...  24.6 us
    ppermute x6, waiting for transfers between devices, batch_stats(): other = lax.ppermute(stat, axis, pairs)  12.3 us
    ppermute x8, waiting for transfers between devices, ahead(): return perm(value, 'chan', [(i, (i + k) % n) for i in range(n)])  12 us
    ppermute x8, starting transfers between devices, ahead(): return perm(value, 'chan', [(i, (i + k) % n) for i in range(n)])  8.46 us
    ppermute x2, starting transfers between devices, on_device(): low1, high1 = (perm(high, 'seq', up), perm(low, 'seq', down))  6.01 us
    ppermute x2, starting transfers between devices, on_device(): low0, high0 = (perm(low, 'seq', up), perm(high, 'seq', down))  5.84 us
    pallas_call x2, Pallas kernels, proj1(): pl.pallas_call(functools.partial(proj1_kernel, runs, n, len(srcs), last),...  5.71 us
    ppermute x6, starting transfers between devices, batch_stats(): other = lax.ppermute(stat, axis, pairs)  4.85 us
  transfers between devices with their start and end apart: 22, of which 13 were waited for; matrix products, arithmetic and copies ran while one was open for 0% of the time, Pallas kernels for 30%

profile of v3, /device:TPU:8, one launch (start us, length us, event | category | flops | bytes accessed | tf_op | source)
XLA Modules:
  0.0 102.2 jit_solution(7391575725877927555)
XLA Ops:
  0.0 1.5 %collective-permute-start.4 = (bf16[640,768]{1,0:T(8,128)(2,1)}, bf16[640,768]{1,0:T(8,128)(2,1)S(1)}, u32[]{:S(2)}, u32[]{:S(2)}) collective-permute-start(bf16[640,768]{1,0:T(8,128)(2,1)} %bitcast.2), channel_id=1, source_target_pairs={{0,2},{2,0},{1,3},{3,1},{4,6},{6,4},{5,7},{7,5},{8,10},{10,8},{9,1... | collective-permute-start | bytes 2949128 | tf_op jit(solution)/shard_map/ppermute | solution.py:460
  4.9 3.2 %collective-permute-done.1.b = f32[2,768]{1,0:T(2,128)S(1)} collective-permute-done((f32[2,768]{1,0:T(2,128)S(1)}, f32[2,768]{1,0:T(2,128)S(1)}, u32[]{:S(2)}, u32[]{:S(2)}) %collective-permute-start.1) | collective-permute-done | bytes 6176 | tf_op jit(solution)/shard_map/ppermute | solution.py:126
  8.1 2.7 %collective-permute-start.2 = (f32[2,768]{1,0:T(2,128)S(1)}, f32[2,768]{1,0:T(2,128)S(1)}, u32[]{:S(2)}, u32[]{:S(2)}) collective-permute-start(f32[2,768]{1,0:T(2,128)S(1)} %merge.5.a), channel_id=1, source_target_pairs={{0,8},{4,12},{8,0},{12,4},{1,9},{5,13},{9,1},{13,5},{2,10},{6,14},... | collective-permute-start | bytes 18440 | tf_op jit(solution)/shard_map/ppermute | solution.py:126
  12.0 2.2 %keeps.1._.keep = f32[4,640,128]{2,1,0:T(8,128)S(1)} custom-call(s32[1,8]{1,0:T(1,128)S(1)} %copy-done.6, s32[2]{0:T(128)S(1)} %copy-done.2), custom_call_target="tpu_custom_call" | custom-call | tf_op jit(solution)/shard_map/keeps/pallas_call | solution.py:219
  16.3 7.9 %collective-permute-done.3.refs_1_ = f32[8,768]{1,0:T(8,128)S(1)} collective-permute-done((f32[8,768]{1,0:T(8,128)S(1)}, f32[8,768]{1,0:T(8,128)S(1)}, u32[]{:S(2)}, u32[]{:S(2)}) %collective-permute-start.3) | collective-permute-done | bytes 24608 | tf_op jit(solution)/shard_map/ppermute | solution.py:460
  25.3 1.6 %collective-permute-start.5 = (bf16[96,1536]{1,0:T(8,128)(2,1)S(1)}, bf16[96,1536]{1,0:T(8,128)(2,1)S(1)}, u32[]{:S(2)}, u32[]{:S(2)}) collective-permute-start(bf16[96,1536]{1,0:T(8,128)(2,1)S(1)} %get-tuple-element.18), channel_id=1, source_target_pairs={{0,2},{2,0},{1,3},{3,1},{4,6},{6,4},{5,7},{7,5},{8,10},{10,8},{9,1... | collective-permute-start | bytes 884744 | tf_op jit(solution)/shard_map/ppermute | solution.py:460
  26.8 7.0 %conv0_1.1.rest_0_ = bf16[512,384]{1,0:T(8,128)(2,1)S(1)} custom-call(s32[2]{0:T(128)S(1)} %copy-done.3, f32[8,1536]{1,0:T(8,128)S(1)} %get-tuple-element.19.stats.joined, f32[4,640,128]{2,1,0:T(8,128)S(1)} %keeps.1._.keep, bf16[2,3,1536,384]{3,2,1,0:T(8,128)(2,1)} %w_hbm.7, bf16[640,768]{1,0:T(8,128)(2,1)S(1)} %bitcast.5, ...), custom_call_target="tpu_custom_call" | custom-call | tf_op jit(solution)/shard_map/conv0_1/pallas_call | solution.py:292
  33.8 1.6 %collective-permute-start.7 = (bf16[96,1536]{1,0:T(8,128)(2,1)S(1)}, bf16[96,1536]{1,0:T(8,128)(2,1)S(1)}, u32[]{:S(2)}, u32[]{:S(2)}) collective-permute-start(bf16[96,1536]{1,0:T(8,128)(2,1)S(1)} %collective-permute-done.5.rest_5_), channel_id=1, source_target_pairs={{0,16},{16,0},{1,17},{17,1},{2,18},{18,2},{3,19},{19,3},{4,20},{20... | collective-permute-start | bytes 884744 | tf_op jit(solution)/shard_map/ppermute | solution.py:483
  35.4 3.5 %collective-permute-start.8 = (bf16[64,1536]{1,0:T(8,128)(2,1)S(1)}, bf16[64,1536]{1,0:T(8,128)(2,1)S(1)}, u32[]{:S(2)}, u32[]{:S(2)}) collective-permute-start(bf16[64,1536]{1,0:T(8,128)(2,1)S(1)} %get-tuple-element.22), channel_id=1, source_target_pairs={{0,4},{4,8},{8,12},{1,5},{5,9},{9,13},{2,6},{6,10},{10,14},{3,7},{... | collective-permute-start | bytes 589832 | tf_op jit(solution)/shard_map/ppermute | solution.py:471
  38.8 2.4 %collective-permute-start.9 = (bf16[64,1536]{1,0:T(8,128)(2,1)S(1)}, bf16[64,1536]{1,0:T(8,128)(2,1)S(1)}, u32[]{:S(2)}, u32[]{:S(2)}) collective-permute-start(bf16[64,1536]{1,0:T(8,128)(2,1)S(1)} %get-tuple-element.23), channel_id=1, source_target_pairs={{4,0},{8,4},{12,8},{5,1},{9,5},{13,9},{6,2},{10,6},{14,10},{7,3},{... | collective-permute-start | bytes 589832 | tf_op jit(solution)/shard_map/ppermute | solution.py:471
  42.9 3.5 %collective-permute-done.9.rest_3_ = bf16[64,1536]{1,0:T(8,128)(2,1)S(1)} collective-permute-done((bf16[64,1536]{1,0:T(8,128)(2,1)S(1)}, bf16[64,1536]{1,0:T(8,128)(2,1)S(1)}, u32[]{:S(2)}, u32[]{:S(2)}) %collective-permute-start.9) | collective-permute-done | bytes 196640 | tf_op jit(solution)/shard_map/ppermute | solution.py:471
  46.4 4.7 %conv0_2.1.rest_2_ = bf16[128,384]{1,0:T(8,128)(2,1)S(1)} custom-call(s32[2]{0:T(128)S(1)} %copy-done.3, f32[8,1536]{1,0:T(8,128)S(1)} %get-tuple-element.19.stats.joined, f32[4,640,128]{2,1,0:T(8,128)S(1)} %keeps.1._.keep, bf16[2,3,1536,384]{3,2,1,0:T(8,128)(2,1)} %w_hbm.7, bf16[640,768]{1,0:T(8,128)(2,1)S(1)} %bitcast.6, ...), custom_call_target="tpu_custom_call" | custom-call | tf_op jit(solution)/shard_map/conv0_2/pallas_call | solution.py:292
  52.7 3.7 %collective-permute-done.10.rest_3_ = bf16[128,384]{1,0:T(8,128)(2,1)S(1)} collective-permute-done((bf16[128,384]{1,0:T(8,128)(2,1)S(1)}, bf16[128,384]{1,0:T(8,128)(2,1)S(1)}, u32[]{:S(2)}, u32[]{:S(2)}) %collective-permute-start.10) | collective-permute-done | bytes 98336 | tf_op jit(solution)/shard_map/ppermute | solution.py:460
  56.5 3.8 %proj0.1 = (bf16[512,1536]{1,0:T(8,128)(2,1)S(1)}, bf16[64,1536]{1,0:T(8,128)(2,1)S(1)}, bf16[64,1536]{1,0:T(8,128)(2,1)S(1)}, f32[2,1536]{1,0:T(2,128)S(1)}, bf16[192,768]{1,0:T(8,128)(2,1)S(1)}) custom-call(bf16[512,384]{1,0:T(8,128)(2,1)S(1)} %conv0_1.1.rest_0_, bf16[512,384]{1,0:T(8,128)(2,1)S(1)} %collective-permute-done.6.rest_1_, ...), custom_call_target="tpu_custom_call" | custom-call | tf_op jit(solution)/shard_map/proj0/pallas_call | solution.py:386
  62.9 3.2 %collective-permute-done.14.b = f32[2,1536]{1,0:T(2,128)S(1)} collective-permute-done((f32[2,1536]{1,0:T(2,128)S(1)}, f32[2,1536]{1,0:T(2,128)S(1)}, u32[]{:S(2)}, u32[]{:S(2)}) %collective-permute-start.14) | collective-permute-done | bytes 12320 | tf_op jit(solution)/shard_map/ppermute | solution.py:126
  67.3 3.6 %collective-permute-done.15.b = f32[2,1536]{1,0:T(2,128)S(1)} collective-permute-done((f32[2,1536]{1,0:T(2,128)S(1)}, f32[2,1536]{1,0:T(2,128)S(1)}, u32[]{:S(2)}, u32[]{:S(2)}) %collective-permute-start.15) | collective-permute-done | bytes 12320 | tf_op jit(solution)/shard_map/ppermute | solution.py:126
  70.9 7.4 %conv1_1.1.rest_0_ = bf16[512,384]{1,0:T(8,128)(2,1)S(1)} custom-call(s32[2]{0:T(128)S(1)} %copy-done.3, f32[8,1536]{1,0:T(8,128)S(1)} %finish.3.stats, f32[4,640,128]{2,1,0:T(8,128)S(1)} %keeps.1._.keep, bf16[2,3,1536,384]{3,2,1,0:T(8,128)(2,1)} %w_hbm.7, bf16[64,1536]{1,0:T(8,128)(2,1)S(1)} %get-tuple-element.27.rest_0_.rest_5_, ...), custom_call_target="tpu_custom_call" | custom-call | tf_op jit(solution)/shard_map/conv1_1/pallas_call | solution.py:292
  79.5 2.4 %collective-permute-start.17 = (bf16[64,1536]{1,0:T(8,128)(2,1)S(1)}, bf16[64,1536]{1,0:T(8,128)(2,1)S(1)}, u32[]{:S(2)}, u32[]{:S(2)}) collective-permute-start(bf16[64,1536]{1,0:T(8,128)(2,1)S(1)} %get-tuple-element.27.rest_0_.rest_5_), channel_id=1, source_target_pairs={{4,0},{8,4},{12,8},{5,1},{9,5},{13,9},{6,2},{10,6},{14,10},{7,3},{... | collective-permute-start | bytes 589832 | tf_op jit(solution)/shard_map/ppermute | solution.py:493
  81.9 3.7 %collective-permute-start.16 = (bf16[64,1536]{1,0:T(8,128)(2,1)S(1)}, bf16[64,1536]{1,0:T(8,128)(2,1)S(1)}, u32[]{:S(2)}, u32[]{:S(2)}) collective-permute-start(bf16[64,1536]{1,0:T(8,128)(2,1)S(1)} %get-tuple-element.29.rest_2_.rest_6_), channel_id=1, source_target_pairs={{0,4},{4,8},{8,12},{1,5},{5,9},{9,13},{2,6},{6,10},{10,14},{3,7},{... | collective-permute-start | bytes 589832 | tf_op jit(solution)/shard_map/ppermute | solution.py:493
  85.7 1.4 %collective-permute-done.17.rest_4_ = bf16[64,1536]{1,0:T(8,128)(2,1)S(1)} collective-permute-done((bf16[64,1536]{1,0:T(8,128)(2,1)S(1)}, bf16[64,1536]{1,0:T(8,128)(2,1)S(1)}, u32[]{:S(2)}, u32[]{:S(2)}) %collective-permute-start.17) | collective-permute-done | bytes 196640 | tf_op jit(solution)/shard_map/ppermute | solution.py:493
  87.1 2.4 %collective-permute-done.16.rest_3_ = bf16[64,1536]{1,0:T(8,128)(2,1)S(1)} collective-permute-done((bf16[64,1536]{1,0:T(8,128)(2,1)S(1)}, bf16[64,1536]{1,0:T(8,128)(2,1)S(1)}, u32[]{:S(2)}, u32[]{:S(2)}) %collective-permute-start.16) | collective-permute-done | bytes 196640 | tf_op jit(solution)/shard_map/ppermute | solution.py:493
  89.5 5.6 %conv1_2.1.rest_0_ = bf16[128,384]{1,0:T(8,128)(2,1)S(1)} custom-call(s32[2]{0:T(128)S(1)} %copy-done.3, f32[8,1536]{1,0:T(8,128)S(1)} %finish.3.stats, f32[4,640,128]{2,1,0:T(8,128)S(1)} %keeps.1._.keep, bf16[2,3,1536,384]{3,2,1,0:T(8,128)(2,1)} %w_hbm.7, bf16[64,1536]{1,0:T(8,128)(2,1)S(1)} %get-tuple-element.27.rest_0_.rest_5_, ...), custom_call_target="tpu_custom_call" | custom-call | tf_op jit(solution)/shard_map/conv1_2/pallas_call | solution.py:292
  96.0 3.4 %proj1_512.1.rest_7_ = bf16[640,768]{1,0:T(8,128)(2,1)} custom-call(bf16[512,384]{1,0:T(8,128)(2,1)S(1)} %conv1_1.1.rest_0_, bf16[512,384]{1,0:T(8,128)(2,1)S(1)} %collective-permute-done.21.rest_1_, bf16[2,384,1536]{2,1,0:T(8,128)(2,1)} %rest_2_.3, bf16[192,768]{1,0:T(8,128)(2,1)S(1)} %collective-permute-done.19.rest_3_, ...), custom_call_target="tpu_custom_call" | custom-call | tf_op jit(solution)/shard_map/proj1_512/pallas_call | solution.py:431
  99.8 2.3 %proj1_128.1 = bf16[640,768]{1,0:T(8,128)(2,1)} custom-call(bf16[128,384]{1,0:T(8,128)(2,1)S(1)} %conv1_2.1.rest_0_, bf16[128,384]{1,0:T(8,128)(2,1)S(1)} %collective-permute-done.18.rest_1_, bf16[2,384,1536]{2,1,0:T(8,128)(2,1)} %rest_2_.3, bf16[192,768]{1,0:T(8,128)(2,1)S(1)} %collective-permute-done.19.rest_3_, ...), custom_call_target="tpu_custom_call", output_to_operand_aliasing={{}: (7, {})} | custom-call | tf_op jit(solution)/shard_map/proj1_128/pallas_call | solution.py:431
  (50 shorter events, 17.4 us)
Async XLA Ops:
  0.0 24.2 %collective-permute-start.4 = (bf16[640,768]{1,0:T(8,128)(2,1)}, bf16[640,768]{1,0:T(8,128)(2,1)S(1)}, u32[]{:S(2)}, u32[]{:S(2)}) collective-permute-start(bf16[640,768]{1,0:T(8,128)(2,1)} %bitcast.2), channel_id=1, source_target_pairs={{0,2},{2,0},{1,3},{3,1},{4,6},{6,4},{5,7},{7,5},{8,10},{10,8},{9,1... | collective-permute-start | bytes 2949128 | tf_op jit(solution)/shard_map/ppermute | solution.py:460
  2.7 21.5 %copy-start.1 = (bf16[1,640,768]{2,1,0:T(8,128)(2,1)S(1)}, bf16[1,640,768]{2,1,0:T(8,128)(2,1)}, u32[]{:S(2)}) copy-start(bf16[1,640,768]{2,1,0:T(8,128)(2,1)} %param.7) | copy-start | bytes 2949124
  3.1 1.2 %collective-permute-start = (f32[2,768]{1,0:T(2,128)S(1)}, f32[2,768]{1,0:T(2,128)S(1)}, u32[]{:S(2)}, u32[]{:S(2)}) collective-permute-start(f32[2,768]{1,0:T(2,128)S(1)} %pre.1.a), channel_id=1, source_target_pairs={{0,1},{1,0},{2,3},{3,2},{4,5},{5,4},{6,7},{7,6},{8,9},{9,8},{10,11... | collective-permute-start | bytes 18440 | tf_op jit(solution)/shard_map/ppermute | solution.py:126
  4.4 3.7 %collective-permute-start.1 = (f32[2,768]{1,0:T(2,128)S(1)}, f32[2,768]{1,0:T(2,128)S(1)}, u32[]{:S(2)}, u32[]{:S(2)}) collective-permute-start(f32[2,768]{1,0:T(2,128)S(1)} %merge.4.a), channel_id=1, source_target_pairs={{0,4},{4,0},{8,12},{12,8},{1,5},{5,1},{9,13},{13,9},{2,6},{6,2},{1... | collective-permute-start | bytes 18440 | tf_op jit(solution)/shard_map/ppermute | solution.py:126
  8.1 6.2 %collective-permute-start.2 = (f32[2,768]{1,0:T(2,128)S(1)}, f32[2,768]{1,0:T(2,128)S(1)}, u32[]{:S(2)}, u32[]{:S(2)}) collective-permute-start(f32[2,768]{1,0:T(2,128)S(1)} %merge.5.a), channel_id=1, source_target_pairs={{0,8},{4,12},{8,0},{12,4},{1,9},{5,13},{9,1},{13,5},{2,10},{6,14},... | collective-permute-start | bytes 18440 | tf_op jit(solution)/shard_map/ppermute | solution.py:126
  15.7 11.1 %copy-start.3 = (s32[2]{0:T(128)S(1)}, s32[2]{0:T(128)}, u32[]{:S(2)}) copy-start(s32[2]{0:T(128)} %dilations.9) | copy-start | bytes 28
  15.7 8.5 %collective-permute-start.3 = (f32[8,768]{1,0:T(8,128)S(1)}, f32[8,768]{1,0:T(8,128)S(1)}, u32[]{:S(2)}, u32[]{:S(2)}) collective-permute-start(f32[8,768]{1,0:T(8,128)S(1)} %finish.2.refs_0_), channel_id=1, source_target_pairs={{0,2},{2,0},{1,3},{3,1},{4,6},{6,4},{5,7},{7,5},{8,10},{10,8},{9,1... | collective-permute-start | bytes 73736 | tf_op jit(solution)/shard_map/ppermute | solution.py:460
  25.3 8.5 %collective-permute-start.5 = (bf16[96,1536]{1,0:T(8,128)(2,1)S(1)}, bf16[96,1536]{1,0:T(8,128)(2,1)S(1)}, u32[]{:S(2)}, u32[]{:S(2)}) collective-permute-start(bf16[96,1536]{1,0:T(8,128)(2,1)S(1)} %get-tuple-element.18), channel_id=1, source_target_pairs={{0,2},{2,0},{1,3},{3,1},{4,6},{6,4},{5,7},{7,5},{8,10},{10,8},{9,1... | collective-permute-start | bytes 884744 | tf_op jit(solution)/shard_map/ppermute | solution.py:460
  33.8 17.4 %collective-permute-start.7 = (bf16[96,1536]{1,0:T(8,128)(2,1)S(1)}, bf16[96,1536]{1,0:T(8,128)(2,1)S(1)}, u32[]{:S(2)}, u32[]{:S(2)}) collective-permute-start(bf16[96,1536]{1,0:T(8,128)(2,1)S(1)} %collective-permute-done.5.rest_5_), channel_id=1, source_target_pairs={{0,16},{16,0},{1,17},{17,1},{2,18},{18,2},{3,19},{19,3},{4,20},{20... | collective-permute-start | bytes 884744 | tf_op jit(solution)/shard_map/ppermute | solution.py:483
  35.4 7.6 %collective-permute-start.8 = (bf16[64,1536]{1,0:T(8,128)(2,1)S(1)}, bf16[64,1536]{1,0:T(8,128)(2,1)S(1)}, u32[]{:S(2)}, u32[]{:S(2)}) collective-permute-start(bf16[64,1536]{1,0:T(8,128)(2,1)S(1)} %get-tuple-element.22), channel_id=1, source_target_pairs={{0,4},{4,8},{8,12},{1,5},{5,9},{9,13},{2,6},{6,10},{10,14},{3,7},{... | collective-permute-start | bytes 589832 | tf_op jit(solution)/shard_map/ppermute | solution.py:471
  38.8 7.6 %collective-permute-start.9 = (bf16[64,1536]{1,0:T(8,128)(2,1)S(1)}, bf16[64,1536]{1,0:T(8,128)(2,1)S(1)}, u32[]{:S(2)}, u32[]{:S(2)}) collective-permute-start(bf16[64,1536]{1,0:T(8,128)(2,1)S(1)} %get-tuple-element.23), channel_id=1, source_target_pairs={{4,0},{8,4},{12,8},{5,1},{9,5},{13,9},{6,2},{10,6},{14,10},{7,3},{... | collective-permute-start | bytes 589832 | tf_op jit(solution)/shard_map/ppermute | solution.py:471
  41.2 15.2 %collective-permute-start.6 = (bf16[512,384]{1,0:T(8,128)(2,1)S(1)}, bf16[512,384]{1,0:T(8,128)(2,1)S(1)}, u32[]{:S(2)}, u32[]{:S(2)}) collective-permute-start(bf16[512,384]{1,0:T(8,128)(2,1)S(1)} %conv0_1.1.rest_0_), channel_id=1, source_target_pairs={{0,2},{2,0},{1,3},{3,1},{4,6},{6,4},{5,7},{7,5},{8,10},{10,8},{9,1... | collective-permute-start | bytes 1179656 | tf_op jit(solution)/shard_map/ppermute | solution.py:460
  51.1 1.6 %collective-permute-start.11 = (bf16[96,1536]{1,0:T(8,128)(2,1)S(1)}, bf16[96,1536]{1,0:T(8,128)(2,1)S(1)}, u32[]{:S(2)}, u32[]{:S(2)}) collective-permute-start(bf16[96,1536]{1,0:T(8,128)(2,1)S(1)} %collective-permute-done.5.rest_5_), channel_id=1, source_target_pairs={{0,1},{1,0},{2,3},{3,2},{4,5},{5,4},{6,7},{7,6},{8,9},{9,8},{10,11... | collective-permute-start | bytes 884744 | tf_op jit(solution)/shard_map/ppermute | solution.py:489
  51.2 5.3 %collective-permute-start.12 = (bf16[96,1536]{1,0:T(8,128)(2,1)S(1)}, bf16[96,1536]{1,0:T(8,128)(2,1)S(1)}, u32[]{:S(2)}, u32[]{:S(2)}) collective-permute-start(bf16[96,1536]{1,0:T(8,128)(2,1)S(1)} %collective-permute-done.7.rest_6_), channel_id=1, source_target_pairs={{0,1},{1,0},{2,3},{3,2},{4,5},{5,4},{6,7},{7,6},{8,9},{9,8},{10,11... | collective-permute-start | bytes 884744 | tf_op jit(solution)/shard_map/ppermute | solution.py:489
  51.7 4.8 %collective-permute-start.10 = (bf16[128,384]{1,0:T(8,128)(2,1)S(1)}, bf16[128,384]{1,0:T(8,128)(2,1)S(1)}, u32[]{:S(2)}, u32[]{:S(2)}) collective-permute-start(bf16[128,384]{1,0:T(8,128)(2,1)S(1)} %conv0_2.1.rest_2_), channel_id=1, source_target_pairs={{0,2},{2,0},{1,3},{3,1},{4,6},{6,4},{5,7},{7,5},{8,10},{10,8},{9,1... | collective-permute-start | bytes 294920 | tf_op jit(solution)/shard_map/ppermute | solution.py:460
  60.3 25.2 %collective-permute-start.19 = (bf16[192,768]{1,0:T(8,128)(2,1)S(1)}, bf16[192,768]{1,0:T(8,128)(2,1)S(1)}, u32[]{:S(2)}, u32[]{:S(2)}) collective-permute-start(bf16[192,768]{1,0:T(8,128)(2,1)S(1)} %get-tuple-element.30), channel_id=1, source_target_pairs={{0,2},{2,0},{1,3},{3,1},{4,6},{6,4},{5,7},{7,5},{8,10},{10,8},{9,1... | collective-permute-start | bytes 884744 | tf_op jit(solution)/shard_map/ppermute | solution.py:460
  61.2 1.2 %collective-permute-start.13 = (f32[2,1536]{1,0:T(2,128)S(1)}, f32[2,1536]{1,0:T(2,128)S(1)}, u32[]{:S(2)}, u32[]{:S(2)}) collective-permute-start(f32[2,1536]{1,0:T(2,128)S(1)} %get-tuple-element.26.a), channel_id=1, source_target_pairs={{0,1},{1,0},{2,3},{3,2},{4,5},{5,4},{6,7},{7,6},{8,9},{9,8},{10,11... | collective-permute-start | bytes 36872 | tf_op jit(solution)/shard_map/ppermute | solution.py:126
  62.4 3.8 %collective-permute-start.14 = (f32[2,1536]{1,0:T(2,128)S(1)}, f32[2,1536]{1,0:T(2,128)S(1)}, u32[]{:S(2)}, u32[]{:S(2)}) collective-permute-start(f32[2,1536]{1,0:T(2,128)S(1)} %merge.6.a), channel_id=1, source_target_pairs={{0,4},{4,0},{8,12},{12,8},{1,5},{5,1},{9,13},{13,9},{2,6},{6,2},{1... | collective-permute-start | bytes 36872 | tf_op jit(solution)/shard_map/ppermute | solution.py:126
  66.2 4.7 %collective-permute-start.15 = (f32[2,1536]{1,0:T(2,128)S(1)}, f32[2,1536]{1,0:T(2,128)S(1)}, u32[]{:S(2)}, u32[]{:S(2)}) collective-permute-start(f32[2,1536]{1,0:T(2,128)S(1)} %merge.7.a), channel_id=1, source_target_pairs={{0,8},{4,12},{8,0},{12,4},{1,9},{5,13},{9,1},{13,5},{2,10},{6,14},... | collective-permute-start | bytes 36872 | tf_op jit(solution)/shard_map/ppermute | solution.py:126
  78.3 17.7 %collective-permute-start.21 = (bf16[512,384]{1,0:T(8,128)(2,1)S(1)}, bf16[512,384]{1,0:T(8,128)(2,1)S(1)}, u32[]{:S(2)}, u32[]{:S(2)}) collective-permute-start(bf16[512,384]{1,0:T(8,128)(2,1)S(1)} %conv1_1.1.rest_0_), channel_id=1, source_target_pairs={{0,2},{2,0},{1,3},{3,1},{4,6},{6,4},{5,7},{7,5},{8,10},{10,8},{9,1... | collective-permute-start | bytes 1179656 | tf_op jit(solution)/shard_map/ppermute | solution.py:460
  79.5 7.6 %collective-permute-start.17 = (bf16[64,1536]{1,0:T(8,128)(2,1)S(1)}, bf16[64,1536]{1,0:T(8,128)(2,1)S(1)}, u32[]{:S(2)}, u32[]{:S(2)}) collective-permute-start(bf16[64,1536]{1,0:T(8,128)(2,1)S(1)} %get-tuple-element.27.rest_0_.rest_5_), channel_id=1, source_target_pairs={{4,0},{8,4},{12,8},{5,1},{9,5},{13,9},{6,2},{10,6},{14,10},{7,3},{... | collective-permute-start | bytes 589832 | tf_op jit(solution)/shard_map/ppermute | solution.py:493
  81.9 7.6 %collective-permute-start.16 = (bf16[64,1536]{1,0:T(8,128)(2,1)S(1)}, bf16[64,1536]{1,0:T(8,128)(2,1)S(1)}, u32[]{:S(2)}, u32[]{:S(2)}) collective-permute-start(bf16[64,1536]{1,0:T(8,128)(2,1)S(1)} %get-tuple-element.29.rest_2_.rest_6_), channel_id=1, source_target_pairs={{0,4},{4,8},{8,12},{1,5},{5,9},{9,13},{2,6},{6,10},{10,14},{3,7},{... | collective-permute-start | bytes 589832 | tf_op jit(solution)/shard_map/ppermute | solution.py:493
  85.6 10.4 %collective-permute-start.20 = (bf16[192,768]{1,0:T(8,128)(2,1)S(1)}, bf16[192,768]{1,0:T(8,128)(2,1)S(1)}, u32[]{:S(2)}, u32[]{:S(2)}) collective-permute-start(bf16[192,768]{1,0:T(8,128)(2,1)S(1)} %collective-permute-done.19.rest_3_), channel_id=1, source_target_pairs={{0,1},{1,0},{2,3},{3,2},{4,5},{5,4},{6,7},{7,6},{8,9},{9,8},{10,11... | collective-permute-start | bytes 884744 | tf_op jit(solution)/shard_map/ppermute | solution.py:498
  95.1 4.7 %collective-permute-start.18 = (bf16[128,384]{1,0:T(8,128)(2,1)S(1)}, bf16[128,384]{1,0:T(8,128)(2,1)S(1)}, u32[]{:S(2)}, u32[]{:S(2)}) collective-permute-start(bf16[128,384]{1,0:T(8,128)(2,1)S(1)} %conv1_2.1.rest_0_), channel_id=1, source_target_pairs={{0,2},{2,0},{1,3},{3,1},{4,6},{6,4},{5,7},{7,5},{8,10},{10,8},{9,1... | collective-permute-start | bytes 294920 | tf_op jit(solution)/shard_map/ppermute | solution.py:460
  (5 other events, 3.9 us)

commit v4 on v3

v4 whole, which is shorter than its diff:
```python
import functools

import jax
import jax.numpy as jnp
from jax import lax
from jax.experimental import pallas as pl
from jax.experimental.pallas import tpu as pltpu
from jax.sharding import PartitionSpec as P

HALO = 64
EPS = 1e-05
F32 = jnp.float32
BF16 = jnp.bfloat16
SWAP = [(0, 1), (1, 0)]

ANY = pl.BlockSpec(memory_space=pl.ANY)
HBM = pl.BlockSpec(memory_space=pltpu.HBM)
INV = pl.BlockSpec(memory_space=pltpu.VMEM)
INS = pl.BlockSpec(memory_space=pltpu.SMEM)
FREE = pl.CostEstimate(flops=0, transcendentals=0, bytes_accessed=0)


def limit(mib):
    return pltpu.CompilerParams(vmem_limit_bytes=mib << 20)


dot = functools.partial(jnp.dot, preferred_element_type=F32)
copy = pltpu.make_async_copy


def shape(dims, dtype):
    return jax.ShapeDtypeStruct(tuple(dims), dtype)


def gelu(x):
    return jax.nn.gelu(x)


def side_of(back, n):
    return lax.rem(lax.axis_index("chan") - back + n, n)


def columns(back, n, width):
    return pl.ds(pl.multiple_of(side_of(back, n) * width, 128), width)


def run(copies):
    for c in copies:
        c.start()
    for c in copies:
        c.wait()


def sums_about(v, pivot):
    gap = (v - pivot).reshape(v.shape[0] // 8, 8, v.shape[1])
    return jnp.sum(gap, axis=0), jnp.sum(gap * gap, axis=0)


def spread_of(pivot, s1, s2, rows):
    s1 = jnp.sum(s1, axis=0, keepdims=True)
    s2 = jnp.sum(s2, axis=0, keepdims=True)
    off = s1 * (1.0 / rows)
    return pivot + off, s2 - s1 * off


def merged(a, b, n):
    gap = a[0:1] - b[0:1]
    return (a[0:1] + b[0:1]) * 0.5, a[1:2] + b[1:2] + gap * gap * (0.5 * n)


def pre_kernel(x, out):
    rows = x.shape[0]
    pivot = jnp.mean(x[0:16, :].astype(F32)[0:8], axis=0, keepdims=True)
    s1 = s2 = jnp.zeros((8, x.shape[1]), F32)
    for r in range(0, rows, 64):
        t1, t2 = sums_about(x[r : r + 64, :].astype(F32), pivot)
        s1, s2 = s1 + t1, s2 + t2
    out[0:1, :], out[1:2, :] = spread_of(pivot, s1, s2, rows)


def pre(own):
    return pl.pallas_call(
        pre_kernel,
        out_shape=shape((2, own.shape[1]), F32),
        in_specs=[INV],
        out_specs=INV,
        compiler_params=limit(2),
        cost_estimate=FREE,
        name="pre",
    )(own)


def merge_kernel(n, a, b, out):
    out[0:1, :], out[1:2, :] = merged(a[...], b[...], n)


def scale_of(m2, n, gain):
    return lax.rsqrt(m2 * (1.0 / n) + EPS) * gain


def finish0_kernel(n, a, b, gains, biases, _, out):
    mean, m2 = merged(a[...], b[...], n)
    out[0:1, :] = mean
    out[1:2, :] = scale_of(m2, 2 * n, gains[0:1, :])
    out[2:3, :] = biases[0:1, :]
    out[3:4, :] = gains[1:2, :]
    out[4:5, :] = biases[1:2, :]


def finish1_kernel(n, a, b, joined, *rest):
    out = rest[-1]
    mean, m2 = merged(a[...], b[...], n)
    out[0:1, :] = mean
    out[1:2, :] = scale_of(m2, 2 * n, joined[3:4, :])
    out[2:3, :] = joined[4:5, :]


def batch_stats(stat, n, kernel, extra, n_order):
    steps = []
    for axis in ("dp", "seq"):
        size, step = lax.axis_size(axis), 1
        while step < size:
            steps.append((axis, [(i, i ^ (2 * step - 1)) for i in range(size)]))
            step *= 2
    channels = stat.shape[1]
    found = []
    for at, (axis, pairs) in enumerate(steps):
        other = lax.ppermute(stat, axis, pairs)
        last = at == len(steps) - 1
        more = extra if last else ()
        stat = pl.pallas_call(
            functools.partial(kernel if last else merge_kernel, n),
            out_shape=shape((8 if last else 2, channels), F32),
            in_specs=[INV] * (2 + len(more) - (n_order if last else 0))
            + [ANY] * (n_order if last else 0),
            out_specs=INV,
            compiler_params=limit(1),
            cost_estimate=FREE,
            name="finish" if last else "merge",
        )(stat, other, *more)
        found.append(stat)
        n *= 2
    return found


def join_kernel(n, n_order, *refs):
    vecs, xs, w, refs = refs[:n], refs[n : 2 * n], refs[2 * n], refs[2 * n + 1 + n_order :]
    joined, send1, send2, wsend, *wsend1, sems = refs
    rows, width = xs[0].shape
    end = rows - HALO
    core, odd = lax.axis_index("dp"), lax.rem(lax.axis_index("seq"), 2)
    part = wsend.shape[0]
    quarter = lax.axis_index("groups") * 2 + core
    copies = [copy(w.at[0, pl.ds(pl.multiple_of(quarter * part, 16), part)], wsend, sems.at[0])]
    for k, dst in enumerate(wsend1):
        size = dst.shape[0]
        mine = pl.ds(pl.multiple_of(core * size, 16), size)
        src = w.at[1, mine, columns(-k - 1, n, width)]
        copies.append(copy(src, dst, sems.at[k + 1]))
    for c in copies:
        c.start()
    for k, (vec, x) in enumerate(zip(vecs, xs)):
        cols = columns(k, n, width)
        joined[:, cols] = vec[...]
        send1[:, cols] = x[pl.ds(pl.multiple_of((1 - odd) * end, HALO), HALO), :]
        send2[:, cols] = x[pl.ds(pl.multiple_of(odd * end, HALO), HALO), :]
    for c in copies:
        c.wait()


def join(vecs, xs, w_proj, order):
    n, width = len(vecs), vecs[0].shape[1]
    hidden, channels = w_proj.shape[1:]
    outs = [shape((8, channels), F32)] + [shape((HALO, channels), BF16)] * 2
    outs += [shape((hidden // 4, channels), BF16)]
    outs += [shape((hidden // 2, width), BF16)] * (n - 1)
    return pl.pallas_call(
        functools.partial(join_kernel, n, len(order)),
        out_shape=outs,
        in_specs=[INV] * (2 * n) + [ANY] * (1 + len(order)),
        out_specs=[INV] * 3 + [ANY] * n,
        scratch_shapes=[pltpu.SemaphoreType.DMA((n,))],
        compiler_params=limit(1),
        cost_estimate=FREE,
        name="join",
    )(*vecs, *xs, w_proj, *order)


def keep_kernel(lengths, dilations, out):
    rows = out.shape[1]
    first = lax.axis_index("seq") * rows
    ends, end = [], jnp.int32(0)
    for k in range(lengths.shape[1]):
        end = end + lengths[0, k]
        ends.append(end)

    def segment(place):
        count = jnp.where(place >= 0, 1, 0)
        for end in ends:
            count = count + jnp.where(place >= end, 1, 0)
        return count

    @pl.loop(0, rows // 32)
    def _(i):
        at = pl.multiple_of(i * 32, 32)
        place = first + at + lax.broadcasted_iota(jnp.int32, (32, 128), 0)
        here = segment(place)
        for layer in range(2):
            d = dilations[layer]
            for side, there in enumerate((place - d, place + d)):
                keep = jnp.where(segment(there) == here, 1.0, 0.0)
                out[2 * layer + side, pl.ds(at, 32), :] = keep


def keeps(lengths, dilations, rows):
    return pl.pallas_call(
        keep_kernel,
        out_shape=shape((4, rows, 128), F32),
        in_specs=[INS, INS],
        out_specs=INV,
        compiler_params=limit(4),
                cost_estimate=FREE,
                name="keeps",
    )(lengths, dilations)


def shifted(ref, start, count):
    base = pl.multiple_of((start // 8) * 8, 8)
    tall = ref[pl.ds(base, count + 8), :]
    return pltpu.roll(tall, (count + 8 - (start - base)) % (count + 8), 0)[:count]


def stage_kernel(w, *rest):
    layers, taps, _, width = w.shape
    outs, bufs, sems = rest[:layers], rest[layers:-1], rest[-1]
    step = outs[0].shape[1] // taps
    order = (0, 2, 1)
    copies = []
    for layer, out in enumerate(outs):
        for at, tap in enumerate(order):
            dst = bufs[0].at[layer, at] if bufs else out.at[:, pl.ds(at * step, width)]
            copies.append(copy(w.at[layer, tap], dst, sems.at[len(copies)]))
    run(copies)
    for buf in bufs:
        for layer, out in enumerate(outs):
            for at in range(taps):
                out[:, at * step : at * step + width] = buf[layer, at]


def stage(w_conv):
    layers, taps, channels, width = w_conv.shape
    step = -(-width // 128) * 128
    bufs = [] if step == width else [pltpu.VMEM(w_conv.shape, BF16)]
    return pl.pallas_call(
        stage_kernel,
        out_shape=[shape((channels, taps * step), BF16)] * layers,
        in_specs=[HBM],
        out_specs=[INV] * layers,
        scratch_shapes=bufs + [pltpu.SemaphoreType.DMA((layers * taps,))],
        compiler_params=limit(8 if bufs else 1),
        cost_estimate=FREE,
        name="stage",
    )(w_conv)


def conv_kernel(pieces, layer, segs, hand, n, n_src, n_order, dilations, stats, keep, w, *rest):
    srcs, (out, *kept, nbuf, p0, p2) = rest[:n_src], rest[n_src + n_order :]
    ext, width = nbuf.shape[0], out.shape[1]
    for src, at, count, to, back, raw in pieces:
        src = srcs[src]
        cols = slice(None) if back is None else columns(back, n, src.shape[1])
        if isinstance(to, tuple):
            odd = lax.rem(lax.axis_index("seq"), 2)
            to = pl.multiple_of(to[0] + odd * (to[1] - to[0]), HALO)
        if not raw:
            nbuf[to : to + count, cols] = src[at : at + count, :]
            continue
        mean, scale, bias = stats[0:1, cols], stats[1:2, cols], stats[2:3, cols]
        block = 128 if count % 128 == 0 else 64

        @pl.loop(0, count // block)
        def _(i):
            rows = pl.multiple_of(i * block, block)
            v = src[pl.ds(at + rows, block), :].astype(F32)
            dst = pl.ds(pl.multiple_of(to + rows, HALO), block)
            nbuf[dst, cols] = gelu((v - mean) * scale + bias).astype(BF16)

    step = w.shape[1] // 3
    sides = dot(nbuf[...], w[:, : 2 * step])
    p0[0 : ext - HALO, :] = sides[: ext - HALO, :width]
    p2[0 : ext - HALO, :] = sides[HALO:, step : step + width]
    mid = dot(nbuf[HALO : ext - HALO, :], w[:, 2 * step : 2 * step + width])
    d = dilations[layer]
    to = 0
    for k, (first, count) in enumerate(segs):
        base = to + 2 * HALO * k
        for r in range(0, count, HALO):
            left = shifted(p0, base + r + HALO - d, HALO)
            right = shifted(p2, base + r + d, HALO)
            here = slice(first + r, first + r + HALO)
            for c in range(0, width, 128):
                wide = min(128, width - c)
                cs = slice(c, c + wide)
                kl, kr = keep[2 * layer, here, :wide] > 0, keep[2 * layer + 1, here, :wide] > 0
                mixed = jnp.where(kl, left[:, cs], 0.0) + jnp.where(kr, right[:, cs], 0.0)
                mixed = mid[base + r : base + r + HALO, cs] + mixed
                out[to + r : to + r + HALO, cs] = gelu(mixed).astype(BF16)
        to += count
    for ref in kept:
        ref[...] = nbuf[hand : hand + 2 * HALO, :]


def conv(pieces, srcs, n, layer, segs, dilations, stats, keep, w, width, order, hand=None):
    channels = w.shape[0]
    rows = sum(count for _, count in segs)
    ext = rows + 2 * HALO * len(segs)
    outs = [shape((rows, width), BF16)]
    outs += [shape((2 * HALO, channels), BF16)] * int(hand is not None)
    cost = pl.CostEstimate(flops=0, transcendentals=0, bytes_accessed=24 << 20)
    return pl.pallas_call(
        functools.partial(conv_kernel, pieces, layer, segs, hand, n, len(srcs), len(order)),
        out_shape=outs,
        in_specs=[INS] + [INV] * (3 + len(srcs)) + [ANY] * len(order),
        out_specs=[INV] * len(outs),
        scratch_shapes=[
            pltpu.VMEM((ext, channels), BF16),
            pltpu.VMEM((ext - HALO + 8, width), F32),
            pltpu.VMEM((ext - HALO + 8, width), F32),
        ],
        compiler_params=limit(10),
        cost_estimate=cost,
        name=f"conv{layer}_{segs[0][0]}",
    )(dilations, stats, keep, w, *srcs, *order)


def weight_copies(sends, wbuf, sems):
    copies = []
    for k, parts in enumerate(sends):
        size = parts[0][0].shape[0]
        for src, at in parts:
            dst = wbuf.at[k, pl.ds(pl.multiple_of(at * size, 16), size), :]
            copies.append(copy(src, dst, sems.at[len(copies)]))
    return copies


def quarters(refs):
    group, core = lax.axis_index("groups"), lax.axis_index("dp")
    ats = (2 * group + core, 2 * (1 - group) + core, 2 * group + 1 - core, 3 - 2 * group - core)
    return [list(zip(refs[i : i + 4], ats)) for i in range(0, len(refs), 4)]


def halves(refs):
    core = lax.axis_index("dp")
    return [list(zip(refs[i : i + 2], (core, 1 - core))) for i in range(0, len(refs), 2)]


def update_of(inners, w, layer, cols, wbuf, others):
    total = dot(inners[0][...], w[layer, :, cols]).astype(BF16).astype(F32)
    for k, inner in enumerate(inners[1:]):
        total = total + dot(inner[...], wbuf[k, :, others]).astype(BF16).astype(F32)
    return total


def proj0_kernel(n, runs, *rest):
    chunks = [rest[i * n : (i + 1) * n] for i in range(len(runs))]
    rest = rest[len(runs) * n :]
    w, sends, rest = rest[0], rest[1 : 4 * n - 3], rest[4 * n - 3 :]
    xs, (mid, low, high, send1, send2, stat, wbuf, wsems) = rest[:n], rest[n:]
    rows, width = xs[0].shape
    end = rows - HALO
    run(weight_copies(quarters(sends), wbuf, wsems))
    even = lax.rem(lax.axis_index("seq"), 2) == 0
    for k, x in enumerate(xs):
        for col in range(0, width, 256):
            wide = min(256, width - col)
            here = slice(col, col + wide)
            cs = pl.ds(pl.multiple_of(side_of(k, n) * width + col, 128), wide)
            pivot, edge = None, {}
            for chunk, spans in zip(chunks, runs):
                update = update_of(chunk, w, 0, cs, wbuf, cs)
                at = 0
                for first, count in spans:
                    new = x[first : first + count, here].astype(F32) + update[at : at + count]
                    new = new.astype(BF16)
                    v = new.astype(F32)
                    if first in (0, end):
                        edge[first] = v
                        (high if first else low)[:, cs] = new
                    else:
                        mid[first - HALO : first - HALO + count, cs] = new
                    if pivot is None:
                        pivot = jnp.mean(v[0:8], axis=0, keepdims=True)
                        s1 = s2 = jnp.zeros((8, wide), F32)
                    t1, t2 = sums_about(v, pivot)
                    s1, s2 = s1 + t1, s2 + t2
                    at += count
            send1[:, cs] = jnp.where(even, edge[end], edge[0]).astype(BF16)
            send2[:, cs] = jnp.where(even, edge[0], edge[end]).astype(BF16)
            stat[0:1, cs], stat[1:2, cs] = spread_of(pivot, s1, s2, rows)


def proj0(runs, inners, w_proj, sends, xs):
    hidden, channels = w_proj.shape[1:]
    n = len(xs)
    rows = xs[0].shape[0]
    outs = [shape((rows - 2 * HALO, channels), BF16)]
    outs += [shape((HALO, channels), BF16)] * 4 + [shape((2, channels), F32)]
    return pl.pallas_call(
        functools.partial(proj0_kernel, n, runs),
        out_shape=outs,
        in_specs=[INV] * (len(runs) * n + 1) + [ANY] * len(sends) + [INV] * n,
        out_specs=[INV] * 6,
        scratch_shapes=[
            pltpu.VMEM((n - 1, hidden, channels), BF16),
            pltpu.SemaphoreType.DMA((4 * n - 4,)),
        ],
        compiler_params=limit(8),
        cost_estimate=FREE,
        name="proj0",
    )(*[x for chunk in inners for x in chunk], w_proj, *sends, *xs)


def proj1_kernel(runs, n, n_src, last, *rest):
    inners, w, sends, rest = rest[:n], rest[n], rest[n + 1 : 3 * n - 1], rest[3 * n - 1 :]
    srcs, (out, obuf, wbuf, sems, wsems) = rest[:n_src], rest[n_src + int(last) :]
    width = obuf.shape[1]
    run(weight_copies(halves(sends), wbuf, wsems))
    for col in range(0, width, 256):
        wide = min(256, width - col)
        here = slice(col, col + wide)
        cs = pl.ds(pl.multiple_of(side_of(0, n) * width + col, 128), wide)
        update = update_of(inners, w, 1, cs, wbuf, here)
        at = 0
        for (_, count, skip), src in zip(runs, srcs):
            new = src[skip : skip + count, cs].astype(F32) + update[at : at + count]
            obuf[at : at + count, here] = new.astype(BF16)
            at += count
    at, outs = 0, []
    for k, (first, count, _) in enumerate(runs):
        outs.append(copy(obuf.at[pl.ds(at, count)], out.at[pl.ds(first, count)], sems.at[k]))
        at += count
    run(outs)


def proj1(runs, total, inners, w_proj, sends, srcs, before=None):
    hidden, channels = w_proj.shape[1:]
    n = len(inners)
    width = channels // n
    rows = sum(count for _, count, _ in runs)
    last = before is not None
    extra = [before] if last else []
    return pl.pallas_call(
        functools.partial(proj1_kernel, runs, n, len(srcs), last),
        out_shape=shape((total, width), BF16),
        in_specs=[INV] * (n + 1)
        + [ANY] * len(sends)
        + [INV] * len(srcs)
        + [HBM] * len(extra),
        out_specs=HBM,
        scratch_shapes=[
            pltpu.VMEM((rows, width), BF16),
            pltpu.VMEM((n - 1, hidden, width), BF16),
            pltpu.SemaphoreType.DMA((len(runs),)),
            pltpu.SemaphoreType.DMA((2 * n - 2,)),
        ],
        input_output_aliases={n + 1 + len(sends) + len(srcs): 0} if last else {},
        compiler_params=limit(5),
        cost_estimate=FREE,
        name=f"proj1_{runs[0][0]}",
    )(*inners, w_proj, *sends, *srcs, *extra)


def on_device(signal, lengths, dilations, w_conv, w_proj, gains, biases):
    own = signal[0]
    rows = own.shape[0]
    width = w_conv.shape[3]
    end = rows - HALO
    n_seq, n = lax.axis_size("seq"), lax.axis_size("chan")
    pairs1 = [(i, i ^ 1) for i in range(n_seq)]
    pairs2 = [(i, i + 1 if i % 2 else i - 1) for i in range(1, n_seq - 1)]
    perm = lax.ppermute
    pinned = pltpu.with_memory_space_constraint
    tied = lax.optimization_barrier

    def others(value):
        return [perm(value, "chan", [(i, (i + k) % n) for i in range(n)]) for k in range(1, n)]

    sent = others(own)
    own = pinned(own, pltpu.VMEM)
    xs = [own] + [pinned(x, pltpu.VMEM) for x in sent]
    taps = [pinned(w, pltpu.VMEM) for w in stage(pinned(w_conv, pltpu.HBM))]
    keep = pinned(keeps(lengths, dilations, rows), pltpu.VMEM)
    found = batch_stats(pre(own), rows, finish0_kernel, (gains, biases, keep), 1)
    w_proj = pinned(w_proj, pltpu.VMEM)
    vecs = [found[-1]] + others(found[-1])
    joined, send1, send2, wsend, *wsend1 = join(vecs, xs, w_proj, taps)
    sent = others(wsend)

    half = rows // 2
    runs = (((HALO, half - HALO),), ((half, half - HALO),), ((0, HALO), (end, HALO)))
    at1, at2 = (5 * HALO, 0), (0, 5 * HALO)

    def inner_rows(layer, chunk, pieces, srcs, stats, *order):
        hand = chunk * (half - HALO)
        return conv(
            pieces,
            srcs,
            n,
            layer,
            runs[chunk],
            dilations,
            stats,
            keep,
            taps[layer],
            width,
            order,
            hand,
        )

    def edge_rows(layer, kept, halos, stats, *order):
        pieces = [(0, 0, 2 * HALO, HALO, None, False), (1, 0, 2 * HALO, 3 * HALO, None, False)]
        srcs = list(kept)
        for halo, at in zip(halos, (at1, at2)):
            pieces += [(len(srcs), 0, HALO, at, None, True)]
            srcs += [halo]
        return conv(
            pieces, srcs, n, layer, runs[2], dilations, stats, keep, taps[layer], width, order
        )[0]

    tall = half + HALO
    pieces_a = [(k, 0, tall, 0, k, True) for k in range(n)]
    pieces_b = [(k, half - HALO, tall, 0, k, True) for k in range(n)]
    inner_a, kept_a = inner_rows(0, 0, pieces_a, xs, joined)
    send1, send2, sent, inner_a = tied((send1, send2, sent, inner_a))
    halos = perm(send1, "seq", pairs1), perm(send2, "seq", pairs2)
    swapped = [perm(w, "groups", SWAP) for w in sent]
    others_a = others(inner_a)
    inner_b, kept_b = inner_rows(0, 1, pieces_b, xs, joined, kept_a)
    inner_c = edge_rows(0, (kept_a, kept_b), halos, joined, *others_a)
    sends0 = []
    for w, w2 in zip(sent, swapped):
        sends0 += [w, w2, perm(w, "dp", SWAP), perm(w2, "dp", SWAP)]
    inners = [[inner_a] + others_a] + [[inner] + others(inner) for inner in (inner_b, inner_c)]
    mid, low, high, send1, send2, stat = proj0(runs, inners, w_proj, sends0, xs)
    found = batch_stats(stat, rows, finish1_kernel, (joined,), 0)
    stats1 = found[-1]
    wsend1, _ = tied((wsend1, found[0]))
    sends1 = []
    for k, w in enumerate(wsend1):
        w = perm(w, "chan", [(i, (i + k + 1) % n) for i in range(n)])
        sends1 += [w, perm(w, "dp", SWAP)]
    send1, send2, _ = tied((send1, send2, stats1))
    halos = perm(send1, "seq", pairs1), perm(send2, "seq", pairs2)

    pieces_a = ((0, 0, HALO, 0, None, True), (1, 0, half, HALO, None, True))
    pieces_b = (
        (1, half - 2 * HALO, half, 0, None, True),
        (2, 0, HALO, half, None, True),
    )
    inner_a, kept_a = inner_rows(1, 0, pieces_a, (low, mid), stats1)
    inner_b, kept_b = inner_rows(1, 1, pieces_b, (low, mid, high), stats1, kept_a)
    inner_c = edge_rows(1, (kept_a, kept_b), halos, stats1)
    inners = [[inner] + others(inner) for inner in (inner_a, inner_b, inner_c)]
    out = proj1(((HALO, half - HALO, 0),), rows, inners[0], w_proj, sends1, (mid,))
    out = proj1(((half, half - HALO, half - HALO),), rows, inners[1], w_proj, sends1, (mid,), out)
    ends = ((0, HALO, 0), (end, HALO, 0))
    return proj1(ends, rows, inners[2], w_proj, sends1, (low, high), out)[None]


def solution(mesh):
    placed = (
        P(("groups", "dp"), "seq", "chan"),
        P(("groups", "dp"), None),
        P(),
        P(None, None, None, "chan"),
        P(None, "chan", None),
        P(None, "chan"),
        P(None, "chan"),
    )
    return jax.shard_map(
        on_device,
        mesh=mesh,
        in_specs=placed,
        out_specs=P(("groups", "dp"), "seq", "chan"),
        check_vma=False,
    )
```

time: 103 us -> 91.2 us (0.89)
  Pallas kernels: 37.9 us -> 31.3 us
  waiting for transfers between devices: 32.6 us -> 27 us
    pallas_call x6 -> x9, Pallas kernels: 29.5 us -> 24.4 us  [the longest x6 18 us: conv(): pl.pallas_call(functools.partial(conv_kernel, pieces, layer, segs, hand,...]
    ppermute x12 -> x14, waiting for transfers between devices: 20.1 us -> 15.5 us  [the longest x9 15.5 us: others(): perm(value, 'chan', [(i, (i + k) % n) for i in range(n)])]
    ppermute x12 -> x14, starting transfers between devices: 20.3 us -> 22.5 us  [the longest x4 11.9 us: on_device(): halos = (perm(send1, 'seq', pairs1), perm(send2, 'seq', pairs2))]
    pallas_call x2 -> x3, Pallas kernels: 5.71 us -> 4.21 us  [proj1(): pl.pallas_call(functools.partial(proj1_kernel, runs, n, len(srcs), last),...]
    ppermute x6, starting transfers between devices: 4.85 us -> 3.77 us  [batch_stats(): other = lax.ppermute(stat, axis, pairs)]
    unnamed x14 -> x16, local copies, waits for them, and re-layouts: 3.93 us -> 3.94 us
  transfers between devices with their start and end apart: 22 -> 24, of which waited for: 13 -> 10; matrix products, arithmetic and copies ran while one was open for 0% -> 0% of each run, Pallas kernels for 30% -> 30%
where the time goes in v4:
time: 91.2 us; the launch traced here: 90.9 us
  Pallas kernels  31.3 us (34%)
  starting transfers between devices  28.3 us (31%)
  waiting for transfers between devices  27 us (30%)
  local copies, waits for them, and re-layouts  3.94 us (4%)
    pallas_call x6, Pallas kernels, conv(): pl.pallas_call(functools.partial(conv_kernel, pieces, layer, segs, hand,...  18 us
    ppermute x9, waiting for transfers between devices, others(): perm(value, 'chan', [(i, (i + k) % n) for i in range(n)])  15.5 us
    ppermute x4, starting transfers between devices, on_device(): halos = (perm(send1, 'seq', pairs1), perm(send2, 'seq', pairs2))  11.9 us
    ppermute x6, waiting for transfers between devices, batch_stats(): other = lax.ppermute(stat, axis, pairs)  11.5 us
    ppermute x9, starting transfers between devices, others(): perm(value, 'chan', [(i, (i + k) % n) for i in range(n)])  9.94 us
    pallas_call x3, Pallas kernels, proj1(): pl.pallas_call(functools.partial(proj1_kernel, runs, n, len(srcs), last),...  4.21 us
    unnamed x16, local copies, waits for them, and re-layouts  3.94 us
    ppermute x6, starting transfers between devices, batch_stats(): other = lax.ppermute(stat, axis, pairs)  3.77 us
  transfers between devices with their start and end apart: 24, of which 10 were waited for; matrix products, arithmetic and copies ran while one was open for 0% of the time, Pallas kernels for 30%

profile of v4, /device:TPU:8, one launch (start us, length us, event | category | flops | bytes accessed | tf_op | source)
XLA Modules:
  0.0 90.9 jit_solution(8640237405693446293)
XLA Ops:
  4.9 3.2 %collective-permute-done.1.b = f32[2,768]{1,0:T(2,128)S(1)} collective-permute-done((f32[2,768]{1,0:T(2,128)S(1)}, f32[2,768]{1,0:T(2,128)S(1)}, u32[]{:S(2)}, u32[]{:S(2)}) %collective-permute-start.1) | collective-permute-done | bytes 6176 | tf_op jit(solution)/shard_map/ppermute | solution.py:128
  8.1 1.6 %collective-permute-start.2 = (f32[2,768]{1,0:T(2,128)S(1)}, f32[2,768]{1,0:T(2,128)S(1)}, u32[]{:S(2)}, u32[]{:S(2)}) collective-permute-start(f32[2,768]{1,0:T(2,128)S(1)} %merge.5.a), channel_id=1, source_target_pairs={{0,12},{4,8},{8,4},{12,0},{1,13},{5,9},{9,5},{13,1},{2,14},{6,10},... | collective-permute-start | bytes 18440 | tf_op jit(solution)/shard_map/ppermute | solution.py:128
  11.0 2.2 %keeps.1._.keep = f32[4,640,128]{2,1,0:T(8,128)S(1)} custom-call(s32[1,8]{1,0:T(1,128)S(1)} %copy-done.7, s32[2]{0:T(128)S(1)} %copy-done.3), custom_call_target="tpu_custom_call" | custom-call | tf_op jit(solution)/shard_map/keeps/pallas_call | solution.py:216
  15.3 3.4 %stage.1 = (bf16[1536,1152]{1,0:T(8,128)(2,1)S(1)}, bf16[1536,1152]{1,0:T(8,128)(2,1)S(1)}) custom-call(bf16[2,3,1536,384]{3,2,1,0:T(8,128)(2,1)} %w.1), custom_call_target="tpu_custom_call" | custom-call | tf_op jit(solution)/shard_map/stage/pallas_call | solution.py:254
  18.7 5.5 %collective-permute-done.3.refs_1_ = f32[8,768]{1,0:T(8,128)S(1)} collective-permute-done((f32[8,768]{1,0:T(8,128)S(1)}, f32[8,768]{1,0:T(8,128)S(1)}, u32[]{:S(2)}, u32[]{:S(2)}) %collective-permute-start.3) | collective-permute-done | bytes 24608 | tf_op jit(solution)/shard_map/ppermute | solution.py:486
  24.4 1.6 %collective-permute-start.5 = (bf16[96,1536]{1,0:T(8,128)(2,1)S(1)}, bf16[96,1536]{1,0:T(8,128)(2,1)S(1)}, u32[]{:S(2)}, u32[]{:S(2)}) collective-permute-start(bf16[96,1536]{1,0:T(8,128)(2,1)S(1)} %get-tuple-element.37), channel_id=1, source_target_pairs={{0,2},{2,0},{1,3},{3,1},{4,6},{6,4},{5,7},{7,5},{8,10},{10,8},{9,1... | collective-permute-start | bytes 884744 | tf_op jit(solution)/shard_map/ppermute | solution.py:486
  26.0 3.5 %conv0_64.1 = (bf16[256,384]{1,0:T(8,128)(2,1)S(1)}, bf16[128,1536]{1,0:T(8,128)(2,1)S(1)}) custom-call(s32[2]{0:T(128)S(1)} %copy-done.4, f32[8,1536]{1,0:T(8,128)S(1)} %get-tuple-element.38.stats.joined, f32[4,640,128]{2,1,0:T(8,128)S(1)} %keeps.1._.keep, bf16[1536,1152]{1,0:T(8,128)(2,1)S(1)} %get-tuple-element.33.refs_5_.w, ...), custom_call_target="tpu_custom_call" | custom-call | bytes 25165824 | tf_op jit(solution)/shard_map/conv0_64/pallas_call | solution.py:320
  29.4 2.9 %collective-permute-done.5.rest_7_ = bf16[96,1536]{1,0:T(8,128)(2,1)S(1)} collective-permute-done((bf16[96,1536]{1,0:T(8,128)(2,1)S(1)}, bf16[96,1536]{1,0:T(8,128)(2,1)S(1)}, u32[]{:S(2)}, u32[]{:S(2)}) %collective-permute-start.5) | collective-permute-done | bytes 294944 | tf_op jit(solution)/shard_map/ppermute | solution.py:486
  32.4 1.5 %collective-permute-start.11 = (bf16[96,1536]{1,0:T(8,128)(2,1)S(1)}, bf16[96,1536]{1,0:T(8,128)(2,1)S(1)}, u32[]{:S(2)}, u32[]{:S(2)}) collective-permute-start(bf16[96,1536]{1,0:T(8,128)(2,1)S(1)} %collective-permute-done.5.rest_7_), channel_id=1, source_target_pairs={{0,16},{16,0},{1,17},{17,1},{2,18},{18,2},{3,19},{19,3},{4,20},{20... | collective-permute-start | bytes 884744 | tf_op jit(solution)/shard_map/ppermute | solution.py:536
  35.8 4.6 %collective-permute-start.9 = (bf16[64,1536]{1,0:T(8,128)(2,1)S(1)}, bf16[64,1536]{1,0:T(8,128)(2,1)S(1)}, u32[]{:S(2)}, u32[]{:S(2)}) collective-permute-start(bf16[64,1536]{1,0:T(8,128)(2,1)S(1)} %get-tuple-element.45), channel_id=1, source_target_pairs={{4,8},{8,4},{5,9},{9,5},{6,10},{10,6},{7,11},{11,7},{20,24},{24,20... | collective-permute-start | bytes 589832 | tf_op jit(solution)/shard_map/ppermute | solution.py:535
  41.0 3.5 %conv0_320.1 = (bf16[256,384]{1,0:T(8,128)(2,1)S(1)}, bf16[128,1536]{1,0:T(8,128)(2,1)S(1)}) custom-call(s32[2]{0:T(128)S(1)} %copy-done.4, f32[8,1536]{1,0:T(8,128)S(1)} %get-tuple-element.38.stats.joined, f32[4,640,128]{2,1,0:T(8,128)S(1)} %keeps.1._.keep, bf16[1536,1152]{1,0:T(8,128)(2,1)S(1)} %get-tuple-element.33.refs_5_.w, ...), custom_call_target="tpu_custom_call" | custom-call | bytes 25165824 | tf_op jit(solution)/shard_map/conv0_320/pallas_call | solution.py:320
  45.1 2.2 %conv0_0.1.rest_4_ = bf16[128,384]{1,0:T(8,128)(2,1)S(1)} custom-call(s32[2]{0:T(128)S(1)} %copy-done.4, f32[8,1536]{1,0:T(8,128)S(1)} %get-tuple-element.38.stats.joined, f32[4,640,128]{2,1,0:T(8,128)S(1)} %keeps.1._.keep, bf16[1536,1152]{1,0:T(8,128)(2,1)S(1)} %get-tuple-element.33.refs_5_.w, bf16[128,1536]{1,0:T(8,128)(2,1)S(1)} %get-tuple-element.41.rest_2_.rest_0_, ...), custom_call_target="tpu_custom_call" | custom-call | bytes 25165824 | tf_op jit(solution)/shard_map/conv0_0/pallas_call | solution.py:320
  47.3 1.6 %collective-permute-start.10 = (bf16[128,384]{1,0:T(8,128)(2,1)S(1)}, bf16[128,384]{1,0:T(8,128)(2,1)S(1)}, u32[]{:S(2)}, u32[]{:S(2)}) collective-permute-start(bf16[128,384]{1,0:T(8,128)(2,1)S(1)} %conv0_0.1.rest_4_), channel_id=1, source_target_pairs={{0,2},{2,0},{1,3},{3,1},{4,6},{6,4},{5,7},{7,5},{8,10},{10,8},{9,1... | collective-permute-start | bytes 294920 | tf_op jit(solution)/shard_map/ppermute | solution.py:486
  48.8 3.5 %collective-permute-done.7.rest_3_ = bf16[256,384]{1,0:T(8,128)(2,1)S(1)} collective-permute-done((bf16[256,384]{1,0:T(8,128)(2,1)S(1)}, bf16[256,384]{1,0:T(8,128)(2,1)S(1)}, u32[]{:S(2)}, u32[]{:S(2)}) %collective-permute-start.7) | collective-permute-done | bytes 196640 | tf_op jit(solution)/shard_map/ppermute | solution.py:486
  53.6 2.8 %proj0.1 = (bf16[512,1536]{1,0:T(8,128)(2,1)S(1)}, bf16[64,1536]{1,0:T(8,128)(2,1)S(1)}, bf16[64,1536]{1,0:T(8,128)(2,1)S(1)}, bf16[64,1536]{1,0:T(8,128)(2,1)S(...) custom-call(bf16[256,384]{1,0:T(8,128)(2,1)S(1)} %get-tuple-element.40.rest_0_, ...), custom_call_target="tpu_custom_call" | custom-call | tf_op jit(solution)/shard_map/proj0/pallas_call | solution.py:408
  58.4 3.6 %collective-permute-done.15.b = f32[2,1536]{1,0:T(2,128)S(1)} collective-permute-done((f32[2,1536]{1,0:T(2,128)S(1)}, f32[2,1536]{1,0:T(2,128)S(1)}, u32[]{:S(2)}, u32[]{:S(2)}) %collective-permute-start.15) | collective-permute-done | bytes 12320 | tf_op jit(solution)/shard_map/ppermute | solution.py:128
  63.3 2.4 %collective-permute-done.16.b = f32[2,1536]{1,0:T(2,128)S(1)} collective-permute-done((f32[2,1536]{1,0:T(2,128)S(1)}, f32[2,1536]{1,0:T(2,128)S(1)}, u32[]{:S(2)}, u32[]{:S(2)}) %collective-permute-start.16) | collective-permute-done | bytes 12320 | tf_op jit(solution)/shard_map/ppermute | solution.py:128
  65.7 2.0 %collective-permute-start.17 = (bf16[64,1536]{1,0:T(8,128)(2,1)S(1)}, bf16[64,1536]{1,0:T(8,128)(2,1)S(1)}, u32[]{:S(2)}, u32[]{:S(2)}) collective-permute-start(bf16[64,1536]{1,0:T(8,128)(2,1)S(1)} %get-tuple-element.55), channel_id=1, source_target_pairs={{0,4},{4,0},{8,12},{12,8},{1,5},{5,1},{9,13},{13,9},{2,6},{6,2},{1... | collective-permute-start | bytes 589832 | tf_op jit(solution)/shard_map/ppermute | solution.py:553
  67.8 4.9 %collective-permute-start.18 = (bf16[64,1536]{1,0:T(8,128)(2,1)S(1)}, bf16[64,1536]{1,0:T(8,128)(2,1)S(1)}, u32[]{:S(2)}, u32[]{:S(2)}) collective-permute-start(bf16[64,1536]{1,0:T(8,128)(2,1)S(1)} %get-tuple-element.56), channel_id=1, source_target_pairs={{4,8},{8,4},{5,9},{9,5},{6,10},{10,6},{7,11},{11,7},{20,24},{24,20... | collective-permute-start | bytes 589832 | tf_op jit(solution)/shard_map/ppermute | solution.py:553
  72.6 3.5 %conv1_64.1 = (bf16[256,384]{1,0:T(8,128)(2,1)S(1)}, bf16[128,1536]{1,0:T(8,128)(2,1)S(1)}) custom-call(s32[2]{0:T(128)S(1)} %copy-done.4, f32[8,1536]{1,0:T(8,128)S(1)} %finish.3.stats, f32[4,640,128]{2,1,0:T(8,128)S(1)} %keeps.1._.keep, bf16[1536,1152]{1,0:T(8,128)(2,1)S(1)} %get-tuple-element.34.refs_6_.w, ...), custom_call_target="tpu_custom_call" | custom-call | bytes 25165824 | tf_op jit(solution)/shard_map/conv1_64/pallas_call | solution.py:320
  76.6 3.3 %conv1_320.1 = (bf16[256,384]{1,0:T(8,128)(2,1)S(1)}, bf16[128,1536]{1,0:T(8,128)(2,1)S(1)}) custom-call(s32[2]{0:T(128)S(1)} %copy-done.4, f32[8,1536]{1,0:T(8,128)S(1)} %finish.3.stats, f32[4,640,128]{2,1,0:T(8,128)S(1)} %keeps.1._.keep, bf16[1536,1152]{1,0:T(8,128)(2,1)S(1)} %get-tuple-element.34.refs_6_.w, ...), custom_call_target="tpu_custom_call" | custom-call | bytes 25165824 | tf_op jit(solution)/shard_map/conv1_320/pallas_call | solution.py:320
  79.9 1.7 %collective-permute-start.22 = (bf16[256,384]{1,0:T(8,128)(2,1)S(1)}, bf16[256,384]{1,0:T(8,128)(2,1)S(1)}, u32[]{:S(2)}, u32[]{:S(2)}) collective-permute-start(bf16[256,384]{1,0:T(8,128)(2,1)S(1)} %get-tuple-element.59.rest_0_), channel_id=1, source_target_pairs={{0,2},{2,0},{1,3},{3,1},{4,6},{6,4},{5,7},{7,5},{8,10},{10,8},{9,1... | collective-permute-start | bytes 589832 | tf_op jit(solution)/shard_map/ppermute | solution.py:486
  81.6 2.2 %conv1_0.1.rest_0_ = bf16[128,384]{1,0:T(8,128)(2,1)S(1)} custom-call(s32[2]{0:T(128)S(1)} %copy-done.4, f32[8,1536]{1,0:T(8,128)S(1)} %finish.3.stats, f32[4,640,128]{2,1,0:T(8,128)S(1)} %keeps.1._.keep, bf16[1536,1152]{1,0:T(8,128)(2,1)S(1)} %get-tuple-element.34.refs_6_.w, bf16[128,1536]{1,0:T(8,128)(2,1)S(1)} %get-tuple-element.50.rest_3_.rest_0_, ...), custom_call_target="tpu_custom_call" | custom-call | bytes 25165824 | tf_op jit(solution)/shard_map/conv1_0/pallas_call | solution.py:320
  85.7 2.3 %collective-permute-done.22.rest_1_ = bf16[256,384]{1,0:T(8,128)(2,1)S(1)} collective-permute-done((bf16[256,384]{1,0:T(8,128)(2,1)S(1)}, bf16[256,384]{1,0:T(8,128)(2,1)S(1)}, u32[]{:S(2)}, u32[]{:S(2)}) %collective-permute-start.22) | collective-permute-done | bytes 196640 | tf_op jit(solution)/shard_map/ppermute | solution.py:486
  (60 shorter events, 21.3 us)
Async XLA Ops:
  0.0 24.2 %collective-permute-start.4 = (bf16[640,768]{1,0:T(8,128)(2,1)}, bf16[640,768]{1,0:T(8,128)(2,1)S(1)}, u32[]{:S(2)}, u32[]{:S(2)}) collective-permute-start(bf16[640,768]{1,0:T(8,128)(2,1)} %bitcast.2), channel_id=1, source_target_pairs={{0,2},{2,0},{1,3},{3,1},{4,6},{6,4},{5,7},{7,5},{8,10},{10,8},{9,1... | collective-permute-start | bytes 2949128 | tf_op jit(solution)/shard_map/ppermute | solution.py:486
  3.1 1.2 %collective-permute-start = (f32[2,768]{1,0:T(2,128)S(1)}, f32[2,768]{1,0:T(2,128)S(1)}, u32[]{:S(2)}, u32[]{:S(2)}) collective-permute-start(f32[2,768]{1,0:T(2,128)S(1)} %pre.1.a), channel_id=1, source_target_pairs={{0,1},{1,0},{2,3},{3,2},{4,5},{5,4},{6,7},{7,6},{8,9},{9,8},{10,11... | collective-permute-start | bytes 18440 | tf_op jit(solution)/shard_map/ppermute | solution.py:128
  4.4 3.7 %collective-permute-start.1 = (f32[2,768]{1,0:T(2,128)S(1)}, f32[2,768]{1,0:T(2,128)S(1)}, u32[]{:S(2)}, u32[]{:S(2)}) collective-permute-start(f32[2,768]{1,0:T(2,128)S(1)} %merge.4.a), channel_id=1, source_target_pairs={{0,4},{4,0},{8,12},{12,8},{1,5},{5,1},{9,13},{13,9},{2,6},{6,2},{1... | collective-permute-start | bytes 18440 | tf_op jit(solution)/shard_map/ppermute | solution.py:128
  8.1 5.2 %collective-permute-start.2 = (f32[2,768]{1,0:T(2,128)S(1)}, f32[2,768]{1,0:T(2,128)S(1)}, u32[]{:S(2)}, u32[]{:S(2)}) collective-permute-start(f32[2,768]{1,0:T(2,128)S(1)} %merge.5.a), channel_id=1, source_target_pairs={{0,12},{4,8},{8,4},{12,0},{1,13},{5,9},{9,5},{13,1},{2,14},{6,10},... | collective-permute-start | bytes 18440 | tf_op jit(solution)/shard_map/ppermute | solution.py:128
  14.7 9.5 %collective-permute-start.3 = (f32[8,768]{1,0:T(8,128)S(1)}, f32[8,768]{1,0:T(8,128)S(1)}, u32[]{:S(2)}, u32[]{:S(2)}) collective-permute-start(f32[8,768]{1,0:T(8,128)S(1)} %finish.2.refs_0_), channel_id=1, source_target_pairs={{0,2},{2,0},{1,3},{3,1},{4,6},{6,4},{5,7},{7,5},{8,10},{10,8},{9,1... | collective-permute-start | bytes 73736 | tf_op jit(solution)/shard_map/ppermute | solution.py:486
  24.4 7.9 %collective-permute-start.5 = (bf16[96,1536]{1,0:T(8,128)(2,1)S(1)}, bf16[96,1536]{1,0:T(8,128)(2,1)S(1)}, u32[]{:S(2)}, u32[]{:S(2)}) collective-permute-start(bf16[96,1536]{1,0:T(8,128)(2,1)S(1)} %get-tuple-element.37), channel_id=1, source_target_pairs={{0,2},{2,0},{1,3},{3,1},{4,6},{6,4},{5,7},{7,5},{8,10},{10,8},{9,1... | collective-permute-start | bytes 884744 | tf_op jit(solution)/shard_map/ppermute | solution.py:486
  32.4 8.2 %collective-permute-start.11 = (bf16[96,1536]{1,0:T(8,128)(2,1)S(1)}, bf16[96,1536]{1,0:T(8,128)(2,1)S(1)}, u32[]{:S(2)}, u32[]{:S(2)}) collective-permute-start(bf16[96,1536]{1,0:T(8,128)(2,1)S(1)} %collective-permute-done.5.rest_7_), channel_id=1, source_target_pairs={{0,16},{16,0},{1,17},{17,1},{2,18},{18,2},{3,19},{19,3},{4,20},{20... | collective-permute-start | bytes 884744 | tf_op jit(solution)/shard_map/ppermute | solution.py:536
  33.9 10.6 %collective-permute-start.6 = (bf16[256,384]{1,0:T(8,128)(2,1)S(1)}, bf16[256,384]{1,0:T(8,128)(2,1)S(1)}, u32[]{:S(2)}, u32[]{:S(2)}) collective-permute-start(bf16[256,384]{1,0:T(8,128)(2,1)S(1)} %get-tuple-element.40.rest_0_), channel_id=1, source_target_pairs={{0,2},{2,0},{1,3},{3,1},{4,6},{6,4},{5,7},{7,5},{8,10},{10,8},{9,1... | collective-permute-start | bytes 589832 | tf_op jit(solution)/shard_map/ppermute | solution.py:486
  35.4 9.7 %collective-permute-start.8 = (bf16[64,1536]{1,0:T(8,128)(2,1)S(1)}, bf16[64,1536]{1,0:T(8,128)(2,1)S(1)}, u32[]{:S(2)}, u32[]{:S(2)}) collective-permute-start(bf16[64,1536]{1,0:T(8,128)(2,1)S(1)} %get-tuple-element.44), channel_id=1, source_target_pairs={{0,4},{4,0},{8,12},{12,8},{1,5},{5,1},{9,13},{13,9},{2,6},{6,2},{1... | collective-permute-start | bytes 589832 | tf_op jit(solution)/shard_map/ppermute | solution.py:535
  35.8 9.3 %collective-permute-start.9 = (bf16[64,1536]{1,0:T(8,128)(2,1)S(1)}, bf16[64,1536]{1,0:T(8,128)(2,1)S(1)}, u32[]{:S(2)}, u32[]{:S(2)}) collective-permute-start(bf16[64,1536]{1,0:T(8,128)(2,1)S(1)} %get-tuple-element.45), channel_id=1, source_target_pairs={{4,8},{8,4},{5,9},{9,5},{6,10},{10,6},{7,11},{11,7},{20,24},{24,20... | collective-permute-start | bytes 589832 | tf_op jit(solution)/shard_map/ppermute | solution.py:535
  40.4 13.1 %collective-permute-start.12 = (bf16[96,1536]{1,0:T(8,128)(2,1)S(1)}, bf16[96,1536]{1,0:T(8,128)(2,1)S(1)}, u32[]{:S(2)}, u32[]{:S(2)}) collective-permute-start(bf16[96,1536]{1,0:T(8,128)(2,1)S(1)} %collective-permute-done.5.rest_7_), channel_id=1, source_target_pairs={{0,1},{1,0},{2,3},{3,2},{4,5},{5,4},{6,7},{7,6},{8,9},{9,8},{10,11... | collective-permute-start | bytes 884744 | tf_op jit(solution)/shard_map/ppermute | solution.py:542
  40.5 13.0 %collective-permute-start.13 = (bf16[96,1536]{1,0:T(8,128)(2,1)S(1)}, bf16[96,1536]{1,0:T(8,128)(2,1)S(1)}, u32[]{:S(2)}, u32[]{:S(2)}) collective-permute-start(bf16[96,1536]{1,0:T(8,128)(2,1)S(1)} %collective-permute-done.11.rest_8_), channel_id=1, source_target_pairs={{0,1},{1,0},{2,3},{3,2},{4,5},{5,4},{6,7},{7,6},{8,9},{9,8},{10,11... | collective-permute-start | bytes 884744 | tf_op jit(solution)/shard_map/ppermute | solution.py:542
  44.5 7.8 %collective-permute-start.7 = (bf16[256,384]{1,0:T(8,128)(2,1)S(1)}, bf16[256,384]{1,0:T(8,128)(2,1)S(1)}, u32[]{:S(2)}, u32[]{:S(2)}) collective-permute-start(bf16[256,384]{1,0:T(8,128)(2,1)S(1)} %get-tuple-element.42.rest_2_), channel_id=1, source_target_pairs={{0,2},{2,0},{1,3},{3,1},{4,6},{6,4},{5,7},{7,5},{8,10},{10,8},{9,1... | collective-permute-start | bytes 589832 | tf_op jit(solution)/shard_map/ppermute | solution.py:486
  47.3 6.3 %collective-permute-start.10 = (bf16[128,384]{1,0:T(8,128)(2,1)S(1)}, bf16[128,384]{1,0:T(8,128)(2,1)S(1)}, u32[]{:S(2)}, u32[]{:S(2)}) collective-permute-start(bf16[128,384]{1,0:T(8,128)(2,1)S(1)} %conv0_0.1.rest_4_), channel_id=1, source_target_pairs={{0,2},{2,0},{1,3},{3,1},{4,6},{6,4},{5,7},{7,5},{8,10},{10,8},{9,1... | collective-permute-start | bytes 294920 | tf_op jit(solution)/shard_map/ppermute | solution.py:486
  56.4 1.2 %collective-permute-start.14 = (f32[2,1536]{1,0:T(2,128)S(1)}, f32[2,1536]{1,0:T(2,128)S(1)}, u32[]{:S(2)}, u32[]{:S(2)}) collective-permute-start(f32[2,1536]{1,0:T(2,128)S(1)} %get-tuple-element.47.a), channel_id=1, source_target_pairs={{0,1},{1,0},{2,3},{3,2},{4,5},{5,4},{6,7},{7,6},{8,9},{9,8},{10,11... | collective-permute-start | bytes 36872 | tf_op jit(solution)/shard_map/ppermute | solution.py:128
  57.6 10.1 %collective-permute-start.20 = (bf16[192,768]{1,0:T(8,128)(2,1)S(1)}, bf16[192,768]{1,0:T(8,128)(2,1)S(1)}, u32[]{:S(2)}, u32[]{:S(2)}) collective-permute-start(bf16[192,768]{1,0:T(8,128)(2,1)S(1)} %get-tuple-element.58), channel_id=1, source_target_pairs={{0,2},{2,0},{1,3},{3,1},{4,6},{6,4},{5,7},{7,5},{8,10},{10,8},{9,1... | collective-permute-start | bytes 884744 | tf_op jit(solution)/shard_map/ppermute | solution.py:550
  58.3 3.7 %collective-permute-start.15 = (f32[2,1536]{1,0:T(2,128)S(1)}, f32[2,1536]{1,0:T(2,128)S(1)}, u32[]{:S(2)}, u32[]{:S(2)}) collective-permute-start(f32[2,1536]{1,0:T(2,128)S(1)} %merge.6.a), channel_id=1, source_target_pairs={{0,4},{4,0},{8,12},{12,8},{1,5},{5,1},{9,13},{13,9},{2,6},{6,2},{1... | collective-permute-start | bytes 36872 | tf_op jit(solution)/shard_map/ppermute | solution.py:128
  62.0 3.8 %collective-permute-start.16 = (f32[2,1536]{1,0:T(2,128)S(1)}, f32[2,1536]{1,0:T(2,128)S(1)}, u32[]{:S(2)}, u32[]{:S(2)}) collective-permute-start(f32[2,1536]{1,0:T(2,128)S(1)} %merge.7.a), channel_id=1, source_target_pairs={{0,12},{4,8},{8,4},{12,0},{1,13},{5,9},{9,5},{13,1},{2,14},{6,10},... | collective-permute-start | bytes 36872 | tf_op jit(solution)/shard_map/ppermute | solution.py:128
  65.7 15.8 %collective-permute-start.17 = (bf16[64,1536]{1,0:T(8,128)(2,1)S(1)}, bf16[64,1536]{1,0:T(8,128)(2,1)S(1)}, u32[]{:S(2)}, u32[]{:S(2)}) collective-permute-start(bf16[64,1536]{1,0:T(8,128)(2,1)S(1)} %get-tuple-element.55), channel_id=1, source_target_pairs={{0,4},{4,0},{8,12},{12,8},{1,5},{5,1},{9,13},{13,9},{2,6},{6,2},{1... | collective-permute-start | bytes 589832 | tf_op jit(solution)/shard_map/ppermute | solution.py:553
  67.8 16.5 %collective-permute-start.21 = (bf16[192,768]{1,0:T(8,128)(2,1)S(1)}, bf16[192,768]{1,0:T(8,128)(2,1)S(1)}, u32[]{:S(2)}, u32[]{:S(2)}) collective-permute-start(bf16[192,768]{1,0:T(8,128)(2,1)S(1)} %collective-permute-done.20.rest_3_), channel_id=1, source_target_pairs={{0,1},{1,0},{2,3},{3,2},{4,5},{5,4},{6,7},{7,6},{8,9},{9,8},{10,11... | collective-permute-start | bytes 884744 | tf_op jit(solution)/shard_map/ppermute | solution.py:551
  67.8 13.8 %collective-permute-start.18 = (bf16[64,1536]{1,0:T(8,128)(2,1)S(1)}, bf16[64,1536]{1,0:T(8,128)(2,1)S(1)}, u32[]{:S(2)}, u32[]{:S(2)}) collective-permute-start(bf16[64,1536]{1,0:T(8,128)(2,1)S(1)} %get-tuple-element.56), channel_id=1, source_target_pairs={{4,8},{8,4},{5,9},{9,5},{6,10},{10,6},{7,11},{11,7},{20,24},{24,20... | collective-permute-start | bytes 589832 | tf_op jit(solution)/shard_map/ppermute | solution.py:553
  76.1 8.1 %collective-permute-start.23 = (bf16[256,384]{1,0:T(8,128)(2,1)S(1)}, bf16[256,384]{1,0:T(8,128)(2,1)S(1)}, u32[]{:S(2)}, u32[]{:S(2)}) collective-permute-start(bf16[256,384]{1,0:T(8,128)(2,1)S(1)} %get-tuple-element.60.rest_0_), channel_id=1, source_target_pairs={{0,2},{2,0},{1,3},{3,1},{4,6},{6,4},{5,7},{7,5},{8,10},{10,8},{9,1... | collective-permute-start | bytes 589832 | tf_op jit(solution)/shard_map/ppermute | solution.py:486
  79.9 8.1 %collective-permute-start.22 = (bf16[256,384]{1,0:T(8,128)(2,1)S(1)}, bf16[256,384]{1,0:T(8,128)(2,1)S(1)}, u32[]{:S(2)}, u32[]{:S(2)}) collective-permute-start(bf16[256,384]{1,0:T(8,128)(2,1)S(1)} %get-tuple-element.59.rest_0_), channel_id=1, source_target_pairs={{0,2},{2,0},{1,3},{3,1},{4,6},{6,4},{5,7},{7,5},{8,10},{10,8},{9,1... | collective-permute-start | bytes 589832 | tf_op jit(solution)/shard_map/ppermute | solution.py:486
  83.8 5.8 %collective-permute-start.19 = (bf16[128,384]{1,0:T(8,128)(2,1)S(1)}, bf16[128,384]{1,0:T(8,128)(2,1)S(1)}, u32[]{:S(2)}, u32[]{:S(2)}) collective-permute-start(bf16[128,384]{1,0:T(8,128)(2,1)S(1)} %conv1_0.1.rest_0_), channel_id=1, source_target_pairs={{0,2},{2,0},{1,3},{3,1},{4,6},{6,4},{5,7},{7,5},{8,10},{10,8},{9,1... | collective-permute-start | bytes 294920 | tf_op jit(solution)/shard_map/ppermute | solution.py:486
  (8 other events, 24.8 us)

commit v5 on v4

--- a/solution.py
+++ b/solution.py
@@ -144,46 +144,59 @@
 
 
 def join_kernel(n, n_order, *refs):
-    vecs, xs, w, refs = refs[:n], refs[n : 2 * n], refs[2 * n], refs[2 * n + 1 + n_order :]
-    joined, send1, send2, wsend, *wsend1, sems = refs
+    vecs, xs, (joined, send1, send2) = refs[:n], refs[n : 2 * n], refs[2 * n + n_order :]
     rows, width = xs[0].shape
     end = rows - HALO
-    core, odd = lax.axis_index("dp"), lax.rem(lax.axis_index("seq"), 2)
-    part = wsend.shape[0]
-    quarter = lax.axis_index("groups") * 2 + core
-    copies = [copy(w.at[0, pl.ds(pl.multiple_of(quarter * part, 16), part)], wsend, sems.at[0])]
-    for k, dst in enumerate(wsend1):
-        size = dst.shape[0]
-        mine = pl.ds(pl.multiple_of(core * size, 16), size)
-        src = w.at[1, mine, columns(-k - 1, n, width)]
-        copies.append(copy(src, dst, sems.at[k + 1]))
-    for c in copies:
-        c.start()
+    odd = lax.rem(lax.axis_index("seq"), 2)
     for k, (vec, x) in enumerate(zip(vecs, xs)):
         cols = columns(k, n, width)
         joined[:, cols] = vec[...]
         send1[:, cols] = x[pl.ds(pl.multiple_of((1 - odd) * end, HALO), HALO), :]
         send2[:, cols] = x[pl.ds(pl.multiple_of(odd * end, HALO), HALO), :]
-    for c in copies:
-        c.wait()
-
-
-def join(vecs, xs, w_proj, order):
+
+
+def join(vecs, xs, order):
     n, width = len(vecs), vecs[0].shape[1]
-    hidden, channels = w_proj.shape[1:]
-    outs = [shape((8, channels), F32)] + [shape((HALO, channels), BF16)] * 2
-    outs += [shape((hidden // 4, channels), BF16)]
-    outs += [shape((hidden // 2, width), BF16)] * (n - 1)
+    outs = [shape((8, n * width), F32)] + [shape((HALO, n * width), BF16)] * 2
     return pl.pallas_call(
         functools.partial(join_kernel, n, len(order)),
         out_shape=outs,
-        in_specs=[INV] * (2 * n) + [ANY] * (1 + len(order)),
-        out_specs=[INV] * 3 + [ANY] * n,
+        in_specs=[INV] * (2 * n) + [ANY] * len(order),
+        out_specs=[INV] * 3,
+        compiler_params=limit(1),
+        cost_estimate=FREE,
+        name="join",
+    )(*vecs, *xs, *order)
+
+
+def cut_kernel(n, w, _, wsend, *rest):
+    wsend1, sems = rest[:-1], rest[-1]
+    core = lax.axis_index("dp")
+    part = wsend.shape[0]
+    quarter = lax.axis_index("groups") * 2 + core
+    copies = [copy(w.at[0, pl.ds(pl.multiple_of(quarter * part, 16), part)], wsend, sems.at[0])]
+    for k, dst in enumerate(wsend1):
+        size, width = dst.shape
+        mine = pl.ds(pl.multiple_of(core * size, 16), size)
+        src = w.at[1, mine, columns(-k - 1, n, width)]
+        copies.append(copy(src, dst, sems.at[k + 1]))
+    run(copies)
+
+
+def cut(w_proj, n, order):
+    hidden, channels = w_proj.shape[1:]
+    outs = [shape((hidden // 4, channels), BF16)]
+    outs += [shape((hidden // 2, channels // n), BF16)] * (n - 1)
+    return pl.pallas_call(
+        functools.partial(cut_kernel, n),
+        out_shape=outs,
+        in_specs=[ANY, ANY],
+        out_specs=[ANY] * n,
         scratch_shapes=[pltpu.SemaphoreType.DMA((n,))],
         compiler_params=limit(1),
         cost_estimate=FREE,
-        name="join",
-    )(*vecs, *xs, w_proj, *order)
+        name="cut",
+    )(w_proj, order)
 
 
 def keep_kernel(lengths, dilations, out):
@@ -278,10 +291,8 @@
         mean, scale, bias = stats[0:1, cols], stats[1:2, cols], stats[2:3, cols]
         block = 128 if count % 128 == 0 else 64
 
-        @pl.loop(0, count // block)
-        def _(i):
-            rows = pl.multiple_of(i * block, block)
-            v = src[pl.ds(at + rows, block), :].astype(F32)
+        for rows in range(0, count, block):
+            v = src[at + rows : at + rows + block, :].astype(F32)
             dst = pl.ds(pl.multiple_of(to + rows, HALO), block)
             nbuf[dst, cols] = gelu((v - mean) * scale + bias).astype(BF16)
 
@@ -492,9 +503,16 @@
     keep = pinned(keeps(lengths, dilations, rows), pltpu.VMEM)
     found = batch_stats(pre(own), rows, finish0_kernel, (gains, biases, keep), 1)
     w_proj = pinned(w_proj, pltpu.VMEM)
-    vecs = [found[-1]] + others(found[-1])
-    joined, send1, send2, wsend, *wsend1 = join(vecs, xs, w_proj, taps)
+    vecs = [found[-1]]
+    for k in range(1, n):
+        pairs = []
+        for z in range(n_seq):
+            for c in range(n):
+                pairs.append((z * n + c, (z ^ 1) * n + (c + k) % n))
+        vecs.append(perm(found[-1], ("seq", "chan"), pairs))
+    wsend, *wsend1 = cut(w_proj, n, found[-1])
     sent = others(wsend)
+    joined, send1, send2 = join(vecs, xs, taps)
 
     half = rows // 2
     runs = (((HALO, half - HALO),), ((half, half - HALO),), ((0, HALO), (end, HALO)))
@@ -536,6 +554,7 @@
     swapped = [perm(w, "groups", SWAP) for w in sent]
     others_a = others(inner_a)
     inner_b, kept_b = inner_rows(0, 1, pieces_b, xs, joined, kept_a)
+    swapped, inner_b = tied((swapped, inner_b))
     inner_c = edge_rows(0, (kept_a, kept_b), halos, joined, *others_a)
     sends0 = []
     for w, w2 in zip(sent, swapped):

time: 91.2 us -> 86.6 us (0.950)
  Pallas kernels: 31.3 us -> 29.1 us
  waiting for transfers between devices: 27 us -> 25.4 us
  starting transfers between devices: 28.3 us -> 26.9 us
    ppermute x0 -> x1, starting transfers between devices: none -> 3.26 us  [on_device(): vecs.append(perm(found[-1], ('seq', 'chan'), pairs))]
    ppermute x4, starting transfers between devices: 11.9 us -> 8.81 us  [on_device(): halos = (perm(send1, 'seq', pairs1), perm(send2, 'seq', pairs2))]
    ppermute x9 -> x8, waiting for transfers between devices: 15.5 us -> 12.6 us  [others(): perm(value, 'chan', [(i, (i + k) % n) for i in range(n)])]
    pallas_call x6, Pallas kernels: 18 us -> 16.1 us  [conv(): pl.pallas_call(functools.partial(conv_kernel, pieces, layer, segs, hand,...]
    ppermute x9 -> x8, starting transfers between devices: 9.94 us -> 8.63 us  [others(): perm(value, 'chan', [(i, (i + k) % n) for i in range(n)])]
    ppermute x4, waiting for transfers between devices: 0.01 us -> 1.22 us  [on_device(): halos = (perm(send1, 'seq', pairs1), perm(send2, 'seq', pairs2))]
  transfers between devices with their start and end apart: 24 -> 24, of which waited for: 10 -> 11; matrix products, arithmetic and copies ran while one was open for 0% -> 0% of each run, Pallas kernels for 30% -> 29%
where the time goes in v5:
time: 86.6 us; the launch traced here: 86.3 us
  Pallas kernels  29.1 us (34%)
  starting transfers between devices  26.9 us (31%)
  waiting for transfers between devices  25.4 us (29%)
  local copies, waits for them, and re-layouts  4.55 us (5%)
    pallas_call x6, Pallas kernels, conv(): pl.pallas_call(functools.partial(conv_kernel, pieces, layer, segs, hand,...  16.1 us
    ppermute x8, waiting for transfers between devices, others(): perm(value, 'chan', [(i, (i + k) % n) for i in range(n)])  12.6 us
    ppermute x6, waiting for transfers between devices, batch_stats(): other = lax.ppermute(stat, axis, pairs)  11.5 us
    ppermute x4, starting transfers between devices, on_device(): halos = (perm(send1, 'seq', pairs1), perm(send2, 'seq', pairs2))  8.81 us
    ppermute x8, starting transfers between devices, others(): perm(value, 'chan', [(i, (i + k) % n) for i in range(n)])  8.63 us
    unnamed x16, local copies, waits for them, and re-layouts  4.55 us
    pallas_call x3, Pallas kernels, proj1(): pl.pallas_call(functools.partial(proj1_kernel, runs, n, len(srcs), last),...  4.22 us
    ppermute x6, starting transfers between devices, batch_stats(): other = lax.ppermute(stat, axis, pairs)  3.77 us
  transfers between devices with their start and end apart: 24, of which 11 were waited for; matrix products, arithmetic and copies ran while one was open for 0% of the time, Pallas kernels for 29%

profile of v5, /device:TPU:8, one launch (start us, length us, event | category | flops | bytes accessed | tf_op | source)
XLA Modules:
  0.0 86.3 jit_solution(17840759575254531342)
XLA Ops:
  0.0 1.5 %collective-permute-start.4 = (bf16[640,768]{1,0:T(8,128)(2,1)}, bf16[640,768]{1,0:T(8,128)(2,1)S(1)}, u32[]{:S(2)}, u32[]{:S(2)}) collective-permute-start(bf16[640,768]{1,0:T(8,128)(2,1)} %bitcast.2), channel_id=1, source_target_pairs={{0,2},{2,0},{1,3},{3,1},{4,6},{6,4},{5,7},{7,5},{8,10},{10,8},{9,1... | collective-permute-start | bytes 2949128 | tf_op jit(solution)/shard_map/ppermute | solution.py:497
  4.9 3.2 %collective-permute-done.1.b = f32[2,768]{1,0:T(2,128)S(1)} collective-permute-done((f32[2,768]{1,0:T(2,128)S(1)}, f32[2,768]{1,0:T(2,128)S(1)}, u32[]{:S(2)}, u32[]{:S(2)}) %collective-permute-start.1) | collective-permute-done | bytes 6176 | tf_op jit(solution)/shard_map/ppermute | solution.py:128
  8.1 1.6 %collective-permute-start.2 = (f32[2,768]{1,0:T(2,128)S(1)}, f32[2,768]{1,0:T(2,128)S(1)}, u32[]{:S(2)}, u32[]{:S(2)}) collective-permute-start(f32[2,768]{1,0:T(2,128)S(1)} %merge.5.a), channel_id=1, source_target_pairs={{0,12},{4,8},{8,4},{12,0},{1,13},{5,9},{9,5},{13,1},{2,14},{6,10},... | collective-permute-start | bytes 18440 | tf_op jit(solution)/shard_map/ppermute | solution.py:128
  11.0 2.2 %keeps.1._.keep = f32[4,640,128]{2,1,0:T(8,128)S(1)} custom-call(s32[1,8]{1,0:T(1,128)S(1)} %copy-done.7, s32[2]{0:T(128)S(1)} %copy-done.3), custom_call_target="tpu_custom_call" | custom-call | tf_op jit(solution)/shard_map/keeps/pallas_call | solution.py:229
  15.6 3.3 %collective-permute-start.3 = (f32[8,768]{1,0:T(8,128)S(1)}, f32[8,768]{1,0:T(8,128)S(1)}, u32[]{:S(2)}, u32[]{:S(2)}) collective-permute-start(f32[8,768]{1,0:T(8,128)S(1)} %finish.2.refs_0_._), channel_id=1, source_target_pairs={{0,6},{2,4},{4,2},{6,0},{8,14},{10,12},{12,10},{14,8},{1,7},{3,5},... | collective-permute-start | bytes 73736 | tf_op jit(solution)/shard_map/ppermute | solution.py:512
  18.8 3.1 %stage.1 = (bf16[1536,1152]{1,0:T(8,128)(2,1)S(1)}, bf16[1536,1152]{1,0:T(8,128)(2,1)S(1)}) custom-call(bf16[2,3,1536,384]{3,2,1,0:T(8,128)(2,1)} %w.2), custom_call_target="tpu_custom_call" | custom-call | tf_op jit(solution)/shard_map/stage/pallas_call | solution.py:267
  21.9 3.4 %collective-permute-done.4.refs_3_.rest_1_.rest_12_ = bf16[640,768]{1,0:T(8,128)(2,1)S(1)} collective-permute-done((bf16[640,768]{1,0:T(8,128)(2,1)}, bf16[640,768]{1,0:T(8,128)(2,1)S(1)}, u32[]{:S(2)}, u32[]{:S(2)}) %collective-permute-start.4) | collective-permute-done | bytes 983072 | tf_op jit(solution)/shard_map/ppermute | solution.py:497
  26.0 3.1 %conv0_64.1 = (bf16[256,384]{1,0:T(8,128)(2,1)S(1)}, bf16[128,1536]{1,0:T(8,128)(2,1)S(1)}) custom-call(s32[2]{0:T(128)S(1)} %copy-done.4, f32[8,1536]{1,0:T(8,128)S(1)} %get-tuple-element.40.stats.joined, f32[4,640,128]{2,1,0:T(8,128)S(1)} %keeps.1._.keep, bf16[1536,1152]{1,0:T(8,128)(2,1)S(1)} %get-tuple-element.35.refs_4_.w, ...), custom_call_target="tpu_custom_call" | custom-call | bytes 25165824 | tf_op jit(solution)/shard_map/conv0_64/pallas_call | solution.py:331
  30.6 1.5 %collective-permute-start.7 = (bf16[96,1536]{1,0:T(8,128)(2,1)S(1)}, bf16[96,1536]{1,0:T(8,128)(2,1)S(1)}, u32[]{:S(2)}, u32[]{:S(2)}) collective-permute-start(bf16[96,1536]{1,0:T(8,128)(2,1)S(1)} %collective-permute-done.5.rest_7_), channel_id=1, source_target_pairs={{0,16},{16,0},{1,17},{17,1},{2,18},{18,2},{3,19},{19,3},{4,20},{20... | collective-permute-start | bytes 884744 | tf_op jit(solution)/shard_map/ppermute | solution.py:554
  32.1 3.5 %collective-permute-start.10 = (bf16[64,1536]{1,0:T(8,128)(2,1)S(1)}, bf16[64,1536]{1,0:T(8,128)(2,1)S(1)}, u32[]{:S(2)}, u32[]{:S(2)}) collective-permute-start(bf16[64,1536]{1,0:T(8,128)(2,1)S(1)} %get-tuple-element.49), channel_id=1, source_target_pairs={{4,8},{8,4},{5,9},{9,5},{6,10},{10,6},{7,11},{11,7},{20,24},{24,20... | collective-permute-start | bytes 589832 | tf_op jit(solution)/shard_map/ppermute | solution.py:553
  35.6 1.6 %collective-permute-start.6 = (bf16[256,384]{1,0:T(8,128)(2,1)S(1)}, bf16[256,384]{1,0:T(8,128)(2,1)S(1)}, u32[]{:S(2)}, u32[]{:S(2)}) collective-permute-start(bf16[256,384]{1,0:T(8,128)(2,1)S(1)} %get-tuple-element.42.rest_0_), channel_id=1, source_target_pairs={{0,2},{2,0},{1,3},{3,1},{4,6},{6,4},{5,7},{7,5},{8,10},{10,8},{9,1... | collective-permute-start | bytes 589832 | tf_op jit(solution)/shard_map/ppermute | solution.py:497
  37.2 3.1 %conv0_320.1 = (bf16[256,384]{1,0:T(8,128)(2,1)S(1)}, bf16[128,1536]{1,0:T(8,128)(2,1)S(1)}) custom-call(s32[2]{0:T(128)S(1)} %copy-done.4, f32[8,1536]{1,0:T(8,128)S(1)} %get-tuple-element.40.stats.joined, f32[4,640,128]{2,1,0:T(8,128)S(1)} %keeps.1._.keep, bf16[1536,1152]{1,0:T(8,128)(2,1)S(1)} %get-tuple-element.35.refs_4_.w, ...), custom_call_target="tpu_custom_call" | custom-call | bytes 25165824 | tf_op jit(solution)/shard_map/conv0_320/pallas_call | solution.py:331
  41.2 1.8 %collective-permute-done.6.rest_4_.rest_1_ = bf16[256,384]{1,0:T(8,128)(2,1)S(1)} collective-permute-done((bf16[256,384]{1,0:T(8,128)(2,1)S(1)}, bf16[256,384]{1,0:T(8,128)(2,1)S(1)}, u32[]{:S(2)}, u32[]{:S(2)}) %collective-permute-start.6) | collective-permute-done | bytes 196640 | tf_op jit(solution)/shard_map/ppermute | solution.py:497
  44.2 2.2 %conv0_0.1.rest_4_ = bf16[128,384]{1,0:T(8,128)(2,1)S(1)} custom-call(s32[2]{0:T(128)S(1)} %copy-done.4, f32[8,1536]{1,0:T(8,128)S(1)} %get-tuple-element.40.stats.joined, f32[4,640,128]{2,1,0:T(8,128)S(1)} %keeps.1._.keep, bf16[1536,1152]{1,0:T(8,128)(2,1)S(1)} %get-tuple-element.35.refs_4_.w, bf16[128,1536]{1,0:T(8,128)(2,1)S(1)} %get-tuple-element.44.rest_2_.rest_0_, ...), custom_call_target="tpu_custom_call" | custom-call | bytes 25165824 | tf_op jit(solution)/shard_map/conv0_0/pallas_call | solution.py:331
  46.9 4.1 %collective-permute-done.11.rest_5_ = bf16[128,384]{1,0:T(8,128)(2,1)S(1)} collective-permute-done((bf16[128,384]{1,0:T(8,128)(2,1)S(1)}, bf16[128,384]{1,0:T(8,128)(2,1)S(1)}, u32[]{:S(2)}, u32[]{:S(2)}) %collective-permute-start.11) | collective-permute-done | bytes 98336 | tf_op jit(solution)/shard_map/ppermute | solution.py:497
  51.0 2.8 %proj0.1 = (bf16[512,1536]{1,0:T(8,128)(2,1)S(1)}, bf16[64,1536]{1,0:T(8,128)(2,1)S(1)}, bf16[64,1536]{1,0:T(8,128)(2,1)S(1)}, bf16[64,1536]{1,0:T(8,128)(2,1)S(...) custom-call(bf16[256,384]{1,0:T(8,128)(2,1)S(1)} %get-tuple-element.42.rest_0_, ...), custom_call_target="tpu_custom_call" | custom-call | tf_op jit(solution)/shard_map/proj0/pallas_call | solution.py:419
  56.7 2.8 %collective-permute-done.15.b = f32[2,1536]{1,0:T(2,128)S(1)} collective-permute-done((f32[2,1536]{1,0:T(2,128)S(1)}, f32[2,1536]{1,0:T(2,128)S(1)}, u32[]{:S(2)}, u32[]{:S(2)}) %collective-permute-start.15) | collective-permute-done | bytes 12320 | tf_op jit(solution)/shard_map/ppermute | solution.py:128
  60.0 3.2 %collective-permute-done.16.b = f32[2,1536]{1,0:T(2,128)S(1)} collective-permute-done((f32[2,1536]{1,0:T(2,128)S(1)}, f32[2,1536]{1,0:T(2,128)S(1)}, u32[]{:S(2)}, u32[]{:S(2)}) %collective-permute-start.16) | collective-permute-done | bytes 12320 | tf_op jit(solution)/shard_map/ppermute | solution.py:128
  63.2 2.9 %collective-permute-start.17 = (bf16[64,1536]{1,0:T(8,128)(2,1)S(1)}, bf16[64,1536]{1,0:T(8,128)(2,1)S(1)}, u32[]{:S(2)}, u32[]{:S(2)}) collective-permute-start(bf16[64,1536]{1,0:T(8,128)(2,1)S(1)} %get-tuple-element.59), channel_id=1, source_target_pairs={{0,4},{4,0},{8,12},{12,8},{1,5},{5,1},{9,13},{13,9},{2,6},{6,2},{1... | collective-permute-start | bytes 589832 | tf_op jit(solution)/shard_map/ppermute | solution.py:572
  66.1 2.4 %collective-permute-start.18 = (bf16[64,1536]{1,0:T(8,128)(2,1)S(1)}, bf16[64,1536]{1,0:T(8,128)(2,1)S(1)}, u32[]{:S(2)}, u32[]{:S(2)}) collective-permute-start(bf16[64,1536]{1,0:T(8,128)(2,1)S(1)} %get-tuple-element.60), channel_id=1, source_target_pairs={{4,8},{8,4},{5,9},{9,5},{6,10},{10,6},{7,11},{11,7},{20,24},{24,20... | collective-permute-start | bytes 589832 | tf_op jit(solution)/shard_map/ppermute | solution.py:572
  68.6 2.8 %conv1_64.1 = (bf16[256,384]{1,0:T(8,128)(2,1)S(1)}, bf16[128,1536]{1,0:T(8,128)(2,1)S(1)}) custom-call(s32[2]{0:T(128)S(1)} %copy-done.4, f32[8,1536]{1,0:T(8,128)S(1)} %finish.3.stats, f32[4,640,128]{2,1,0:T(8,128)S(1)} %keeps.1._.keep, bf16[1536,1152]{1,0:T(8,128)(2,1)S(1)} %get-tuple-element.36.refs_5_.w, ...), custom_call_target="tpu_custom_call" | custom-call | bytes 25165824 | tf_op jit(solution)/shard_map/conv1_64/pallas_call | solution.py:331
  72.8 2.8 %conv1_320.1 = (bf16[256,384]{1,0:T(8,128)(2,1)S(1)}, bf16[128,1536]{1,0:T(8,128)(2,1)S(1)}) custom-call(s32[2]{0:T(128)S(1)} %copy-done.4, f32[8,1536]{1,0:T(8,128)S(1)} %finish.3.stats, f32[4,640,128]{2,1,0:T(8,128)S(1)} %keeps.1._.keep, bf16[1536,1152]{1,0:T(8,128)(2,1)S(1)} %get-tuple-element.36.refs_5_.w, ...), custom_call_target="tpu_custom_call" | custom-call | bytes 25165824 | tf_op jit(solution)/shard_map/conv1_320/pallas_call | solution.py:331
  76.3 2.2 %conv1_0.1.rest_0_ = bf16[128,384]{1,0:T(8,128)(2,1)S(1)} custom-call(s32[2]{0:T(128)S(1)} %copy-done.4, f32[8,1536]{1,0:T(8,128)S(1)} %finish.3.stats, f32[4,640,128]{2,1,0:T(8,128)S(1)} %keeps.1._.keep, bf16[1536,1152]{1,0:T(8,128)(2,1)S(1)} %get-tuple-element.36.refs_5_.w, bf16[128,1536]{1,0:T(8,128)(2,1)S(1)} %get-tuple-element.54.rest_3_.rest_0_, ...), custom_call_target="tpu_custom_call" | custom-call | bytes 25165824 | tf_op jit(solution)/shard_map/conv1_0/pallas_call | solution.py:331
  81.4 2.0 %collective-permute-done.22.rest_1_ = bf16[256,384]{1,0:T(8,128)(2,1)S(1)} collective-permute-done((bf16[256,384]{1,0:T(8,128)(2,1)S(1)}, bf16[256,384]{1,0:T(8,128)(2,1)S(1)}, u32[]{:S(2)}, u32[]{:S(2)}) %collective-permute-start.22) | collective-permute-done | bytes 196640 | tf_op jit(solution)/shard_map/ppermute | solution.py:497
  (61 shorter events, 22.9 us)
Async XLA Ops:
  0.0 25.4 %collective-permute-start.4 = (bf16[640,768]{1,0:T(8,128)(2,1)}, bf16[640,768]{1,0:T(8,128)(2,1)S(1)}, u32[]{:S(2)}, u32[]{:S(2)}) collective-permute-start(bf16[640,768]{1,0:T(8,128)(2,1)} %bitcast.2), channel_id=1, source_target_pairs={{0,2},{2,0},{1,3},{3,1},{4,6},{6,4},{5,7},{7,5},{8,10},{10,8},{9,1... | collective-permute-start | bytes 2949128 | tf_op jit(solution)/shard_map/ppermute | solution.py:497
  3.1 1.2 %collective-permute-start = (f32[2,768]{1,0:T(2,128)S(1)}, f32[2,768]{1,0:T(2,128)S(1)}, u32[]{:S(2)}, u32[]{:S(2)}) collective-permute-start(f32[2,768]{1,0:T(2,128)S(1)} %pre.1.a), channel_id=1, source_target_pairs={{0,1},{1,0},{2,3},{3,2},{4,5},{5,4},{6,7},{7,6},{8,9},{9,8},{10,11... | collective-permute-start | bytes 18440 | tf_op jit(solution)/shard_map/ppermute | solution.py:128
  4.4 3.7 %collective-permute-start.1 = (f32[2,768]{1,0:T(2,128)S(1)}, f32[2,768]{1,0:T(2,128)S(1)}, u32[]{:S(2)}, u32[]{:S(2)}) collective-permute-start(f32[2,768]{1,0:T(2,128)S(1)} %merge.4.a), channel_id=1, source_target_pairs={{0,4},{4,0},{8,12},{12,8},{1,5},{5,1},{9,13},{13,9},{2,6},{6,2},{1... | collective-permute-start | bytes 18440 | tf_op jit(solution)/shard_map/ppermute | solution.py:128
  8.1 5.2 %collective-permute-start.2 = (f32[2,768]{1,0:T(2,128)S(1)}, f32[2,768]{1,0:T(2,128)S(1)}, u32[]{:S(2)}, u32[]{:S(2)}) collective-permute-start(f32[2,768]{1,0:T(2,128)S(1)} %merge.5.a), channel_id=1, source_target_pairs={{0,12},{4,8},{8,4},{12,0},{1,13},{5,9},{9,5},{13,1},{2,14},{6,10},... | collective-permute-start | bytes 18440 | tf_op jit(solution)/shard_map/ppermute | solution.py:128
  14.8 15.7 %collective-permute-start.5 = (bf16[96,1536]{1,0:T(8,128)(2,1)S(1)}, bf16[96,1536]{1,0:T(8,128)(2,1)S(1)}, u32[]{:S(2)}, u32[]{:S(2)}) collective-permute-start(bf16[96,1536]{1,0:T(8,128)(2,1)S(1)} %get-tuple-element.39), channel_id=1, source_target_pairs={{0,2},{2,0},{1,3},{3,1},{4,6},{6,4},{5,7},{7,5},{8,10},{10,8},{9,1... | collective-permute-start | bytes 884744 | tf_op jit(solution)/shard_map/ppermute | solution.py:497
  15.6 6.4 %collective-permute-start.3 = (f32[8,768]{1,0:T(8,128)S(1)}, f32[8,768]{1,0:T(8,128)S(1)}, u32[]{:S(2)}, u32[]{:S(2)}) collective-permute-start(f32[8,768]{1,0:T(8,128)S(1)} %finish.2.refs_0_._), channel_id=1, source_target_pairs={{0,6},{2,4},{4,2},{6,0},{8,14},{10,12},{12,10},{14,8},{1,7},{3,5},... | collective-permute-start | bytes 73736 | tf_op jit(solution)/shard_map/ppermute | solution.py:512
  30.6 9.8 %collective-permute-start.7 = (bf16[96,1536]{1,0:T(8,128)(2,1)S(1)}, bf16[96,1536]{1,0:T(8,128)(2,1)S(1)}, u32[]{:S(2)}, u32[]{:S(2)}) collective-permute-start(bf16[96,1536]{1,0:T(8,128)(2,1)S(1)} %collective-permute-done.5.rest_7_), channel_id=1, source_target_pairs={{0,16},{16,0},{1,17},{17,1},{2,18},{18,2},{3,19},{19,3},{4,20},{20... | collective-permute-start | bytes 884744 | tf_op jit(solution)/shard_map/ppermute | solution.py:554
  32.1 8.5 %collective-permute-start.10 = (bf16[64,1536]{1,0:T(8,128)(2,1)S(1)}, bf16[64,1536]{1,0:T(8,128)(2,1)S(1)}, u32[]{:S(2)}, u32[]{:S(2)}) collective-permute-start(bf16[64,1536]{1,0:T(8,128)(2,1)S(1)} %get-tuple-element.49), channel_id=1, source_target_pairs={{4,8},{8,4},{5,9},{9,5},{6,10},{10,6},{7,11},{11,7},{20,24},{24,20... | collective-permute-start | bytes 589832 | tf_op jit(solution)/shard_map/ppermute | solution.py:553
  35.6 15.5 %collective-permute-start.12 = (bf16[96,1536]{1,0:T(8,128)(2,1)S(1)}, bf16[96,1536]{1,0:T(8,128)(2,1)S(1)}, u32[]{:S(2)}, u32[]{:S(2)}) collective-permute-start(bf16[96,1536]{1,0:T(8,128)(2,1)S(1)} %collective-permute-done.5.rest_7_), channel_id=1, source_target_pairs={{0,1},{1,0},{2,3},{3,2},{4,5},{5,4},{6,7},{7,6},{8,9},{9,8},{10,11... | collective-permute-start | bytes 884744 | tf_op jit(solution)/shard_map/ppermute | solution.py:561
  35.6 7.3 %collective-permute-start.6 = (bf16[256,384]{1,0:T(8,128)(2,1)S(1)}, bf16[256,384]{1,0:T(8,128)(2,1)S(1)}, u32[]{:S(2)}, u32[]{:S(2)}) collective-permute-start(bf16[256,384]{1,0:T(8,128)(2,1)S(1)} %get-tuple-element.42.rest_0_), channel_id=1, source_target_pairs={{0,2},{2,0},{1,3},{3,1},{4,6},{6,4},{5,7},{7,5},{8,10},{10,8},{9,1... | collective-permute-start | bytes 589832 | tf_op jit(solution)/shard_map/ppermute | solution.py:497
  37.2 7.0 %collective-permute-start.9 = (bf16[64,1536]{1,0:T(8,128)(2,1)S(1)}, bf16[64,1536]{1,0:T(8,128)(2,1)S(1)}, u32[]{:S(2)}, u32[]{:S(2)}) collective-permute-start(bf16[64,1536]{1,0:T(8,128)(2,1)S(1)} %get-tuple-element.48), channel_id=1, source_target_pairs={{0,4},{4,0},{8,12},{12,8},{1,5},{5,1},{9,13},{13,9},{2,6},{6,2},{1... | collective-permute-start | bytes 589832 | tf_op jit(solution)/shard_map/ppermute | solution.py:553
  40.3 10.7 %collective-permute-start.13 = (bf16[96,1536]{1,0:T(8,128)(2,1)S(1)}, bf16[96,1536]{1,0:T(8,128)(2,1)S(1)}, u32[]{:S(2)}, u32[]{:S(2)}) collective-permute-start(bf16[96,1536]{1,0:T(8,128)(2,1)S(1)} %collective-permute-done.7.rest_8_), channel_id=1, source_target_pairs={{0,1},{1,0},{2,3},{3,2},{4,5},{5,4},{6,7},{7,6},{8,9},{9,8},{10,11... | collective-permute-start | bytes 884744 | tf_op jit(solution)/shard_map/ppermute | solution.py:561
  40.6 10.4 %collective-permute-start.8 = (bf16[256,384]{1,0:T(8,128)(2,1)S(1)}, bf16[256,384]{1,0:T(8,128)(2,1)S(1)}, u32[]{:S(2)}, u32[]{:S(2)}) collective-permute-start(bf16[256,384]{1,0:T(8,128)(2,1)S(1)} %get-tuple-element.46.rest_2_), channel_id=1, source_target_pairs={{0,2},{2,0},{1,3},{3,1},{4,6},{6,4},{5,7},{7,5},{8,10},{10,8},{9,1... | collective-permute-start | bytes 589832 | tf_op jit(solution)/shard_map/ppermute | solution.py:497
  46.3 4.7 %collective-permute-start.11 = (bf16[128,384]{1,0:T(8,128)(2,1)S(1)}, bf16[128,384]{1,0:T(8,128)(2,1)S(1)}, u32[]{:S(2)}, u32[]{:S(2)}) collective-permute-start(bf16[128,384]{1,0:T(8,128)(2,1)S(1)} %conv0_0.1.rest_4_), channel_id=1, source_target_pairs={{0,2},{2,0},{1,3},{3,1},{4,6},{6,4},{5,7},{7,5},{8,10},{10,8},{9,1... | collective-permute-start | bytes 294920 | tf_op jit(solution)/shard_map/ppermute | solution.py:497
  53.9 1.2 %collective-permute-start.14 = (f32[2,1536]{1,0:T(2,128)S(1)}, f32[2,1536]{1,0:T(2,128)S(1)}, u32[]{:S(2)}, u32[]{:S(2)}) collective-permute-start(f32[2,1536]{1,0:T(2,128)S(1)} %get-tuple-element.51.a), channel_id=1, source_target_pairs={{0,1},{1,0},{2,3},{3,2},{4,5},{5,4},{6,7},{7,6},{8,9},{9,8},{10,11... | collective-permute-start | bytes 36872 | tf_op jit(solution)/shard_map/ppermute | solution.py:128
  55.1 11.0 %collective-permute-start.20 = (bf16[192,768]{1,0:T(8,128)(2,1)S(1)}, bf16[192,768]{1,0:T(8,128)(2,1)S(1)}, u32[]{:S(2)}, u32[]{:S(2)}) collective-permute-start(bf16[192,768]{1,0:T(8,128)(2,1)S(1)} %get-tuple-element.62), channel_id=1, source_target_pairs={{0,2},{2,0},{1,3},{3,1},{4,6},{6,4},{5,7},{7,5},{8,10},{10,8},{9,1... | collective-permute-start | bytes 884744 | tf_op jit(solution)/shard_map/ppermute | solution.py:569
  55.7 3.7 %collective-permute-start.15 = (f32[2,1536]{1,0:T(2,128)S(1)}, f32[2,1536]{1,0:T(2,128)S(1)}, u32[]{:S(2)}, u32[]{:S(2)}) collective-permute-start(f32[2,1536]{1,0:T(2,128)S(1)} %merge.6.a), channel_id=1, source_target_pairs={{0,4},{4,0},{8,12},{12,8},{1,5},{5,1},{9,13},{13,9},{2,6},{6,2},{1... | collective-permute-start | bytes 36872 | tf_op jit(solution)/shard_map/ppermute | solution.py:128
  59.4 3.8 %collective-permute-start.16 = (f32[2,1536]{1,0:T(2,128)S(1)}, f32[2,1536]{1,0:T(2,128)S(1)}, u32[]{:S(2)}, u32[]{:S(2)}) collective-permute-start(f32[2,1536]{1,0:T(2,128)S(1)} %merge.7.a), channel_id=1, source_target_pairs={{0,12},{4,8},{8,4},{12,0},{1,13},{5,9},{9,5},{13,1},{2,14},{6,10},... | collective-permute-start | bytes 36872 | tf_op jit(solution)/shard_map/ppermute | solution.py:128
  63.2 13.0 %collective-permute-start.17 = (bf16[64,1536]{1,0:T(8,128)(2,1)S(1)}, bf16[64,1536]{1,0:T(8,128)(2,1)S(1)}, u32[]{:S(2)}, u32[]{:S(2)}) collective-permute-start(bf16[64,1536]{1,0:T(8,128)(2,1)S(1)} %get-tuple-element.59), channel_id=1, source_target_pairs={{0,4},{4,0},{8,12},{12,8},{1,5},{5,1},{9,13},{13,9},{2,6},{6,2},{1... | collective-permute-start | bytes 589832 | tf_op jit(solution)/shard_map/ppermute | solution.py:572
  66.1 13.8 %collective-permute-start.21 = (bf16[192,768]{1,0:T(8,128)(2,1)S(1)}, bf16[192,768]{1,0:T(8,128)(2,1)S(1)}, u32[]{:S(2)}, u32[]{:S(2)}) collective-permute-start(bf16[192,768]{1,0:T(8,128)(2,1)S(1)} %collective-permute-done.20.rest_3_), channel_id=1, source_target_pairs={{0,1},{1,0},{2,3},{3,2},{4,5},{5,4},{6,7},{7,6},{8,9},{9,8},{10,11... | collective-permute-start | bytes 884744 | tf_op jit(solution)/shard_map/ppermute | solution.py:570
  66.1 10.1 %collective-permute-start.18 = (bf16[64,1536]{1,0:T(8,128)(2,1)S(1)}, bf16[64,1536]{1,0:T(8,128)(2,1)S(1)}, u32[]{:S(2)}, u32[]{:S(2)}) collective-permute-start(bf16[64,1536]{1,0:T(8,128)(2,1)S(1)} %get-tuple-element.60), channel_id=1, source_target_pairs={{4,8},{8,4},{5,9},{9,5},{6,10},{10,6},{7,11},{11,7},{20,24},{24,20... | collective-permute-start | bytes 589832 | tf_op jit(solution)/shard_map/ppermute | solution.py:572
  71.3 8.6 %collective-permute-start.23 = (bf16[256,384]{1,0:T(8,128)(2,1)S(1)}, bf16[256,384]{1,0:T(8,128)(2,1)S(1)}, u32[]{:S(2)}, u32[]{:S(2)}) collective-permute-start(bf16[256,384]{1,0:T(8,128)(2,1)S(1)} %get-tuple-element.64.rest_0_), channel_id=1, source_target_pairs={{0,2},{2,0},{1,3},{3,1},{4,6},{6,4},{5,7},{7,5},{8,10},{10,8},{9,1... | collective-permute-start | bytes 589832 | tf_op jit(solution)/shard_map/ppermute | solution.py:497
  75.6 7.8 %collective-permute-start.22 = (bf16[256,384]{1,0:T(8,128)(2,1)S(1)}, bf16[256,384]{1,0:T(8,128)(2,1)S(1)}, u32[]{:S(2)}, u32[]{:S(2)}) collective-permute-start(bf16[256,384]{1,0:T(8,128)(2,1)S(1)} %get-tuple-element.63.rest_0_), channel_id=1, source_target_pairs={{0,2},{2,0},{1,3},{3,1},{4,6},{6,4},{5,7},{7,5},{8,10},{10,8},{9,1... | collective-permute-start | bytes 589832 | tf_op jit(solution)/shard_map/ppermute | solution.py:497
  78.4 6.5 %collective-permute-start.19 = (bf16[128,384]{1,0:T(8,128)(2,1)S(1)}, bf16[128,384]{1,0:T(8,128)(2,1)S(1)}, u32[]{:S(2)}, u32[]{:S(2)}) collective-permute-start(bf16[128,384]{1,0:T(8,128)(2,1)S(1)} %conv1_0.1.rest_0_), channel_id=1, source_target_pairs={{0,2},{2,0},{1,3},{3,1},{4,6},{6,4},{5,7},{7,5},{8,10},{10,8},{9,1... | collective-permute-start | bytes 294920 | tf_op jit(solution)/shard_map/ppermute | solution.py:497
  (8 other events, 29.8 us)

commit v6 on v5

--- a/solution.py
+++ b/solution.py
@@ -68,26 +68,48 @@
     return (a[0:1] + b[0:1]) * 0.5, a[1:2] + b[1:2] + gap * gap * (0.5 * n)
 
 
-def pre_kernel(x, out):
+def pre_kernel(x_hbm, gains, biases, x, out, send1, send2, gains_out, biases_out, sems):
     rows = x.shape[0]
+    load = copy(x_hbm, x, sems.at[2])
+    load.start()
+    copies = [copy(gains, gains_out, sems.at[0]), copy(biases, biases_out, sems.at[1])]
+    for c in copies:
+        c.start()
+    load.wait()
     pivot = jnp.mean(x[0:16, :].astype(F32)[0:8], axis=0, keepdims=True)
     s1 = s2 = jnp.zeros((8, x.shape[1]), F32)
     for r in range(0, rows, 64):
         t1, t2 = sums_about(x[r : r + 64, :].astype(F32), pivot)
         s1, s2 = s1 + t1, s2 + t2
     out[0:1, :], out[1:2, :] = spread_of(pivot, s1, s2, rows)
-
-
-def pre(own):
+    odd = lax.rem(lax.axis_index("seq"), 2)
+    end = rows - HALO
+    send1[...] = x[pl.ds(pl.multiple_of((1 - odd) * end, HALO), HALO), :]
+    send2[...] = x[pl.ds(pl.multiple_of(odd * end, HALO), HALO), :]
+    for c in copies:
+        c.wait()
+
+
+def pre(own, gains, biases):
+    edge = shape((HALO, own.shape[1]), BF16)
+    vector = shape(gains.shape, F32)
     return pl.pallas_call(
         pre_kernel,
-        out_shape=shape((2, own.shape[1]), F32),
-        in_specs=[INV],
-        out_specs=INV,
-        compiler_params=limit(2),
+        out_shape=(
+            shape(own.shape, BF16),
+            shape((2, own.shape[1]), F32),
+            edge,
+            edge,
+            vector,
+            vector,
+        ),
+        in_specs=[HBM] * 3,
+        out_specs=(INV,) * 6,
+        scratch_shapes=[pltpu.SemaphoreType.DMA((3,))],
+        compiler_params=limit(4),
         cost_estimate=FREE,
         name="pre",
-    )(own)
+    )(own, gains, biases)
 
 
 def merge_kernel(n, a, b, out):
@@ -98,7 +120,8 @@
     return lax.rsqrt(m2 * (1.0 / n) + EPS) * gain
 
 
-def finish0_kernel(n, a, b, gains, biases, _, out):
+def finish0_kernel(n, a, b, gains, biases, *rest):
+    out = rest[-1]
     mean, m2 = merged(a[...], b[...], n)
     out[0:1, :] = mean
     out[1:2, :] = scale_of(m2, 2 * n, gains[0:1, :])
@@ -120,7 +143,7 @@
     for axis in ("dp", "seq"):
         size, step = lax.axis_size(axis), 1
         while step < size:
-            steps.append((axis, [(i, i ^ (2 * step - 1)) for i in range(size)]))
+            steps.append((axis, [(i, i ^ step) for i in range(size)]))
             step *= 2
     channels = stat.shape[1]
     found = []
@@ -163,7 +186,7 @@
         out_shape=outs,
         in_specs=[INV] * (2 * n) + [ANY] * len(order),
         out_specs=[INV] * 3,
-        compiler_params=limit(1),
+        compiler_params=limit(4),
         cost_estimate=FREE,
         name="join",
     )(*vecs, *xs, *order)
@@ -199,8 +222,9 @@
     )(w_proj, order)
 
 
-def keep_kernel(lengths, dilations, out):
+def keep_kernel(lengths_hbm, dilations_hbm, out, lengths, dilations, sems):
     rows = out.shape[1]
+    run([copy(lengths_hbm, lengths, sems.at[0]), copy(dilations_hbm, dilations, sems.at[1])])
     first = lax.axis_index("seq") * rows
     ends, end = [], jnp.int32(0)
     for k in range(lengths.shape[1]):
@@ -229,8 +253,13 @@
     return pl.pallas_call(
         keep_kernel,
         out_shape=shape((4, rows, 128), F32),
-        in_specs=[INS, INS],
+        in_specs=[HBM, HBM],
         out_specs=INV,
+        scratch_shapes=[
+            pltpu.SMEM(lengths.shape, jnp.int32),
+            pltpu.SMEM(dilations.shape, jnp.int32),
+            pltpu.SemaphoreType.DMA((2,)),
+        ],
         compiler_params=limit(4),
                 cost_estimate=FREE,
                 name="keeps",
@@ -276,8 +305,11 @@
     )(w_conv)
 
 
-def conv_kernel(pieces, layer, segs, hand, n, n_src, n_order, dilations, stats, keep, w, *rest):
-    srcs, (out, *kept, nbuf, p0, p2) = rest[:n_src], rest[n_src + n_order :]
+def conv_kernel(pieces, layer, segs, hand, n, n_src, n_order, dilations_hbm, stats, keep, w, *rest):
+    srcs, rest = rest[:n_src], rest[n_src + n_order :]
+    out, *kept, nbuf, p0, p2, dilations, sem = rest
+    load = copy(dilations_hbm, dilations, sem)
+    load.start()
     ext, width = nbuf.shape[0], out.shape[1]
     for src, at, count, to, back, raw in pieces:
         src = srcs[src]
@@ -301,6 +333,7 @@
     p0[0 : ext - HALO, :] = sides[: ext - HALO, :width]
     p2[0 : ext - HALO, :] = sides[HALO:, step : step + width]
     mid = dot(nbuf[HALO : ext - HALO, :], w[:, 2 * step : 2 * step + width])
+    load.wait()
     d = dilations[layer]
     to = 0
     for k, (first, count) in enumerate(segs):
@@ -331,12 +364,14 @@
     return pl.pallas_call(
         functools.partial(conv_kernel, pieces, layer, segs, hand, n, len(srcs), len(order)),
         out_shape=outs,
-        in_specs=[INS] + [INV] * (3 + len(srcs)) + [ANY] * len(order),
+        in_specs=[HBM] + [INV] * (3 + len(srcs)) + [ANY] * len(order),
         out_specs=[INV] * len(outs),
         scratch_shapes=[
             pltpu.VMEM((ext, channels), BF16),
             pltpu.VMEM((ext - HALO + 8, width), F32),
             pltpu.VMEM((ext - HALO + 8, width), F32),
+            pltpu.SMEM(dilations.shape, jnp.int32),
+            pltpu.SemaphoreType.DMA,
         ],
         compiler_params=limit(10),
         cost_estimate=cost,
@@ -497,11 +532,14 @@
         return [perm(value, "chan", [(i, (i + k) % n) for i in range(n)]) for k in range(1, n)]
 
     sent = others(own)
-    own = pinned(own, pltpu.VMEM)
-    xs = [own] + [pinned(x, pltpu.VMEM) for x in sent]
+    own = pinned(own, pltpu.HBM)
     taps = [pinned(w, pltpu.VMEM) for w in stage(pinned(w_conv, pltpu.HBM))]
+    lengths, dilations = pinned(lengths, pltpu.HBM), pinned(dilations, pltpu.HBM)
     keep = pinned(keeps(lengths, dilations, rows), pltpu.VMEM)
-    found = batch_stats(pre(own), rows, finish0_kernel, (gains, biases, keep), 1)
+    gains, biases = pinned(gains, pltpu.HBM), pinned(biases, pltpu.HBM)
+    own, stat, _, _, gains, biases = pre(own, gains, biases)
+    xs = [pinned(own, pltpu.VMEM)] + [pinned(x, pltpu.VMEM) for x in sent]
+    found = batch_stats(stat, rows, finish0_kernel, (gains, biases, keep), 1)
     w_proj = pinned(w_proj, pltpu.VMEM)
     vecs = [found[-1]]
     for k in range(1, n):

time: 86.6 us -> 86.2 us (level)
  local copies, waits for them, and re-layouts: 4.55 us -> 0.01 us
  waiting for transfers between devices: 25.4 us -> 29.5 us
  starting transfers between devices: 26.9 us -> 24.3 us
  Pallas kernels: 29.1 us -> 31.3 us
    unnamed x16 -> x2, local copies, waits for them, and re-layouts: 4.55 us -> 0.01 us
    ppermute x8, waiting for transfers between devices: 12.6 us -> 15.6 us  [others(): perm(value, 'chan', [(i, (i + k) % n) for i in range(n)])]
    ppermute x1, starting transfers between devices: 3.26 us -> 1.24 us  [on_device(): vecs.append(perm(found[-1], ('seq', 'chan'), pairs))]
    pallas_call x1, Pallas kernels: 0.39 us -> 2.32 us  [pre(): pl.pallas_call(pre_kernel, out_shape=(shape(own.shape, BF16), shape((2, o...]
    ppermute x4, starting transfers between devices: 8.81 us -> 6.97 us  [on_device(): halos = (perm(send1, 'seq', pairs1), perm(send2, 'seq', pairs2))]
    ppermute x6, starting transfers between devices: 3.77 us -> 5.07 us  [batch_stats(): other = lax.ppermute(stat, axis, pairs)]
  transfers between devices with their start and end apart: 24 -> 24, of which waited for: 11 -> 12; matrix products, arithmetic and copies ran while one was open for 0% -> 0% of each run, Pallas kernels for 29% -> 32%
where the time goes in v6:
time: 86.2 us; the launch traced here: 85.5 us
  Pallas kernels  31.3 us (36%)
  waiting for transfers between devices  29.5 us (34%)
  starting transfers between devices  24.3 us (28%)
    pallas_call x6, Pallas kernels, conv(): pl.pallas_call(functools.partial(conv_kernel, pieces, layer, segs, hand,...  16.3 us
    ppermute x8, waiting for transfers between devices, others(): perm(value, 'chan', [(i, (i + k) % n) for i in range(n)])  15.6 us
    ppermute x6, waiting for transfers between devices, batch_stats(): other = lax.ppermute(stat, axis, pairs)  12.1 us
    ppermute x8, starting transfers between devices, others(): perm(value, 'chan', [(i, (i + k) % n) for i in range(n)])  8.63 us
    ppermute x4, starting transfers between devices, on_device(): halos = (perm(send1, 'seq', pairs1), perm(send2, 'seq', pairs2))  6.97 us
    ppermute x6, starting transfers between devices, batch_stats(): other = lax.ppermute(stat, axis, pairs)  5.07 us
    pallas_call x3, Pallas kernels, proj1(): pl.pallas_call(functools.partial(proj1_kernel, runs, n, len(srcs), last),...  4.19 us
    pallas_call x1, Pallas kernels, stage(): pl.pallas_call(stage_kernel, out_shape=[shape((channels, taps * step), BF...  3.09 us
  transfers between devices with their start and end apart: 24, of which 12 were waited for; matrix products, arithmetic and copies ran while one was open for 0% of the time, Pallas kernels for 32%

profile of v6, /device:TPU:8, one launch (start us, length us, event | category | flops | bytes accessed | tf_op | source)
XLA Modules:
  0.0 85.5 jit_solution(7272015802532809862)
XLA Ops:
  0.0 1.5 %collective-permute-start.4 = (bf16[640,768]{1,0:T(8,128)(2,1)}, bf16[640,768]{1,0:T(8,128)(2,1)S(1)}, u32[]{:S(2)}, u32[]{:S(2)}) collective-permute-start(bf16[640,768]{1,0:T(8,128)(2,1)} %bitcast.2), channel_id=1, source_target_pairs={{0,2},{2,0},{1,3},{3,1},{4,6},{6,4},{5,7},{7,5},{8,10},{10,8},{9,1... | collective-permute-start | bytes 2949128 | tf_op jit(solution)/shard_map/ppermute | solution.py:532
  1.5 2.3 %pre.1 = (bf16[640,768]{1,0:T(8,128)(2,1)S(1)}, f32[2,768]{1,0:T(2,128)S(1)}, bf16[64,768]{1,0:T(8,128)(2,1)}, bf16[64,768]{1,0:T(8,128)(2,1)}, f32[2,768]{1,0:T(2,128)S(1)}, /*index=5*/f32[2,768]{1,0:T(2,128)S(1)}) custom-call(bf16[640,768]{1,0:T(8,128)(2,1)} %bitcast.3, f32[2,768]{1,0:T(2,128)} %gains.1, f32[2,768]{1,0:T(2,128)} %biases.1), custom_call_target="tpu_custom_call" | custom-call | tf_op jit(solution)/shard_map/pre/pallas_call | solution.py:96
  5.6 3.2 %collective-permute-done.1.b = f32[2,768]{1,0:T(2,128)S(1)} collective-permute-done((f32[2,768]{1,0:T(2,128)S(1)}, f32[2,768]{1,0:T(2,128)S(1)}, u32[]{:S(2)}, u32[]{:S(2)}) %collective-permute-start.1) | collective-permute-done | bytes 6176 | tf_op jit(solution)/shard_map/ppermute | solution.py:151
  8.8 2.7 %collective-permute-start.2 = (f32[2,768]{1,0:T(2,128)S(1)}, f32[2,768]{1,0:T(2,128)S(1)}, u32[]{:S(2)}, u32[]{:S(2)}) collective-permute-start(f32[2,768]{1,0:T(2,128)S(1)} %merge.5.a), channel_id=1, source_target_pairs={{0,8},{4,12},{8,0},{12,4},{1,9},{5,13},{9,1},{13,5},{2,10},{6,14},... | collective-permute-start | bytes 18440 | tf_op jit(solution)/shard_map/ppermute | solution.py:151
  11.4 2.4 %keeps.1.rest_0_.keep = f32[4,640,128]{2,1,0:T(8,128)S(1)} custom-call(s32[1,8]{1,0:T(1,128)} %lengths_hbm.1, s32[2]{0:T(128)} %dilations_hbm.13), custom_call_target="tpu_custom_call" | custom-call | tf_op jit(solution)/shard_map/keeps/pallas_call | solution.py:253
  16.0 3.1 %stage.1 = (bf16[1536,1152]{1,0:T(8,128)(2,1)S(1)}, bf16[1536,1152]{1,0:T(8,128)(2,1)S(1)}) custom-call(bf16[2,3,1536,384]{3,2,1,0:T(8,128)(2,1)} %w.2), custom_call_target="tpu_custom_call" | custom-call | tf_op jit(solution)/shard_map/stage/pallas_call | solution.py:296
  19.6 5.8 %collective-permute-done.4.refs_3_.rest_1_.rest_12_ = bf16[640,768]{1,0:T(8,128)(2,1)S(1)} collective-permute-done((bf16[640,768]{1,0:T(8,128)(2,1)}, bf16[640,768]{1,0:T(8,128)(2,1)S(1)}, u32[]{:S(2)}, u32[]{:S(2)}) %collective-permute-start.4) | collective-permute-done | bytes 983072 | tf_op jit(solution)/shard_map/ppermute | solution.py:532
  25.4 3.1 %conv0_64.1 = (bf16[256,384]{1,0:T(8,128)(2,1)S(1)}, bf16[128,1536]{1,0:T(8,128)(2,1)S(1)}) custom-call(s32[2]{0:T(128)} %dilations_hbm.13, f32[8,1536]{1,0:T(8,128)S(1)} %get-tuple-element.48.stats.joined, f32[4,640,128]{2,1,0:T(8,128)S(1)} %keeps.1.rest_0_.keep, bf16[1536,1152]{1,0:T(8,128)(2,1)S(1)} %get-tuple-element.43.refs_4_.w, ...), custom_call_target="tpu_custom_call" | custom-call | bytes 25165824 | tf_op jit(solution)/shard_map/conv0_64/pallas_call | solution.py:364
  28.5 2.0 %collective-permute-done.5.rest_7_ = bf16[96,1536]{1,0:T(8,128)(2,1)S(1)} collective-permute-done((bf16[96,1536]{1,0:T(8,128)(2,1)S(1)}, bf16[96,1536]{1,0:T(8,128)(2,1)S(1)}, u32[]{:S(2)}, u32[]{:S(2)}) %collective-permute-start.5) | collective-permute-done | bytes 294944 | tf_op jit(solution)/shard_map/ppermute | solution.py:532
  30.6 1.5 %collective-permute-start.7 = (bf16[96,1536]{1,0:T(8,128)(2,1)S(1)}, bf16[96,1536]{1,0:T(8,128)(2,1)S(1)}, u32[]{:S(2)}, u32[]{:S(2)}) collective-permute-start(bf16[96,1536]{1,0:T(8,128)(2,1)S(1)} %collective-permute-done.5.rest_7_), channel_id=1, source_target_pairs={{0,16},{16,0},{1,17},{17,1},{2,18},{18,2},{3,19},{19,3},{4,20},{20... | collective-permute-start | bytes 884744 | tf_op jit(solution)/shard_map/ppermute | solution.py:592
  32.1 3.5 %collective-permute-start.10 = (bf16[64,1536]{1,0:T(8,128)(2,1)S(1)}, bf16[64,1536]{1,0:T(8,128)(2,1)S(1)}, u32[]{:S(2)}, u32[]{:S(2)}) collective-permute-start(bf16[64,1536]{1,0:T(8,128)(2,1)S(1)} %get-tuple-element.57), channel_id=1, source_target_pairs={{4,8},{8,4},{5,9},{9,5},{6,10},{10,6},{7,11},{11,7},{20,24},{24,20... | collective-permute-start | bytes 589832 | tf_op jit(solution)/shard_map/ppermute | solution.py:591
  35.6 1.6 %collective-permute-start.6 = (bf16[256,384]{1,0:T(8,128)(2,1)S(1)}, bf16[256,384]{1,0:T(8,128)(2,1)S(1)}, u32[]{:S(2)}, u32[]{:S(2)}) collective-permute-start(bf16[256,384]{1,0:T(8,128)(2,1)S(1)} %get-tuple-element.50.rest_0_), channel_id=1, source_target_pairs={{0,2},{2,0},{1,3},{3,1},{4,6},{6,4},{5,7},{7,5},{8,10},{10,8},{9,1... | collective-permute-start | bytes 589832 | tf_op jit(solution)/shard_map/ppermute | solution.py:532
  37.2 3.1 %conv0_320.1 = (bf16[256,384]{1,0:T(8,128)(2,1)S(1)}, bf16[128,1536]{1,0:T(8,128)(2,1)S(1)}) custom-call(s32[2]{0:T(128)} %dilations_hbm.13, f32[8,1536]{1,0:T(8,128)S(1)} %get-tuple-element.48.stats.joined, f32[4,640,128]{2,1,0:T(8,128)S(1)} %keeps.1.rest_0_.keep, bf16[1536,1152]{1,0:T(8,128)(2,1)S(1)} %get-tuple-element.43.refs_4_.w, ...), custom_call_target="tpu_custom_call" | custom-call | bytes 25165824 | tf_op jit(solution)/shard_map/conv0_320/pallas_call | solution.py:364
  41.2 1.8 %collective-permute-done.6.rest_4_.rest_1_ = bf16[256,384]{1,0:T(8,128)(2,1)S(1)} collective-permute-done((bf16[256,384]{1,0:T(8,128)(2,1)S(1)}, bf16[256,384]{1,0:T(8,128)(2,1)S(1)}, u32[]{:S(2)}, u32[]{:S(2)}) %collective-permute-start.6) | collective-permute-done | bytes 196640 | tf_op jit(solution)/shard_map/ppermute | solution.py:532
  44.2 2.2 %conv0_0.1.rest_4_ = bf16[128,384]{1,0:T(8,128)(2,1)S(1)} custom-call(s32[2]{0:T(128)} %dilations_hbm.13, f32[8,1536]{1,0:T(8,128)S(1)} %get-tuple-element.48.stats.joined, f32[4,640,128]{2,1,0:T(8,128)S(1)} %keeps.1.rest_0_.keep, bf16[1536,1152]{1,0:T(8,128)(2,1)S(1)} %get-tuple-element.43.refs_4_.w, ...), custom_call_target="tpu_custom_call" | custom-call | bytes 25165824 | tf_op jit(solution)/shard_map/conv0_0/pallas_call | solution.py:364
  47.0 4.1 %collective-permute-done.11.rest_5_ = bf16[128,384]{1,0:T(8,128)(2,1)S(1)} collective-permute-done((bf16[128,384]{1,0:T(8,128)(2,1)S(1)}, bf16[128,384]{1,0:T(8,128)(2,1)S(1)}, u32[]{:S(2)}, u32[]{:S(2)}) %collective-permute-start.11) | collective-permute-done | bytes 98336 | tf_op jit(solution)/shard_map/ppermute | solution.py:532
  51.1 2.8 %proj0.1 = (bf16[512,1536]{1,0:T(8,128)(2,1)S(1)}, bf16[64,1536]{1,0:T(8,128)(2,1)S(1)}, bf16[64,1536]{1,0:T(8,128)(2,1)S(1)}, bf16[64,1536]{1,0:T(8,128)(2,1)S(...) custom-call(bf16[256,384]{1,0:T(8,128)(2,1)S(1)} %get-tuple-element.50.rest_0_, ...), custom_call_target="tpu_custom_call" | custom-call | tf_op jit(solution)/shard_map/proj0/pallas_call | solution.py:454
  56.6 2.8 %collective-permute-done.15.b = f32[2,1536]{1,0:T(2,128)S(1)} collective-permute-done((f32[2,1536]{1,0:T(2,128)S(1)}, f32[2,1536]{1,0:T(2,128)S(1)}, u32[]{:S(2)}, u32[]{:S(2)}) %collective-permute-start.15) | collective-permute-done | bytes 12320 | tf_op jit(solution)/shard_map/ppermute | solution.py:151
  60.3 3.8 %collective-permute-done.16.b = f32[2,1536]{1,0:T(2,128)S(1)} collective-permute-done((f32[2,1536]{1,0:T(2,128)S(1)}, f32[2,1536]{1,0:T(2,128)S(1)}, u32[]{:S(2)}, u32[]{:S(2)}) %collective-permute-start.16) | collective-permute-done | bytes 12320 | tf_op jit(solution)/shard_map/ppermute | solution.py:151
  65.1 2.5 %collective-permute-start.18 = (bf16[64,1536]{1,0:T(8,128)(2,1)S(1)}, bf16[64,1536]{1,0:T(8,128)(2,1)S(1)}, u32[]{:S(2)}, u32[]{:S(2)}) collective-permute-start(bf16[64,1536]{1,0:T(8,128)(2,1)S(1)} %get-tuple-element.68), channel_id=1, source_target_pairs={{4,8},{8,4},{5,9},{9,5},{6,10},{10,6},{7,11},{11,7},{20,24},{24,20... | collective-permute-start | bytes 589832 | tf_op jit(solution)/shard_map/ppermute | solution.py:610
  67.6 2.8 %conv1_64.1 = (bf16[256,384]{1,0:T(8,128)(2,1)S(1)}, bf16[128,1536]{1,0:T(8,128)(2,1)S(1)}) custom-call(s32[2]{0:T(128)} %dilations_hbm.13, f32[8,1536]{1,0:T(8,128)S(1)} %finish.3.stats, f32[4,640,128]{2,1,0:T(8,128)S(1)} %keeps.1.rest_0_.keep, bf16[1536,1152]{1,0:T(8,128)(2,1)S(1)} %get-tuple-element.44.refs_5_.w, ...), custom_call_target="tpu_custom_call" | custom-call | bytes 25165824 | tf_op jit(solution)/shard_map/conv1_64/pallas_call | solution.py:364
  71.9 2.8 %conv1_320.1 = (bf16[256,384]{1,0:T(8,128)(2,1)S(1)}, bf16[128,1536]{1,0:T(8,128)(2,1)S(1)}) custom-call(s32[2]{0:T(128)} %dilations_hbm.13, f32[8,1536]{1,0:T(8,128)S(1)} %finish.3.stats, f32[4,640,128]{2,1,0:T(8,128)S(1)} %keeps.1.rest_0_.keep, bf16[1536,1152]{1,0:T(8,128)(2,1)S(1)} %get-tuple-element.44.refs_5_.w, ...), custom_call_target="tpu_custom_call" | custom-call | bytes 25165824 | tf_op jit(solution)/shard_map/conv1_320/pallas_call | solution.py:364
  75.5 2.2 %conv1_0.1.rest_0_ = bf16[128,384]{1,0:T(8,128)(2,1)S(1)} custom-call(s32[2]{0:T(128)} %dilations_hbm.13, f32[8,1536]{1,0:T(8,128)S(1)} %finish.3.stats, f32[4,640,128]{2,1,0:T(8,128)S(1)} %keeps.1.rest_0_.keep, bf16[1536,1152]{1,0:T(8,128)(2,1)S(1)} %get-tuple-element.44.refs_5_.w, bf16[128,1536]{1,0:T(8,128)(2,1)S(1)} %get-tuple-element.62.rest_3_.rest_0_, ...), custom_call_target="tpu_custom_call" | custom-call | bytes 25165824 | tf_op jit(solution)/shard_map/conv1_0/pallas_call | solution.py:364
  80.6 2.0 %collective-permute-done.22.rest_1_ = bf16[256,384]{1,0:T(8,128)(2,1)S(1)} collective-permute-done((bf16[256,384]{1,0:T(8,128)(2,1)S(1)}, bf16[256,384]{1,0:T(8,128)(2,1)S(1)}, u32[]{:S(2)}, u32[]{:S(2)}) %collective-permute-start.22) | collective-permute-done | bytes 196640 | tf_op jit(solution)/shard_map/ppermute | solution.py:532
  (47 shorter events, 19.6 us)
Async XLA Ops:
  0.0 25.4 %collective-permute-start.4 = (bf16[640,768]{1,0:T(8,128)(2,1)}, bf16[640,768]{1,0:T(8,128)(2,1)S(1)}, u32[]{:S(2)}, u32[]{:S(2)}) collective-permute-start(bf16[640,768]{1,0:T(8,128)(2,1)} %bitcast.2), channel_id=1, source_target_pairs={{0,2},{2,0},{1,3},{3,1},{4,6},{6,4},{5,7},{7,5},{8,10},{10,8},{9,1... | collective-permute-start | bytes 2949128 | tf_op jit(solution)/shard_map/ppermute | solution.py:532
  3.8 1.2 %collective-permute-start = (f32[2,768]{1,0:T(2,128)S(1)}, f32[2,768]{1,0:T(2,128)S(1)}, u32[]{:S(2)}, u32[]{:S(2)}) collective-permute-start(f32[2,768]{1,0:T(2,128)S(1)} %get-tuple-element.39.a), channel_id=1, source_target_pairs={{0,1},{1,0},{2,3},{3,2},{4,5},{5,4},{6,7},{7,6},{8,9},{9,8},{10,11... | collective-permute-start | bytes 18440 | tf_op jit(solution)/shard_map/ppermute | solution.py:151
  5.1 3.7 %collective-permute-start.1 = (f32[2,768]{1,0:T(2,128)S(1)}, f32[2,768]{1,0:T(2,128)S(1)}, u32[]{:S(2)}, u32[]{:S(2)}) collective-permute-start(f32[2,768]{1,0:T(2,128)S(1)} %merge.4.a), channel_id=1, source_target_pairs={{0,4},{4,0},{8,12},{12,8},{1,5},{5,1},{9,13},{13,9},{2,6},{6,2},{1... | collective-permute-start | bytes 18440 | tf_op jit(solution)/shard_map/ppermute | solution.py:151
  8.8 5.0 %collective-permute-start.2 = (f32[2,768]{1,0:T(2,128)S(1)}, f32[2,768]{1,0:T(2,128)S(1)}, u32[]{:S(2)}, u32[]{:S(2)}) collective-permute-start(f32[2,768]{1,0:T(2,128)S(1)} %merge.5.a), channel_id=1, source_target_pairs={{0,8},{4,12},{8,0},{12,4},{1,9},{5,13},{9,1},{13,5},{2,10},{6,14},... | collective-permute-start | bytes 18440 | tf_op jit(solution)/shard_map/ppermute | solution.py:151
  14.0 16.6 %collective-permute-start.5 = (bf16[96,1536]{1,0:T(8,128)(2,1)S(1)}, bf16[96,1536]{1,0:T(8,128)(2,1)S(1)}, u32[]{:S(2)}, u32[]{:S(2)}) collective-permute-start(bf16[96,1536]{1,0:T(8,128)(2,1)S(1)} %get-tuple-element.47), channel_id=1, source_target_pairs={{0,2},{2,0},{1,3},{3,1},{4,6},{6,4},{5,7},{7,5},{8,10},{10,8},{9,1... | collective-permute-start | bytes 884744 | tf_op jit(solution)/shard_map/ppermute | solution.py:532
  14.7 4.8 %collective-permute-start.3 = (f32[8,768]{1,0:T(8,128)S(1)}, f32[8,768]{1,0:T(8,128)S(1)}, u32[]{:S(2)}, u32[]{:S(2)}) collective-permute-start(f32[8,768]{1,0:T(8,128)S(1)} %finish.2.refs_0_._), channel_id=1, source_target_pairs={{0,6},{2,4},{4,2},{6,0},{8,14},{10,12},{12,10},{14,8},{1,7},{3,5},... | collective-permute-start | bytes 73736 | tf_op jit(solution)/shard_map/ppermute | solution.py:550
  30.6 9.8 %collective-permute-start.7 = (bf16[96,1536]{1,0:T(8,128)(2,1)S(1)}, bf16[96,1536]{1,0:T(8,128)(2,1)S(1)}, u32[]{:S(2)}, u32[]{:S(2)}) collective-permute-start(bf16[96,1536]{1,0:T(8,128)(2,1)S(1)} %collective-permute-done.5.rest_7_), channel_id=1, source_target_pairs={{0,16},{16,0},{1,17},{17,1},{2,18},{18,2},{3,19},{19,3},{4,20},{20... | collective-permute-start | bytes 884744 | tf_op jit(solution)/shard_map/ppermute | solution.py:592
  32.1 8.5 %collective-permute-start.10 = (bf16[64,1536]{1,0:T(8,128)(2,1)S(1)}, bf16[64,1536]{1,0:T(8,128)(2,1)S(1)}, u32[]{:S(2)}, u32[]{:S(2)}) collective-permute-start(bf16[64,1536]{1,0:T(8,128)(2,1)S(1)} %get-tuple-element.57), channel_id=1, source_target_pairs={{4,8},{8,4},{5,9},{9,5},{6,10},{10,6},{7,11},{11,7},{20,24},{24,20... | collective-permute-start | bytes 589832 | tf_op jit(solution)/shard_map/ppermute | solution.py:591
  35.6 15.5 %collective-permute-start.12 = (bf16[96,1536]{1,0:T(8,128)(2,1)S(1)}, bf16[96,1536]{1,0:T(8,128)(2,1)S(1)}, u32[]{:S(2)}, u32[]{:S(2)}) collective-permute-start(bf16[96,1536]{1,0:T(8,128)(2,1)S(1)} %collective-permute-done.5.rest_7_), channel_id=1, source_target_pairs={{0,1},{1,0},{2,3},{3,2},{4,5},{5,4},{6,7},{7,6},{8,9},{9,8},{10,11... | collective-permute-start | bytes 884744 | tf_op jit(solution)/shard_map/ppermute | solution.py:599
  35.6 7.3 %collective-permute-start.6 = (bf16[256,384]{1,0:T(8,128)(2,1)S(1)}, bf16[256,384]{1,0:T(8,128)(2,1)S(1)}, u32[]{:S(2)}, u32[]{:S(2)}) collective-permute-start(bf16[256,384]{1,0:T(8,128)(2,1)S(1)} %get-tuple-element.50.rest_0_), channel_id=1, source_target_pairs={{0,2},{2,0},{1,3},{3,1},{4,6},{6,4},{5,7},{7,5},{8,10},{10,8},{9,1... | collective-permute-start | bytes 589832 | tf_op jit(solution)/shard_map/ppermute | solution.py:532
  37.2 7.0 %collective-permute-start.9 = (bf16[64,1536]{1,0:T(8,128)(2,1)S(1)}, bf16[64,1536]{1,0:T(8,128)(2,1)S(1)}, u32[]{:S(2)}, u32[]{:S(2)}) collective-permute-start(bf16[64,1536]{1,0:T(8,128)(2,1)S(1)} %get-tuple-element.56), channel_id=1, source_target_pairs={{0,4},{4,0},{8,12},{12,8},{1,5},{5,1},{9,13},{13,9},{2,6},{6,2},{1... | collective-permute-start | bytes 589832 | tf_op jit(solution)/shard_map/ppermute | solution.py:591
  40.3 10.7 %collective-permute-start.13 = (bf16[96,1536]{1,0:T(8,128)(2,1)S(1)}, bf16[96,1536]{1,0:T(8,128)(2,1)S(1)}, u32[]{:S(2)}, u32[]{:S(2)}) collective-permute-start(bf16[96,1536]{1,0:T(8,128)(2,1)S(1)} %collective-permute-done.7.rest_8_), channel_id=1, source_target_pairs={{0,1},{1,0},{2,3},{3,2},{4,5},{5,4},{6,7},{7,6},{8,9},{9,8},{10,11... | collective-permute-start | bytes 884744 | tf_op jit(solution)/shard_map/ppermute | solution.py:599
  40.6 10.5 %collective-permute-start.8 = (bf16[256,384]{1,0:T(8,128)(2,1)S(1)}, bf16[256,384]{1,0:T(8,128)(2,1)S(1)}, u32[]{:S(2)}, u32[]{:S(2)}) collective-permute-start(bf16[256,384]{1,0:T(8,128)(2,1)S(1)} %get-tuple-element.54.rest_2_), channel_id=1, source_target_pairs={{0,2},{2,0},{1,3},{3,1},{4,6},{6,4},{5,7},{7,5},{8,10},{10,8},{9,1... | collective-permute-start | bytes 589832 | tf_op jit(solution)/shard_map/ppermute | solution.py:532
  46.4 4.7 %collective-permute-start.11 = (bf16[128,384]{1,0:T(8,128)(2,1)S(1)}, bf16[128,384]{1,0:T(8,128)(2,1)S(1)}, u32[]{:S(2)}, u32[]{:S(2)}) collective-permute-start(bf16[128,384]{1,0:T(8,128)(2,1)S(1)} %conv0_0.1.rest_4_), channel_id=1, source_target_pairs={{0,2},{2,0},{1,3},{3,1},{4,6},{6,4},{5,7},{7,5},{8,10},{10,8},{9,1... | collective-permute-start | bytes 294920 | tf_op jit(solution)/shard_map/ppermute | solution.py:532
  53.8 1.2 %collective-permute-start.14 = (f32[2,1536]{1,0:T(2,128)S(1)}, f32[2,1536]{1,0:T(2,128)S(1)}, u32[]{:S(2)}, u32[]{:S(2)}) collective-permute-start(f32[2,1536]{1,0:T(2,128)S(1)} %get-tuple-element.59.a), channel_id=1, source_target_pairs={{0,1},{1,0},{2,3},{3,2},{4,5},{5,4},{6,7},{7,6},{8,9},{9,8},{10,11... | collective-permute-start | bytes 36872 | tf_op jit(solution)/shard_map/ppermute | solution.py:151
  55.1 10.0 %collective-permute-start.20 = (bf16[192,768]{1,0:T(8,128)(2,1)S(1)}, bf16[192,768]{1,0:T(8,128)(2,1)S(1)}, u32[]{:S(2)}, u32[]{:S(2)}) collective-permute-start(bf16[192,768]{1,0:T(8,128)(2,1)S(1)} %get-tuple-element.70), channel_id=1, source_target_pairs={{0,2},{2,0},{1,3},{3,1},{4,6},{6,4},{5,7},{7,5},{8,10},{10,8},{9,1... | collective-permute-start | bytes 884744 | tf_op jit(solution)/shard_map/ppermute | solution.py:607
  55.7 3.7 %collective-permute-start.15 = (f32[2,1536]{1,0:T(2,128)S(1)}, f32[2,1536]{1,0:T(2,128)S(1)}, u32[]{:S(2)}, u32[]{:S(2)}) collective-permute-start(f32[2,1536]{1,0:T(2,128)S(1)} %merge.6.a), channel_id=1, source_target_pairs={{0,4},{4,0},{8,12},{12,8},{1,5},{5,1},{9,13},{13,9},{2,6},{6,2},{1... | collective-permute-start | bytes 36872 | tf_op jit(solution)/shard_map/ppermute | solution.py:151
  59.4 4.7 %collective-permute-start.16 = (f32[2,1536]{1,0:T(2,128)S(1)}, f32[2,1536]{1,0:T(2,128)S(1)}, u32[]{:S(2)}, u32[]{:S(2)}) collective-permute-start(f32[2,1536]{1,0:T(2,128)S(1)} %merge.7.a), channel_id=1, source_target_pairs={{0,8},{4,12},{8,0},{12,4},{1,9},{5,13},{9,1},{13,5},{2,10},{6,14},... | collective-permute-start | bytes 36872 | tf_op jit(solution)/shard_map/ppermute | solution.py:151
  64.1 11.4 %collective-permute-start.17 = (bf16[64,1536]{1,0:T(8,128)(2,1)S(1)}, bf16[64,1536]{1,0:T(8,128)(2,1)S(1)}, u32[]{:S(2)}, u32[]{:S(2)}) collective-permute-start(bf16[64,1536]{1,0:T(8,128)(2,1)S(1)} %get-tuple-element.67), channel_id=1, source_target_pairs={{0,4},{4,0},{8,12},{12,8},{1,5},{5,1},{9,13},{13,9},{2,6},{6,2},{1... | collective-permute-start | bytes 589832 | tf_op jit(solution)/shard_map/ppermute | solution.py:610
  65.1 14.1 %collective-permute-start.21 = (bf16[192,768]{1,0:T(8,128)(2,1)S(1)}, bf16[192,768]{1,0:T(8,128)(2,1)S(1)}, u32[]{:S(2)}, u32[]{:S(2)}) collective-permute-start(bf16[192,768]{1,0:T(8,128)(2,1)S(1)} %collective-permute-done.20.rest_3_), channel_id=1, source_target_pairs={{0,1},{1,0},{2,3},{3,2},{4,5},{5,4},{6,7},{7,6},{8,9},{9,8},{10,11... | collective-permute-start | bytes 884744 | tf_op jit(solution)/shard_map/ppermute | solution.py:608
  65.1 10.4 %collective-permute-start.18 = (bf16[64,1536]{1,0:T(8,128)(2,1)S(1)}, bf16[64,1536]{1,0:T(8,128)(2,1)S(1)}, u32[]{:S(2)}, u32[]{:S(2)}) collective-permute-start(bf16[64,1536]{1,0:T(8,128)(2,1)S(1)} %get-tuple-element.68), channel_id=1, source_target_pairs={{4,8},{8,4},{5,9},{9,5},{6,10},{10,6},{7,11},{11,7},{20,24},{24,20... | collective-permute-start | bytes 589832 | tf_op jit(solution)/shard_map/ppermute | solution.py:610
  70.5 8.7 %collective-permute-start.23 = (bf16[256,384]{1,0:T(8,128)(2,1)S(1)}, bf16[256,384]{1,0:T(8,128)(2,1)S(1)}, u32[]{:S(2)}, u32[]{:S(2)}) collective-permute-start(bf16[256,384]{1,0:T(8,128)(2,1)S(1)} %get-tuple-element.72.rest_0_), channel_id=1, source_target_pairs={{0,2},{2,0},{1,3},{3,1},{4,6},{6,4},{5,7},{7,5},{8,10},{10,8},{9,1... | collective-permute-start | bytes 589832 | tf_op jit(solution)/shard_map/ppermute | solution.py:532
  74.8 7.8 %collective-permute-start.22 = (bf16[256,384]{1,0:T(8,128)(2,1)S(1)}, bf16[256,384]{1,0:T(8,128)(2,1)S(1)}, u32[]{:S(2)}, u32[]{:S(2)}) collective-permute-start(bf16[256,384]{1,0:T(8,128)(2,1)S(1)} %get-tuple-element.71.rest_0_), channel_id=1, source_target_pairs={{0,2},{2,0},{1,3},{3,1},{4,6},{6,4},{5,7},{7,5},{8,10},{10,8},{9,1... | collective-permute-start | bytes 589832 | tf_op jit(solution)/shard_map/ppermute | solution.py:532
  77.7 6.4 %collective-permute-start.19 = (bf16[128,384]{1,0:T(8,128)(2,1)S(1)}, bf16[128,384]{1,0:T(8,128)(2,1)S(1)}, u32[]{:S(2)}, u32[]{:S(2)}) collective-permute-start(bf16[128,384]{1,0:T(8,128)(2,1)S(1)} %conv1_0.1.rest_0_), channel_id=1, source_target_pairs={{0,2},{2,0},{1,3},{3,1},{4,6},{6,4},{5,7},{7,5},{8,10},{10,8},{9,1... | collective-permute-start | bytes 294920 | tf_op jit(solution)/shard_map/ppermute | solution.py:532
  (1 other events, 13.9 us)

commit v7 on v6

--- a/solution.py
+++ b/solution.py
@@ -321,11 +321,11 @@
             nbuf[to : to + count, cols] = src[at : at + count, :]
             continue
         mean, scale, bias = stats[0:1, cols], stats[1:2, cols], stats[2:3, cols]
-        block = 128 if count % 128 == 0 else 64
+        block = 32
 
         for rows in range(0, count, block):
             v = src[at + rows : at + rows + block, :].astype(F32)
-            dst = pl.ds(pl.multiple_of(to + rows, HALO), block)
+            dst = pl.ds(pl.multiple_of(to + rows, 32), block)
             nbuf[dst, cols] = gelu((v - mean) * scale + bias).astype(BF16)
 
     step = w.shape[1] // 3

time: 86.2 us -> 86.2 us (level)
  no operation moved by 1% of the time
where the time goes in v7:
time: 86.2 us; the launch traced here: 85.5 us
  Pallas kernels  31.3 us (36%)
  waiting for transfers between devices  29.5 us (34%)
  starting transfers between devices  24.3 us (28%)
    pallas_call x6, Pallas kernels, conv(): pl.pallas_call(functools.partial(conv_kernel, pieces, layer, segs, hand,...  16.3 us
    ppermute x8, waiting for transfers between devices, others(): perm(value, 'chan', [(i, (i + k) % n) for i in range(n)])  15.6 us
    ppermute x6, waiting for transfers between devices, batch_stats(): other = lax.ppermute(stat, axis, pairs)  12.1 us
    ppermute x8, starting transfers between devices, others(): perm(value, 'chan', [(i, (i + k) % n) for i in range(n)])  8.63 us
    ppermute x4, starting transfers between devices, on_device(): halos = (perm(send1, 'seq', pairs1), perm(send2, 'seq', pairs2))  6.96 us
    ppermute x6, starting transfers between devices, batch_stats(): other = lax.ppermute(stat, axis, pairs)  5.05 us
    pallas_call x3, Pallas kernels, proj1(): pl.pallas_call(functools.partial(proj1_kernel, runs, n, len(srcs), last),...  4.19 us
    pallas_call x1, Pallas kernels, stage(): pl.pallas_call(stage_kernel, out_shape=[shape((channels, taps * step), BF...  3.09 us
  transfers between devices with their start and end apart: 24, of which 12 were waited for; matrix products, arithmetic and copies ran while one was open for 0% of the time, Pallas kernels for 32%

profile of v7, /device:TPU:8, one launch (start us, length us, event | category | flops | bytes accessed | tf_op | source)
XLA Modules:
  0.0 85.5 jit_solution(4815076502375296978)
XLA Ops:
  0.0 1.5 %collective-permute-start.4 = (bf16[640,768]{1,0:T(8,128)(2,1)}, bf16[640,768]{1,0:T(8,128)(2,1)S(1)}, u32[]{:S(2)}, u32[]{:S(2)}) collective-permute-start(bf16[640,768]{1,0:T(8,128)(2,1)} %bitcast.2), channel_id=1, source_target_pairs={{0,2},{2,0},{1,3},{3,1},{4,6},{6,4},{5,7},{7,5},{8,10},{10,8},{9,1... | collective-permute-start | bytes 2949128 | tf_op jit(solution)/shard_map/ppermute | solution.py:532
  1.5 2.3 %pre.1 = (bf16[640,768]{1,0:T(8,128)(2,1)S(1)}, f32[2,768]{1,0:T(2,128)S(1)}, bf16[64,768]{1,0:T(8,128)(2,1)}, bf16[64,768]{1,0:T(8,128)(2,1)}, f32[2,768]{1,0:T(2,128)S(1)}, /*index=5*/f32[2,768]{1,0:T(2,128)S(1)}) custom-call(bf16[640,768]{1,0:T(8,128)(2,1)} %bitcast.3, f32[2,768]{1,0:T(2,128)} %gains.1, f32[2,768]{1,0:T(2,128)} %biases.1), custom_call_target="tpu_custom_call" | custom-call | tf_op jit(solution)/shard_map/pre/pallas_call | solution.py:96
  5.6 3.2 %collective-permute-done.1.b = f32[2,768]{1,0:T(2,128)S(1)} collective-permute-done((f32[2,768]{1,0:T(2,128)S(1)}, f32[2,768]{1,0:T(2,128)S(1)}, u32[]{:S(2)}, u32[]{:S(2)}) %collective-permute-start.1) | collective-permute-done | bytes 6176 | tf_op jit(solution)/shard_map/ppermute | solution.py:151
  8.8 2.7 %collective-permute-start.2 = (f32[2,768]{1,0:T(2,128)S(1)}, f32[2,768]{1,0:T(2,128)S(1)}, u32[]{:S(2)}, u32[]{:S(2)}) collective-permute-start(f32[2,768]{1,0:T(2,128)S(1)} %merge.5.a), channel_id=1, source_target_pairs={{0,8},{4,12},{8,0},{12,4},{1,9},{5,13},{9,1},{13,5},{2,10},{6,14},... | collective-permute-start | bytes 18440 | tf_op jit(solution)/shard_map/ppermute | solution.py:151
  11.4 2.4 %keeps.1.rest_0_.keep = f32[4,640,128]{2,1,0:T(8,128)S(1)} custom-call(s32[1,8]{1,0:T(1,128)} %lengths_hbm.1, s32[2]{0:T(128)} %dilations_hbm.13), custom_call_target="tpu_custom_call" | custom-call | tf_op jit(solution)/shard_map/keeps/pallas_call | solution.py:253
  16.0 3.1 %stage.1 = (bf16[1536,1152]{1,0:T(8,128)(2,1)S(1)}, bf16[1536,1152]{1,0:T(8,128)(2,1)S(1)}) custom-call(bf16[2,3,1536,384]{3,2,1,0:T(8,128)(2,1)} %w.2), custom_call_target="tpu_custom_call" | custom-call | tf_op jit(solution)/shard_map/stage/pallas_call | solution.py:296
  19.6 5.8 %collective-permute-done.4.refs_3_.rest_1_.rest_12_ = bf16[640,768]{1,0:T(8,128)(2,1)S(1)} collective-permute-done((bf16[640,768]{1,0:T(8,128)(2,1)}, bf16[640,768]{1,0:T(8,128)(2,1)S(1)}, u32[]{:S(2)}, u32[]{:S(2)}) %collective-permute-start.4) | collective-permute-done | bytes 983072 | tf_op jit(solution)/shard_map/ppermute | solution.py:532
  25.4 3.1 %conv0_64.1 = (bf16[256,384]{1,0:T(8,128)(2,1)S(1)}, bf16[128,1536]{1,0:T(8,128)(2,1)S(1)}) custom-call(s32[2]{0:T(128)} %dilations_hbm.13, f32[8,1536]{1,0:T(8,128)S(1)} %get-tuple-element.48.stats.joined, f32[4,640,128]{2,1,0:T(8,128)S(1)} %keeps.1.rest_0_.keep, bf16[1536,1152]{1,0:T(8,128)(2,1)S(1)} %get-tuple-element.43.refs_4_.w, ...), custom_call_target="tpu_custom_call" | custom-call | bytes 25165824 | tf_op jit(solution)/shard_map/conv0_64/pallas_call | solution.py:364
  28.6 2.0 %collective-permute-done.5.rest_7_ = bf16[96,1536]{1,0:T(8,128)(2,1)S(1)} collective-permute-done((bf16[96,1536]{1,0:T(8,128)(2,1)S(1)}, bf16[96,1536]{1,0:T(8,128)(2,1)S(1)}, u32[]{:S(2)}, u32[]{:S(2)}) %collective-permute-start.5) | collective-permute-done | bytes 294944 | tf_op jit(solution)/shard_map/ppermute | solution.py:532
  30.6 1.5 %collective-permute-start.7 = (bf16[96,1536]{1,0:T(8,128)(2,1)S(1)}, bf16[96,1536]{1,0:T(8,128)(2,1)S(1)}, u32[]{:S(2)}, u32[]{:S(2)}) collective-permute-start(bf16[96,1536]{1,0:T(8,128)(2,1)S(1)} %collective-permute-done.5.rest_7_), channel_id=1, source_target_pairs={{0,16},{16,0},{1,17},{17,1},{2,18},{18,2},{3,19},{19,3},{4,20},{20... | collective-permute-start | bytes 884744 | tf_op jit(solution)/shard_map/ppermute | solution.py:592
  32.1 3.5 %collective-permute-start.10 = (bf16[64,1536]{1,0:T(8,128)(2,1)S(1)}, bf16[64,1536]{1,0:T(8,128)(2,1)S(1)}, u32[]{:S(2)}, u32[]{:S(2)}) collective-permute-start(bf16[64,1536]{1,0:T(8,128)(2,1)S(1)} %get-tuple-element.57), channel_id=1, source_target_pairs={{4,8},{8,4},{5,9},{9,5},{6,10},{10,6},{7,11},{11,7},{20,24},{24,20... | collective-permute-start | bytes 589832 | tf_op jit(solution)/shard_map/ppermute | solution.py:591
  35.6 1.6 %collective-permute-start.6 = (bf16[256,384]{1,0:T(8,128)(2,1)S(1)}, bf16[256,384]{1,0:T(8,128)(2,1)S(1)}, u32[]{:S(2)}, u32[]{:S(2)}) collective-permute-start(bf16[256,384]{1,0:T(8,128)(2,1)S(1)} %get-tuple-element.50.rest_0_), channel_id=1, source_target_pairs={{0,2},{2,0},{1,3},{3,1},{4,6},{6,4},{5,7},{7,5},{8,10},{10,8},{9,1... | collective-permute-start | bytes 589832 | tf_op jit(solution)/shard_map/ppermute | solution.py:532
  37.2 3.1 %conv0_320.1 = (bf16[256,384]{1,0:T(8,128)(2,1)S(1)}, bf16[128,1536]{1,0:T(8,128)(2,1)S(1)}) custom-call(s32[2]{0:T(128)} %dilations_hbm.13, f32[8,1536]{1,0:T(8,128)S(1)} %get-tuple-element.48.stats.joined, f32[4,640,128]{2,1,0:T(8,128)S(1)} %keeps.1.rest_0_.keep, bf16[1536,1152]{1,0:T(8,128)(2,1)S(1)} %get-tuple-element.43.refs_4_.w, ...), custom_call_target="tpu_custom_call" | custom-call | bytes 25165824 | tf_op jit(solution)/shard_map/conv0_320/pallas_call | solution.py:364
  41.2 1.8 %collective-permute-done.6.rest_4_.rest_1_ = bf16[256,384]{1,0:T(8,128)(2,1)S(1)} collective-permute-done((bf16[256,384]{1,0:T(8,128)(2,1)S(1)}, bf16[256,384]{1,0:T(8,128)(2,1)S(1)}, u32[]{:S(2)}, u32[]{:S(2)}) %collective-permute-start.6) | collective-permute-done | bytes 196640 | tf_op jit(solution)/shard_map/ppermute | solution.py:532
  44.2 2.2 %conv0_0.1.rest_4_ = bf16[128,384]{1,0:T(8,128)(2,1)S(1)} custom-call(s32[2]{0:T(128)} %dilations_hbm.13, f32[8,1536]{1,0:T(8,128)S(1)} %get-tuple-element.48.stats.joined, f32[4,640,128]{2,1,0:T(8,128)S(1)} %keeps.1.rest_0_.keep, bf16[1536,1152]{1,0:T(8,128)(2,1)S(1)} %get-tuple-element.43.refs_4_.w, ...), custom_call_target="tpu_custom_call" | custom-call | bytes 25165824 | tf_op jit(solution)/shard_map/conv0_0/pallas_call | solution.py:364
  47.0 4.1 %collective-permute-done.11.rest_5_ = bf16[128,384]{1,0:T(8,128)(2,1)S(1)} collective-permute-done((bf16[128,384]{1,0:T(8,128)(2,1)S(1)}, bf16[128,384]{1,0:T(8,128)(2,1)S(1)}, u32[]{:S(2)}, u32[]{:S(2)}) %collective-permute-start.11) | collective-permute-done | bytes 98336 | tf_op jit(solution)/shard_map/ppermute | solution.py:532
  51.1 2.8 %proj0.1 = (bf16[512,1536]{1,0:T(8,128)(2,1)S(1)}, bf16[64,1536]{1,0:T(8,128)(2,1)S(1)}, bf16[64,1536]{1,0:T(8,128)(2,1)S(1)}, bf16[64,1536]{1,0:T(8,128)(2,1)S(...) custom-call(bf16[256,384]{1,0:T(8,128)(2,1)S(1)} %get-tuple-element.50.rest_0_, ...), custom_call_target="tpu_custom_call" | custom-call | tf_op jit(solution)/shard_map/proj0/pallas_call | solution.py:454
  56.6 2.8 %collective-permute-done.15.b = f32[2,1536]{1,0:T(2,128)S(1)} collective-permute-done((f32[2,1536]{1,0:T(2,128)S(1)}, f32[2,1536]{1,0:T(2,128)S(1)}, u32[]{:S(2)}, u32[]{:S(2)}) %collective-permute-start.15) | collective-permute-done | bytes 12320 | tf_op jit(solution)/shard_map/ppermute | solution.py:151
  60.3 3.8 %collective-permute-done.16.b = f32[2,1536]{1,0:T(2,128)S(1)} collective-permute-done((f32[2,1536]{1,0:T(2,128)S(1)}, f32[2,1536]{1,0:T(2,128)S(1)}, u32[]{:S(2)}, u32[]{:S(2)}) %collective-permute-start.16) | collective-permute-done | bytes 12320 | tf_op jit(solution)/shard_map/ppermute | solution.py:151
  65.1 2.5 %collective-permute-start.18 = (bf16[64,1536]{1,0:T(8,128)(2,1)S(1)}, bf16[64,1536]{1,0:T(8,128)(2,1)S(1)}, u32[]{:S(2)}, u32[]{:S(2)}) collective-permute-start(bf16[64,1536]{1,0:T(8,128)(2,1)S(1)} %get-tuple-element.68), channel_id=1, source_target_pairs={{4,8},{8,4},{5,9},{9,5},{6,10},{10,6},{7,11},{11,7},{20,24},{24,20... | collective-permute-start | bytes 589832 | tf_op jit(solution)/shard_map/ppermute | solution.py:610
  67.6 2.9 %conv1_64.1 = (bf16[256,384]{1,0:T(8,128)(2,1)S(1)}, bf16[128,1536]{1,0:T(8,128)(2,1)S(1)}) custom-call(s32[2]{0:T(128)} %dilations_hbm.13, f32[8,1536]{1,0:T(8,128)S(1)} %finish.3.stats, f32[4,640,128]{2,1,0:T(8,128)S(1)} %keeps.1.rest_0_.keep, bf16[1536,1152]{1,0:T(8,128)(2,1)S(1)} %get-tuple-element.44.refs_5_.w, ...), custom_call_target="tpu_custom_call" | custom-call | bytes 25165824 | tf_op jit(solution)/shard_map/conv1_64/pallas_call | solution.py:364
  71.9 2.8 %conv1_320.1 = (bf16[256,384]{1,0:T(8,128)(2,1)S(1)}, bf16[128,1536]{1,0:T(8,128)(2,1)S(1)}) custom-call(s32[2]{0:T(128)} %dilations_hbm.13, f32[8,1536]{1,0:T(8,128)S(1)} %finish.3.stats, f32[4,640,128]{2,1,0:T(8,128)S(1)} %keeps.1.rest_0_.keep, bf16[1536,1152]{1,0:T(8,128)(2,1)S(1)} %get-tuple-element.44.refs_5_.w, ...), custom_call_target="tpu_custom_call" | custom-call | bytes 25165824 | tf_op jit(solution)/shard_map/conv1_320/pallas_call | solution.py:364
  75.5 2.2 %conv1_0.1.rest_0_ = bf16[128,384]{1,0:T(8,128)(2,1)S(1)} custom-call(s32[2]{0:T(128)} %dilations_hbm.13, f32[8,1536]{1,0:T(8,128)S(1)} %finish.3.stats, f32[4,640,128]{2,1,0:T(8,128)S(1)} %keeps.1.rest_0_.keep, bf16[1536,1152]{1,0:T(8,128)(2,1)S(1)} %get-tuple-element.44.refs_5_.w, bf16[128,1536]{1,0:T(8,128)(2,1)S(1)} %get-tuple-element.62.rest_3_.rest_0_, ...), custom_call_target="tpu_custom_call" | custom-call | bytes 25165824 | tf_op jit(solution)/shard_map/conv1_0/pallas_call | solution.py:364
  80.6 2.0 %collective-permute-done.22.rest_1_ = bf16[256,384]{1,0:T(8,128)(2,1)S(1)} collective-permute-done((bf16[256,384]{1,0:T(8,128)(2,1)S(1)}, bf16[256,384]{1,0:T(8,128)(2,1)S(1)}, u32[]{:S(2)}, u32[]{:S(2)}) %collective-permute-start.22) | collective-permute-done | bytes 196640 | tf_op jit(solution)/shard_map/ppermute | solution.py:532
  (47 shorter events, 19.6 us)
Async XLA Ops:
  0.0 25.4 %collective-permute-start.4 = (bf16[640,768]{1,0:T(8,128)(2,1)}, bf16[640,768]{1,0:T(8,128)(2,1)S(1)}, u32[]{:S(2)}, u32[]{:S(2)}) collective-permute-start(bf16[640,768]{1,0:T(8,128)(2,1)} %bitcast.2), channel_id=1, source_target_pairs={{0,2},{2,0},{1,3},{3,1},{4,6},{6,4},{5,7},{7,5},{8,10},{10,8},{9,1... | collective-permute-start | bytes 2949128 | tf_op jit(solution)/shard_map/ppermute | solution.py:532
  3.8 1.2 %collective-permute-start = (f32[2,768]{1,0:T(2,128)S(1)}, f32[2,768]{1,0:T(2,128)S(1)}, u32[]{:S(2)}, u32[]{:S(2)}) collective-permute-start(f32[2,768]{1,0:T(2,128)S(1)} %get-tuple-element.39.a), channel_id=1, source_target_pairs={{0,1},{1,0},{2,3},{3,2},{4,5},{5,4},{6,7},{7,6},{8,9},{9,8},{10,11... | collective-permute-start | bytes 18440 | tf_op jit(solution)/shard_map/ppermute | solution.py:151
  5.1 3.7 %collective-permute-start.1 = (f32[2,768]{1,0:T(2,128)S(1)}, f32[2,768]{1,0:T(2,128)S(1)}, u32[]{:S(2)}, u32[]{:S(2)}) collective-permute-start(f32[2,768]{1,0:T(2,128)S(1)} %merge.4.a), channel_id=1, source_target_pairs={{0,4},{4,0},{8,12},{12,8},{1,5},{5,1},{9,13},{13,9},{2,6},{6,2},{1... | collective-permute-start | bytes 18440 | tf_op jit(solution)/shard_map/ppermute | solution.py:151
  8.8 5.0 %collective-permute-start.2 = (f32[2,768]{1,0:T(2,128)S(1)}, f32[2,768]{1,0:T(2,128)S(1)}, u32[]{:S(2)}, u32[]{:S(2)}) collective-permute-start(f32[2,768]{1,0:T(2,128)S(1)} %merge.5.a), channel_id=1, source_target_pairs={{0,8},{4,12},{8,0},{12,4},{1,9},{5,13},{9,1},{13,5},{2,10},{6,14},... | collective-permute-start | bytes 18440 | tf_op jit(solution)/shard_map/ppermute | solution.py:151
  14.0 16.6 %collective-permute-start.5 = (bf16[96,1536]{1,0:T(8,128)(2,1)S(1)}, bf16[96,1536]{1,0:T(8,128)(2,1)S(1)}, u32[]{:S(2)}, u32[]{:S(2)}) collective-permute-start(bf16[96,1536]{1,0:T(8,128)(2,1)S(1)} %get-tuple-element.47), channel_id=1, source_target_pairs={{0,2},{2,0},{1,3},{3,1},{4,6},{6,4},{5,7},{7,5},{8,10},{10,8},{9,1... | collective-permute-start | bytes 884744 | tf_op jit(solution)/shard_map/ppermute | solution.py:532
  14.7 4.8 %collective-permute-start.3 = (f32[8,768]{1,0:T(8,128)S(1)}, f32[8,768]{1,0:T(8,128)S(1)}, u32[]{:S(2)}, u32[]{:S(2)}) collective-permute-start(f32[8,768]{1,0:T(8,128)S(1)} %finish.2.refs_0_._), channel_id=1, source_target_pairs={{0,6},{2,4},{4,2},{6,0},{8,14},{10,12},{12,10},{14,8},{1,7},{3,5},... | collective-permute-start | bytes 73736 | tf_op jit(solution)/shard_map/ppermute | solution.py:550
  30.6 9.8 %collective-permute-start.7 = (bf16[96,1536]{1,0:T(8,128)(2,1)S(1)}, bf16[96,1536]{1,0:T(8,128)(2,1)S(1)}, u32[]{:S(2)}, u32[]{:S(2)}) collective-permute-start(bf16[96,1536]{1,0:T(8,128)(2,1)S(1)} %collective-permute-done.5.rest_7_), channel_id=1, source_target_pairs={{0,16},{16,0},{1,17},{17,1},{2,18},{18,2},{3,19},{19,3},{4,20},{20... | collective-permute-start | bytes 884744 | tf_op jit(solution)/shard_map/ppermute | solution.py:592
  32.1 8.5 %collective-permute-start.10 = (bf16[64,1536]{1,0:T(8,128)(2,1)S(1)}, bf16[64,1536]{1,0:T(8,128)(2,1)S(1)}, u32[]{:S(2)}, u32[]{:S(2)}) collective-permute-start(bf16[64,1536]{1,0:T(8,128)(2,1)S(1)} %get-tuple-element.57), channel_id=1, source_target_pairs={{4,8},{8,4},{5,9},{9,5},{6,10},{10,6},{7,11},{11,7},{20,24},{24,20... | collective-permute-start | bytes 589832 | tf_op jit(solution)/shard_map/ppermute | solution.py:591
  35.6 15.5 %collective-permute-start.12 = (bf16[96,1536]{1,0:T(8,128)(2,1)S(1)}, bf16[96,1536]{1,0:T(8,128)(2,1)S(1)}, u32[]{:S(2)}, u32[]{:S(2)}) collective-permute-start(bf16[96,1536]{1,0:T(8,128)(2,1)S(1)} %collective-permute-done.5.rest_7_), channel_id=1, source_target_pairs={{0,1},{1,0},{2,3},{3,2},{4,5},{5,4},{6,7},{7,6},{8,9},{9,8},{10,11... | collective-permute-start | bytes 884744 | tf_op jit(solution)/shard_map/ppermute | solution.py:599
  35.6 7.3 %collective-permute-start.6 = (bf16[256,384]{1,0:T(8,128)(2,1)S(1)}, bf16[256,384]{1,0:T(8,128)(2,1)S(1)}, u32[]{:S(2)}, u32[]{:S(2)}) collective-permute-start(bf16[256,384]{1,0:T(8,128)(2,1)S(1)} %get-tuple-element.50.rest_0_), channel_id=1, source_target_pairs={{0,2},{2,0},{1,3},{3,1},{4,6},{6,4},{5,7},{7,5},{8,10},{10,8},{9,1... | collective-permute-start | bytes 589832 | tf_op jit(solution)/shard_map/ppermute | solution.py:532
  37.2 7.0 %collective-permute-start.9 = (bf16[64,1536]{1,0:T(8,128)(2,1)S(1)}, bf16[64,1536]{1,0:T(8,128)(2,1)S(1)}, u32[]{:S(2)}, u32[]{:S(2)}) collective-permute-start(bf16[64,1536]{1,0:T(8,128)(2,1)S(1)} %get-tuple-element.56), channel_id=1, source_target_pairs={{0,4},{4,0},{8,12},{12,8},{1,5},{5,1},{9,13},{13,9},{2,6},{6,2},{1... | collective-permute-start | bytes 589832 | tf_op jit(solution)/shard_map/ppermute | solution.py:591
  40.3 10.7 %collective-permute-start.13 = (bf16[96,1536]{1,0:T(8,128)(2,1)S(1)}, bf16[96,1536]{1,0:T(8,128)(2,1)S(1)}, u32[]{:S(2)}, u32[]{:S(2)}) collective-permute-start(bf16[96,1536]{1,0:T(8,128)(2,1)S(1)} %collective-permute-done.7.rest_8_), channel_id=1, source_target_pairs={{0,1},{1,0},{2,3},{3,2},{4,5},{5,4},{6,7},{7,6},{8,9},{9,8},{10,11... | collective-permute-start | bytes 884744 | tf_op jit(solution)/shard_map/ppermute | solution.py:599
  40.6 10.5 %collective-permute-start.8 = (bf16[256,384]{1,0:T(8,128)(2,1)S(1)}, bf16[256,384]{1,0:T(8,128)(2,1)S(1)}, u32[]{:S(2)}, u32[]{:S(2)}) collective-permute-start(bf16[256,384]{1,0:T(8,128)(2,1)S(1)} %get-tuple-element.54.rest_2_), channel_id=1, source_target_pairs={{0,2},{2,0},{1,3},{3,1},{4,6},{6,4},{5,7},{7,5},{8,10},{10,8},{9,1... | collective-permute-start | bytes 589832 | tf_op jit(solution)/shard_map/ppermute | solution.py:532
  46.4 4.7 %collective-permute-start.11 = (bf16[128,384]{1,0:T(8,128)(2,1)S(1)}, bf16[128,384]{1,0:T(8,128)(2,1)S(1)}, u32[]{:S(2)}, u32[]{:S(2)}) collective-permute-start(bf16[128,384]{1,0:T(8,128)(2,1)S(1)} %conv0_0.1.rest_4_), channel_id=1, source_target_pairs={{0,2},{2,0},{1,3},{3,1},{4,6},{6,4},{5,7},{7,5},{8,10},{10,8},{9,1... | collective-permute-start | bytes 294920 | tf_op jit(solution)/shard_map/ppermute | solution.py:532
  53.8 1.2 %collective-permute-start.14 = (f32[2,1536]{1,0:T(2,128)S(1)}, f32[2,1536]{1,0:T(2,128)S(1)}, u32[]{:S(2)}, u32[]{:S(2)}) collective-permute-start(f32[2,1536]{1,0:T(2,128)S(1)} %get-tuple-element.59.a), channel_id=1, source_target_pairs={{0,1},{1,0},{2,3},{3,2},{4,5},{5,4},{6,7},{7,6},{8,9},{9,8},{10,11... | collective-permute-start | bytes 36872 | tf_op jit(solution)/shard_map/ppermute | solution.py:151
  55.1 10.0 %collective-permute-start.20 = (bf16[192,768]{1,0:T(8,128)(2,1)S(1)}, bf16[192,768]{1,0:T(8,128)(2,1)S(1)}, u32[]{:S(2)}, u32[]{:S(2)}) collective-permute-start(bf16[192,768]{1,0:T(8,128)(2,1)S(1)} %get-tuple-element.70), channel_id=1, source_target_pairs={{0,2},{2,0},{1,3},{3,1},{4,6},{6,4},{5,7},{7,5},{8,10},{10,8},{9,1... | collective-permute-start | bytes 884744 | tf_op jit(solution)/shard_map/ppermute | solution.py:607
  55.7 3.7 %collective-permute-start.15 = (f32[2,1536]{1,0:T(2,128)S(1)}, f32[2,1536]{1,0:T(2,128)S(1)}, u32[]{:S(2)}, u32[]{:S(2)}) collective-permute-start(f32[2,1536]{1,0:T(2,128)S(1)} %merge.6.a), channel_id=1, source_target_pairs={{0,4},{4,0},{8,12},{12,8},{1,5},{5,1},{9,13},{13,9},{2,6},{6,2},{1... | collective-permute-start | bytes 36872 | tf_op jit(solution)/shard_map/ppermute | solution.py:151
  59.4 4.7 %collective-permute-start.16 = (f32[2,1536]{1,0:T(2,128)S(1)}, f32[2,1536]{1,0:T(2,128)S(1)}, u32[]{:S(2)}, u32[]{:S(2)}) collective-permute-start(f32[2,1536]{1,0:T(2,128)S(1)} %merge.7.a), channel_id=1, source_target_pairs={{0,8},{4,12},{8,0},{12,4},{1,9},{5,13},{9,1},{13,5},{2,10},{6,14},... | collective-permute-start | bytes 36872 | tf_op jit(solution)/shard_map/ppermute | solution.py:151
  64.1 11.4 %collective-permute-start.17 = (bf16[64,1536]{1,0:T(8,128)(2,1)S(1)}, bf16[64,1536]{1,0:T(8,128)(2,1)S(1)}, u32[]{:S(2)}, u32[]{:S(2)}) collective-permute-start(bf16[64,1536]{1,0:T(8,128)(2,1)S(1)} %get-tuple-element.67), channel_id=1, source_target_pairs={{0,4},{4,0},{8,12},{12,8},{1,5},{5,1},{9,13},{13,9},{2,6},{6,2},{1... | collective-permute-start | bytes 589832 | tf_op jit(solution)/shard_map/ppermute | solution.py:610
  65.1 14.1 %collective-permute-start.21 = (bf16[192,768]{1,0:T(8,128)(2,1)S(1)}, bf16[192,768]{1,0:T(8,128)(2,1)S(1)}, u32[]{:S(2)}, u32[]{:S(2)}) collective-permute-start(bf16[192,768]{1,0:T(8,128)(2,1)S(1)} %collective-permute-done.20.rest_3_), channel_id=1, source_target_pairs={{0,1},{1,0},{2,3},{3,2},{4,5},{5,4},{6,7},{7,6},{8,9},{9,8},{10,11... | collective-permute-start | bytes 884744 | tf_op jit(solution)/shard_map/ppermute | solution.py:608
  65.1 10.4 %collective-permute-start.18 = (bf16[64,1536]{1,0:T(8,128)(2,1)S(1)}, bf16[64,1536]{1,0:T(8,128)(2,1)S(1)}, u32[]{:S(2)}, u32[]{:S(2)}) collective-permute-start(bf16[64,1536]{1,0:T(8,128)(2,1)S(1)} %get-tuple-element.68), channel_id=1, source_target_pairs={{4,8},{8,4},{5,9},{9,5},{6,10},{10,6},{7,11},{11,7},{20,24},{24,20... | collective-permute-start | bytes 589832 | tf_op jit(solution)/shard_map/ppermute | solution.py:610
  70.5 8.7 %collective-permute-start.23 = (bf16[256,384]{1,0:T(8,128)(2,1)S(1)}, bf16[256,384]{1,0:T(8,128)(2,1)S(1)}, u32[]{:S(2)}, u32[]{:S(2)}) collective-permute-start(bf16[256,384]{1,0:T(8,128)(2,1)S(1)} %get-tuple-element.72.rest_0_), channel_id=1, source_target_pairs={{0,2},{2,0},{1,3},{3,1},{4,6},{6,4},{5,7},{7,5},{8,10},{10,8},{9,1... | collective-permute-start | bytes 589832 | tf_op jit(solution)/shard_map/ppermute | solution.py:532
  74.8 7.8 %collective-permute-start.22 = (bf16[256,384]{1,0:T(8,128)(2,1)S(1)}, bf16[256,384]{1,0:T(8,128)(2,1)S(1)}, u32[]{:S(2)}, u32[]{:S(2)}) collective-permute-start(bf16[256,384]{1,0:T(8,128)(2,1)S(1)} %get-tuple-element.71.rest_0_), channel_id=1, source_target_pairs={{0,2},{2,0},{1,3},{3,1},{4,6},{6,4},{5,7},{7,5},{8,10},{10,8},{9,1... | collective-permute-start | bytes 589832 | tf_op jit(solution)/shard_map/ppermute | solution.py:532
  77.7 6.4 %collective-permute-start.19 = (bf16[128,384]{1,0:T(8,128)(2,1)S(1)}, bf16[128,384]{1,0:T(8,128)(2,1)S(1)}, u32[]{:S(2)}, u32[]{:S(2)}) collective-permute-start(bf16[128,384]{1,0:T(8,128)(2,1)S(1)} %conv1_0.1.rest_0_), channel_id=1, source_target_pairs={{0,2},{2,0},{1,3},{3,1},{4,6},{6,4},{5,7},{7,5},{8,10},{10,8},{9,1... | collective-permute-start | bytes 294920 | tf_op jit(solution)/shard_map/ppermute | solution.py:532
  (1 other events, 13.9 us)
